TPU v7x, 32 devices: a whole 2x2x4 slice. The times are simulated.
32 devices in a mesh: batch: 8 (over z, y), mp: 4 (over x, core).
Axes of the slice: x: 2, y: 2, z: 4, core: 2. Of those that a mesh axis runs over, the one named last changes fastest.
Arguments:
- tokens: bfloat16 [768, 128, 768], P('batch'), may hold values from -6 to 6
- lengths: int32 [768], P('batch'), may hold values from 20 to 128, as said below
- base_gains: float32 [2, 768], replicated, may hold values from 0.25 to 1.75
- base_qkv: bfloat16 [3, 768, 768], P(None, None, 'mp'), may hold values from -0.109375 to 0.109375
- base_out: bfloat16 [768, 768], replicated, may hold values from -0.75 to 0.75
- base_up: bfloat16 [768, 3072], replicated, may hold values from -0.21875 to 0.21875
- base_down: bfloat16 [3072, 768], replicated, may hold values from -0.15625 to 0.15625
- base_table: float32 [32, 12], replicated, may hold values from -4 to 4
- side_input: float32 [768, 128, 96], P(('batch', 'mp')), may hold values from -6 to 6
- output_grad: float32 [768, 128, 96], P(('batch', 'mp')), may hold values from -6 to 6
- side_weights: float32 [184320], P(('batch', 'mp'))
- weights_first: float32 [184320], P(('batch', 'mp')), may hold values from -0.00390625 to 0.00390625
- weights_second: float32 [184320], P(('batch', 'mp')), may hold values from 5.4253473e-09 to 2.170139e-08
- side_gains: float32 [3, 96], replicated
- gains_first: float32 [3, 96], replicated, may hold values from -0.0068359375 to 0.0068359375
- gains_second: float32 [3, 96], replicated, may hold values from 5.4253473e-09 to 2.7126736e-08
- side_table: float32 [32, 12], replicated, may hold values from -4 to 4
- table_first: float32 [32, 12], replicated, may hold values from -0.0014648438 to 0.0014648438
- table_second: float32 [32, 12], replicated, may hold values from 2.7126737e-10 to 1.0850695e-09
Outputs:
- side_output: float32 [768, 128, 96], P(('batch', 'mp'))
- input_grad: float32 [768, 128, 96], P(('batch', 'mp'))
- grad_norm: float32 [], replicated
- weights_moment: float32 [184320], P(('batch', 'mp'))
- weights_square: float32 [184320], P(('batch', 'mp'))
- weights_new: float32 [184320], P(('batch', 'mp'))
- weights_copy: bfloat16 [184320], P(('batch', 'mp'))
- gains_moment: float32 [3, 96], replicated
- gains_square: float32 [3, 96], replicated
- gains_new: float32 [3, 96], replicated
- table_moment: float32 [32, 12], replicated
- table_square: float32 [32, 12], replicated
- table_new: float32 [32, 12], replicated
Inputs may be any that keep to these rules, and one draw needn't show every extreme that they name: `lengths`: each sentence has 20 to 128 true tokens, and the first sentence has exactly 128.
All inputs are finite; a program needn't handle non-finite values.
Results may differ from a plain program's by a relative error of at most 0.024.
Values may be sent and summed in bfloat16 or wider, within the bound.
No kernel may reach another device: no remote copies, remote signals or barrier semaphores. Data moves between devices by JAX's collectives and lax.ppermute only.
A program may use at most 192 MiB of HBM per device.

v0:
```python
import jax
import jax.numpy as jnp
import numpy as np
from jax import lax
from jax.sharding import PartitionSpec as P

D = 768
HD = 64
DS = 96
SH = 12
SHD = 8
SFF = 384
MAXD = 128
L = 128
ADAM_STEP = 10


NORM_EPS = 1e-06
CLIP_NORM = 1.0
BETA_ONE = 0.9
BETA_TWO = 0.999
ADAM_EPS = 1e-08
RATE_MATRIX = 0.1
RATE_SMALL = 0.5
WEIGHT_DECAY = 0.01
MASKED = -1e30
PRECISE = lax.Precision.HIGHEST


def bucket_ids(length, buckets, reach):
    offset = np.arange(length)[None, :] - np.arange(length)[:, None]
    half_count = buckets // 2
    exact_count = half_count // 2
    distance = np.abs(offset)
    spread_part = (
        np.log(np.maximum(distance, 1) / exact_count)
        / np.log(reach / exact_count)
        * (half_count - exact_count)
    )
    far_bucket = np.minimum(exact_count + np.floor(spread_part).astype(np.int32), half_count - 1)
    near_side = np.where(distance < exact_count, distance, far_bucket)
    return (near_side + (offset > 0) * half_count).astype(np.int32)


def bucket_onehot(buckets):
    flat_ids = jnp.asarray(bucket_ids(L, buckets, MAXD).reshape(-1))
    return (flat_ids[:, None] == jnp.arange(buckets, dtype=jnp.int32)[None, :]).astype(jnp.float32)


def position_bias(table, onehot):
    flat_bias = jnp.dot(onehot, table, precision=PRECISE)
    return jnp.transpose(flat_bias).reshape(table.shape[1], L, L)


def rms_scale(values):
    return lax.rsqrt(jnp.mean(values * values, axis=-1, keepdims=True) + NORM_EPS)


def block_size(count):
    return min(count, max(1, 512 // L))


def masked_scores(query_blk, key_blk, length_blk, pos_bias):
    scores = (
        jnp.einsum("bqhe,bkhe->bhqk", query_blk, key_blk, preferred_element_type=jnp.float32)
        + pos_bias[None]
    )
    visible = (jnp.arange(L)[None, :] < length_blk[:, None])[:, None, None, :]
    return jnp.where(visible, scores, MASKED)


def base_attention(queries, keys_all, values_all, row_lengths, pos_bias):
    count, heads, depth = (queries.shape[0], queries.shape[2], queries.shape[3])
    block = block_size(count)
    steps_count = count // block

    def one_block(items):
        query_blk, key_blk, value_blk, length_blk = items
        scores = masked_scores(query_blk, key_blk, length_blk, pos_bias)
        row_max = jnp.max(scores, axis=-1, keepdims=True)
        exp_scores = jnp.exp(scores - row_max)
        attn_probs = (exp_scores / jnp.sum(exp_scores, axis=-1, keepdims=True)).astype(jnp.bfloat16)
        context = jnp.einsum(
            "bhqk,bkhe->bqhe", attn_probs, value_blk, preferred_element_type=jnp.float32
        )
        return context.astype(jnp.bfloat16).reshape(block, L, heads * depth)

    shaped = (
        queries.reshape(steps_count, block, L, heads, depth),
        keys_all.reshape(steps_count, block, L, heads, depth),
        values_all.reshape(steps_count, block, L, heads, depth),
        row_lengths.reshape(steps_count, block),
    )
    return lax.map(one_block, shaped).reshape(count, L, heads * depth)


def split_side(projected_blk):
    count = projected_blk.shape[0]
    return (
        projected_blk[..., :DS].reshape(count, L, SH, SHD),
        projected_blk[..., DS : 2 * DS].reshape(count, L, SH, SHD),
        projected_blk[..., 2 * DS :].reshape(count, L, SH, SHD),
    )


def side_attention(projected, row_lengths, pos_bias):
    count = projected.shape[0]
    block = block_size(count)
    steps_count = count // block

    def one_block(items):
        projected_blk, length_blk = items
        queries, keys_all, values_all = split_side(projected_blk)
        scores = masked_scores(queries, keys_all, length_blk, pos_bias)
        row_max = jnp.max(scores, axis=-1, keepdims=True)
        exp_scores = jnp.exp(scores - row_max)
        row_total = jnp.sum(exp_scores, axis=-1, keepdims=True)
        attn_probs = (exp_scores / row_total).astype(jnp.bfloat16)
        context = jnp.einsum(
            "bhqk,bkhe->bqhe", attn_probs, values_all, preferred_element_type=jnp.float32
        )
        log_total = (row_max + jnp.log(row_total))[..., 0]
        return (context.astype(jnp.bfloat16).reshape(block, L, DS), log_total)

    context, log_total = lax.map(
        one_block,
        (projected.reshape(steps_count, block, L, 3 * DS), row_lengths.reshape(steps_count, block)),
    )
    return (context.reshape(count, L, DS), log_total)


def side_attention_back(projected, grad_context, log_total, row_lengths, pos_bias):
    count = projected.shape[0]
    block = block_size(count)
    steps_count = count // block

    def one_block(items):
        projected_blk, grad_blk, log_blk, length_blk = items
        queries, keys_all, values_all = split_side(projected_blk)
        scores = masked_scores(queries, keys_all, length_blk, pos_bias)
        attn_float = jnp.exp(scores - log_blk[..., None])
        attn_low = attn_float.astype(jnp.bfloat16)
        grad_heads = grad_blk.reshape(block, L, SH, SHD)
        grad_values = jnp.einsum(
            "bhqk,bqhe->bkhe", attn_low, grad_heads, preferred_element_type=jnp.float32
        ).astype(jnp.bfloat16)
        grad_probs = jnp.einsum(
            "bqhe,bkhe->bhqk", grad_heads, values_all, preferred_element_type=jnp.float32
        )
        row_dot = jnp.sum(attn_float * grad_probs, axis=-1, keepdims=True)
        grad_scores = (attn_float * (grad_probs - row_dot)).astype(jnp.bfloat16)
        grad_queries = jnp.einsum(
            "bhqk,bkhe->bqhe", grad_scores, keys_all, preferred_element_type=jnp.float32
        ).astype(jnp.bfloat16)
        grad_keys = jnp.einsum(
            "bhqk,bqhe->bkhe", grad_scores, queries, preferred_element_type=jnp.float32
        ).astype(jnp.bfloat16)
        joined = jnp.concatenate(
            [
                grad_queries.reshape(block, L, DS),
                grad_keys.reshape(block, L, DS),
                grad_values.reshape(block, L, DS),
            ],
            axis=-1,
        )
        return (joined, jnp.sum(grad_scores.astype(jnp.float32), axis=0))

    shaped = (
        projected.reshape(steps_count, block, L, 3 * DS),
        grad_context.reshape(steps_count, block, L, DS),
        log_total,
        row_lengths.reshape(steps_count, block),
    )
    joined, bias_grad = lax.map(one_block, shaped)
    return (joined.reshape(count * L, 3 * DS), jnp.sum(bias_grad, axis=0))


def norm_back(values, scale, gain_vec, grad_normed):
    unit = values * scale
    gain_grad = jnp.sum(grad_normed * unit, axis=0)
    scaled = grad_normed * gain_vec
    return (scale * (scaled - unit * jnp.mean(scaled * unit, axis=-1, keepdims=True)), gain_grad)


def unpack(flat):
    first_end = D * DS
    second_end = first_end + 3 * DS * DS
    third_end = second_end + DS * DS
    fourth_end = third_end + DS * SFF
    return (
        flat[:first_end].reshape(D, DS),
        flat[first_end:second_end].reshape(DS, 3 * DS),
        flat[second_end:third_end].reshape(DS, DS),
        flat[third_end:fourth_end].reshape(DS, SFF),
        flat[fourth_end:].reshape(SFF, DS),
    )


def transposed_product(left, right):
    return jnp.einsum("ti,tj->ij", left, right, preferred_element_type=jnp.float32)


def back_product(left, weight):
    return jnp.einsum("tj,ij->ti", left, weight, preferred_element_type=jnp.float32)


def adamw_update(weight_now, first_now, second_now, gradient, rate, decay_rate):
    first_new = BETA_ONE * first_now + (1.0 - BETA_ONE) * gradient
    second_new = BETA_TWO * second_now + (1.0 - BETA_TWO) * gradient * gradient
    first_hat = first_new / (1.0 - BETA_ONE**ADAM_STEP)
    second_hat = second_new / (1.0 - BETA_TWO**ADAM_STEP)
    weight_new = weight_now - rate * (
        first_hat / (jnp.sqrt(second_hat) + ADAM_EPS) + decay_rate * weight_now
    )
    return (first_new, second_new, weight_new)


def on_device(
    tokens,
    lengths,
    base_gains,
    base_qkv,
    base_out,
    base_up,
    base_down,
    base_table,
    side_input,
    output_grad,
    side_weights,
    weights_first,
    weights_second,
    side_gains,
    gains_first,
    gains_second,
    side_table,
    table_first,
    table_second,
):
    model_size = lax.axis_size("mp")
    model_index = lax.axis_index("mp")
    group_seqs = tokens.shape[0]
    own_seqs = group_seqs // model_size
    own_rows = own_seqs * L
    own_tokens = lax.dynamic_slice_in_dim(tokens, model_index * own_seqs, own_seqs, 0)
    own_lengths = lax.dynamic_slice_in_dim(lengths, model_index * own_seqs, own_seqs, 0)
    weights_low = lax.all_gather(
        side_weights.astype(jnp.bfloat16), ("batch", "mp"), axis=0, tiled=True
    )
    base_onehot = bucket_onehot(base_table.shape[0])
    own_float = own_tokens.reshape(own_rows, D).astype(jnp.float32)
    local_heads = base_qkv.shape[2] // HD
    group_float = tokens.reshape(group_seqs * L, D).astype(jnp.float32)
    normed = (group_float * rms_scale(group_float) * base_gains[0]).astype(jnp.bfloat16)
    projected = jnp.einsum(
        "td,kdc->ktc", normed, base_qkv, preferred_element_type=jnp.float32
    ).astype(jnp.bfloat16)
    table_part = lax.dynamic_slice_in_dim(base_table, model_index * local_heads, local_heads, 1)
    pieces = projected.reshape(3, group_seqs, L, local_heads, HD)
    context = base_attention(
        pieces[0], pieces[1], pieces[2], lengths, position_bias(table_part, base_onehot)
    )
    context = lax.all_to_all(context, "mp", split_axis=0, concat_axis=2, tiled=True)
    base_middle = own_float + jnp.dot(
        context.reshape(own_rows, D), base_out, preferred_element_type=jnp.float32
    )
    base_normed = (base_middle * rms_scale(base_middle) * base_gains[1]).astype(jnp.bfloat16)
    base_hidden = jax.nn.gelu(
        jnp.dot(base_normed, base_up, preferred_element_type=jnp.float32)
    ).astype(jnp.bfloat16)
    taps = (
        base_middle + jnp.dot(base_hidden, base_down, preferred_element_type=jnp.float32)
    ).astype(jnp.bfloat16)
    w_down, w_qkv, w_out, w_up, w_back = unpack(weights_low)
    side_rows = side_input.reshape(own_rows, DS)
    keep_rows = (
        (jnp.arange(L)[None, :] < own_lengths[:, None]).astype(jnp.float32).reshape(own_rows, 1)
    )
    grad_out = output_grad.reshape(own_rows, DS) * keep_rows
    mixing = jax.nn.sigmoid(side_gains[2])
    tapped = jnp.dot(taps, w_down, preferred_element_type=jnp.float32)
    mixed = mixing * side_rows + (1.0 - mixing) * tapped
    scale_one = rms_scale(mixed)
    normed_one = (mixed * scale_one * side_gains[0]).astype(jnp.bfloat16)
    projected_side = jnp.dot(normed_one, w_qkv, preferred_element_type=jnp.float32).astype(
        jnp.bfloat16
    )
    side_onehot = bucket_onehot(side_table.shape[0])
    side_bias = position_bias(side_table, side_onehot)
    projected_seq = projected_side.reshape(own_seqs, L, 3 * DS)
    context_side, log_total = side_attention(projected_seq, own_lengths, side_bias)
    context_flat = context_side.reshape(own_rows, DS)
    middle = mixed + jnp.dot(context_flat, w_out, preferred_element_type=jnp.float32)
    scale_two = rms_scale(middle)
    normed_two = (middle * scale_two * side_gains[1]).astype(jnp.bfloat16)
    pre_act = jnp.dot(normed_two, w_up, preferred_element_type=jnp.float32)
    activated, gelu_back = jax.vjp(jax.nn.gelu, pre_act)
    hidden = activated.astype(jnp.bfloat16)
    side_output = middle + jnp.dot(hidden, w_back, preferred_element_type=jnp.float32)
    grad_low = grad_out.astype(jnp.bfloat16)
    grad_back = transposed_product(hidden, grad_low)
    grad_pre = gelu_back(back_product(grad_low, w_back))[0].astype(jnp.bfloat16)
    grad_up = transposed_product(normed_two, grad_pre)
    grad_normed_two = back_product(grad_pre, w_up)
    norm_part, gain_two_grad = norm_back(middle, scale_two, side_gains[1], grad_normed_two)
    grad_middle = grad_out + norm_part
    grad_attended = grad_middle.astype(jnp.bfloat16)
    grad_out_proj = transposed_product(context_flat, grad_attended)
    grad_context = back_product(grad_attended, w_out).astype(jnp.bfloat16)
    grad_qkv, bias_grad = side_attention_back(
        projected_seq, grad_context.reshape(own_seqs, L, DS), log_total, own_lengths, side_bias
    )
    table_grad = jnp.einsum(
        "hp,pn->nh", bias_grad.reshape(SH, L * L), side_onehot, precision=PRECISE
    )
    grad_qkv_weight = transposed_product(normed_one, grad_qkv)
    grad_normed_one = back_product(grad_qkv, w_qkv)
    norm_part_one, gain_one_grad = norm_back(mixed, scale_one, side_gains[0], grad_normed_one)
    grad_mixed = grad_middle + norm_part_one
    input_grad = mixing * grad_mixed
    grad_tap = ((1.0 - mixing) * grad_mixed).astype(jnp.bfloat16)
    grad_down = transposed_product(taps, grad_tap)
    gate_grad = jnp.sum(grad_mixed * (side_rows - tapped), axis=0) * mixing * (1.0 - mixing)
    flat_grad = jnp.concatenate(
        [
            grad_down.reshape(-1),
            grad_qkv_weight.reshape(-1),
            grad_out_proj.reshape(-1),
            grad_up.reshape(-1),
            grad_back.reshape(-1),
        ]
    )
    grad_shard = lax.psum_scatter(flat_grad, ("batch", "mp"), scatter_dimension=0, tiled=True)
    gains_part = jnp.stack([gain_one_grad, gain_two_grad, gate_grad])
    gains_total, table_total, square_total = lax.psum(
        (gains_part, table_grad, jnp.sum(grad_shard * grad_shard)), ("batch", "mp")
    )
    grad_norm = jnp.sqrt(
        square_total + jnp.sum(gains_total * gains_total) + jnp.sum(table_total * table_total)
    )
    factor = CLIP_NORM / jnp.maximum(grad_norm, CLIP_NORM)
    weights_moment, weights_square, weights_new = adamw_update(
        side_weights, weights_first, weights_second, factor * grad_shard, RATE_MATRIX, WEIGHT_DECAY
    )
    gains_moment, gains_square, gains_new = adamw_update(
        side_gains, gains_first, gains_second, factor * gains_total, RATE_SMALL, 0.0
    )
    table_moment, table_square, table_new = adamw_update(
        side_table, table_first, table_second, factor * table_total, RATE_SMALL, 0.0
    )
    return (
        side_output.reshape(own_seqs, L, DS),
        input_grad.reshape(own_seqs, L, DS),
        grad_norm,
        weights_moment,
        weights_square,
        weights_new,
        weights_new.astype(jnp.bfloat16),
        gains_moment,
        gains_square,
        gains_new,
        table_moment,
        table_square,
        table_new,
    )


def solution(mesh):
    return jax.shard_map(
        on_device,
        mesh=mesh,
        in_specs=(
            P("batch", None, None),
            P("batch"),
            P(),
            P(None, None, "mp"),
            P(),
            P(),
            P(),
            P(),
            P(("batch", "mp"), None, None),
            P(("batch", "mp"), None, None),
            P(("batch", "mp")),
            P(("batch", "mp")),
            P(("batch", "mp")),
            P(),
            P(),
            P(),
            P(),
            P(),
            P(),
        ),
        out_specs=(
            P(("batch", "mp"), None, None),
            P(("batch", "mp"), None, None),
            P(),
            P(("batch", "mp")),
            P(("batch", "mp")),
            P(("batch", "mp")),
            P(("batch", "mp")),
            P(),
            P(),
            P(),
            P(),
            P(),
            P(),
        ),
        check_vma=False,
    )
```

profile of v0, /device:TPU:0, one launch (start us, length us, event | category | flops | bytes accessed | tf_op | source)
XLA Modules:
  0.0 765.9 jit_solution(16169485788570757900)
XLA Ops:
  8.1 8.7 %multiply_reduce_fusion.1 = f32[96,128]{1,0:T(8,128)S(1)} fusion(bf16[96,128,768]{2,1,0:T(8,128)(2,1)} %param.27), kind=kLoop, calls=%fused_computation.77 | loop fusion | flops 28299264 | bytes 18923520 | tf_op jit(solution)/shard_map/reduce_sum | solution.py:56
  16.7 3.3 copy-done.2
  20.1 10.1 %fusion.36 = bf16[12288,768]{1,0:T(8,128)(2,1)} fusion(f32[768]{0:T(1024)S(1)} %get-tuple-element.374, f32[12288]{0:T(1024)S(1)} %rsqrt_bitcast_fusion, bf16[96,128,768]{2,1,0:T(8,128)(2,1)S(1)} %copy-done.2), kind=kLoop, calls=%fused_computation.76 | loop fusion | flops 37748736 | bytes 37800960 | tf_op jit(solution)/shard_map/convert_element_type | solution.py:253
  30.1 34.4 %fusion.94 = f32[12288,576]{0,1} fusion(bf16[12288,768]{1,0:T(8,128)(2,1)} %fusion.36, bf16[768,576]{0,1:T(8,128)(2,1)S(1)} %bitcast.320), kind=kOutput, calls=%fused_computation.190 | convolution fusion | flops 10871635968 | bytes 48070656
  64.5 10.5 %convert_bitcast_fusion = bf16[3,12288,192]{1,2,0:T(8,128)(2,1)S(1)} fusion(f32[12288,3,192]{0,2,1:T(8,128)} %bitcast.306), kind=kLoop, calls=%fused_computation.80 | loop fusion | flops 7077888 | bytes 42467328 | tf_op jit(solution)/shard_map/convert_element_type | solution.py:256
  75.1 5.1 fusion.92
  80.2 8.1 %reshape_squeeze.10 = bf16[24,4,128,3,64]{2,1,0,4,3:T(4,128)(2,1)} reshape(bf16[1,12288,192]{1,2,0:T(8,128)(2,1)} %get-tuple-element.445) | data formatting | bytes 9437184 | tf_op jit(solution)/shard_map/reshape;squeeze | solution.py:89
  88.3 8.2 %reshape_squeeze.11 = bf16[24,4,128,3,64]{2,1,0,4,3:T(4,128)(2,1)} reshape(bf16[1,12288,192]{1,2,0:T(8,128)(2,1)} %get-tuple-element.444) | data formatting | bytes 9437184 | tf_op jit(solution)/shard_map/reshape;squeeze | solution.py:90
  96.5 8.2 %reshape_squeeze.9 = bf16[24,4,128,3,64]{2,1,0,4,3:T(4,128)(2,1)} reshape(bf16[1,12288,192]{1,2,0:T(8,128)(2,1)} %get-tuple-element.446) | data formatting | bytes 9437184 | tf_op jit(solution)/shard_map/reshape;squeeze | solution.py:91
  106.2 103.0 %while.34 = (s32[]{:T(128)}, bf16[24,4,128,192]{2,3,1,0:T(8,128)(2,1)}, bf16[24,4,128,3,64]{2,1,0,4,3:T(4,128)(2,1)}, s32[24,4]{1,0:T(8,128)S(1)}, bf16[24,4,128...) while((s32[]{:T(128)}, ...), condition=%wide.region_4.5_spmd, body=%wide.region_1.4_spmd.sunk | while | flops 77367552 | bytes 5519505 | solution.py:94
  209.2 5.1 all-to-all-start
  214.4 90.6 %all-gather = bf16[32,1,5760]{2,1,0:T(2,128)(2,1)S(1)} all-gather(bf16[1,1,5760]{2,1,0:T(2,128)(2,1)S(1)} %reshape.349), channel_id=1, replica_groups=mesh['batch'=8,'mp'=4] {'batch','mp'}, dimensions={0}, use_global_device_ids=true | all-gather | bytes 380160 | tf_op jit(solution)/shard_map/all_gather | solution.py:246
  305.0 2.2 reduce.2
  307.8 2.8 constant_dynamic-slice_fusion.7
  310.6 4.7 bitcast_convert_fusion
  315.3 9.7 %copy.213 = f32[3072,768]{0,1:T(8,128)} copy(f32[3072,768]{1,0:T(8,128)} %bitcast_convert_fusion) | data formatting | bytes 18874368 | tf_op jit(solution)/shard_map/convert_element_type | solution.py:250
  327.6 5.5 copy.192
  333.2 6.9 multiply_reduce_fusion.2
  340.1 42.9 %add_convert_fusion = bf16[3072,768]{0,1:T(8,128)(2,1)} fusion(f32[3072,768]{0,1:T(8,128)} %get-tuple-element.454, bf16[3072,768]{1,0:T(8,128)(2,1)} %param.33, bf16[768,3072]{1,0:T(8,128)(2,1)} %param.32, f32[768]{0:T(1024)S(1)} %get-tuple-element.373, f32[3072]{0:T(1024)S(1)} %add_rsqrt_fusion.2), kind=kOutput, calls=%fused_computation.81 | convolution fusion | flops 29087760384 | bytes 23608320 | tf_op jit(solution)/shard_map/dot_general | solution.py:271
  383.0 4.4 multiply_reduce_fusion.8
  387.4 1.9 convolution_convert_fusion.3
  389.4 4.4 reshape_reshape.10
  393.8 3.0 copy.194
  396.8 42.3 %while.35 = (s32[]{:T(128)}, bf16[6,4,128,96]{2,1,0,3:T(4,128)(2,1)}, f32[6,4,12,128]{3,2,1,0:T(8,128)}, bf16[6,4,128,288]{2,3,1,0:T(8,128)(2,1)}, s32[6,4]{1,0:T(8,128)S(1)}, /*index=5*/f32[12,16384]{1,0:T(8,128)}, s32[]{:T(128)}) while((s32[]{:T(128)}, bf16[6,4,128,96]{2,1,0,3:T(4,128)(2,1)}, f32[6,4,12,128]{3,2,1,0:T(8,128)}, ...), condition=%wide.region_10.11_spmd, body=%wide.region_7.10_spmd.sunk | while | flops 34646528 | bytes 18443396 | solution.py:125
  442.8 3.6 fusion.47
  451.9 103.6 %while.36 = (s32[]{:T(128)}, bf16[6,4,128,288]{2,1,0,3:T(4,128)(2,1)}, f32[6,12,128,128]{2,3,1,0:T(8,128)}, bf16[6,4,128,288]{2,3,1,0:T(8,128)(2,1)}, s32[6,4]{1...) while((s32[]{:T(128)}, ...), condition=%wide.region_16.17_spmd, body=%wide.region_13.16_spmd.sunk | while | flops 72395264 | bytes 39775244 | solution.py:174
  459.2 2.3 copy.299
  461.6 2.5 multiply_reduce_fusion.13
  476.5 2.3 copy.299
  478.8 2.5 multiply_reduce_fusion.13
  493.8 2.3 copy.299
  496.1 2.5 multiply_reduce_fusion.13
  511.1 2.3 copy.299
  513.4 2.5 multiply_reduce_fusion.13
  528.3 2.3 copy.299
  530.6 2.5 multiply_reduce_fusion.13
  545.6 2.3 copy.299
  547.9 2.5 multiply_reduce_fusion.13
  555.5 3.4 reshape.338
  558.9 2.3 multiply_reduce_fusion.4
  562.0 5.2 fusion.70
  567.3 2.9 fusion.57
  573.0 3.1 fusion.60
  576.0 3.8 fusion.65
  581.9 2.8 reduce_sum.167
  587.0 118.5 %all-reduce.4.cloned.1.call-done = f32[184320]{0:T(1024)} async-done(((f32[184320]{0:T(1024)}), f32[184320]{0:T(1024)}) %all-reduce.4.cloned.1.call-update) | async-done | bytes 737296
  706.9 2.9 copy_bitcast_fusion.14
  709.8 40.5 %all-reduce.1 = (f32[]{:T(128)}, f32[3,96]{1,0:T(4,128)S(1)}, f32[32,12]{0,1:T(8,128)S(1)}) all-reduce(f32[]{:T(128)} %multiply_reduce_fusion.9, f32[3,96]{1,0:T(4,128)S(1)} %pad_maximum_fusion, f32[32,12]{0,1:T(8,128)S(1)} %fusion.55), channel_id=1, replica_groups=mesh['batch'=8,'mp'=4] {'batch','mp'}, use_global_device_ids=true, to_apply=%region_20.21 | all-reduce | flops 673 | bytes 5384 | tf_op jit(solution)/shard_map/psum | solution.py:334
  (613 shorter events, 247.4 us)
Async XLA Ops:
  7.2 326.0 %copy-start = (bf16[768,768]{1,0:T(8,128)(2,1)S(1)}, bf16[768,768]{1,0:T(8,128)(2,1)}, u32[]{:S(2)}) copy-start(bf16[768,768]{1,0:T(8,128)(2,1)} %param.31) | copy-start | bytes 3538948
  8.0 12.0 %copy-start.2 = (bf16[96,128,768]{2,1,0:T(8,128)(2,1)S(1)}, bf16[96,128,768]{2,1,0:T(8,128)(2,1)}, u32[]{:S(2)}) copy-start(bf16[96,128,768]{2,1,0:T(8,128)(2,1)} %param.27) | copy-start | bytes 56623108
  20.1 10.1 %copy-start.51 = (bf16[3,768,192]{1,2,0:T(8,128)(2,1)S(1)}, bf16[3,768,192]{1,2,0:T(8,128)(2,1)}, u32[]{:S(2)}) copy-start(bf16[3,768,192]{1,2,0:T(8,128)(2,1)} %param.30) | copy-start | bytes 2654212
  96.5 8.2 %copy-start.49 = (s32[96]{0:T(128)S(1)}, s32[96]{0:T(128)}, u32[]{:S(2)}) copy-start(s32[96]{0:T(128)} %param.28) | copy-start | bytes 1156
  96.5 8.3 %copy-start.24 = (s32[16384]{0:T(1024)S(1)}, s32[16384]{0:T(1024)}, u32[]{:S(2)}) copy-start(s32[16384]{0:T(1024)} %constant.88.clone) | copy-start | bytes 196612
  209.2 5.1 copy-start.31
  209.2 118.4 %all-to-all-start = ((bf16[96,128,192]{1,2,0:T(8,128)(2,1)}), bf16[96,128,192]{1,2,0:T(8,128)(2,1)}, u32[]{:S(2)}, u32[]{:S(2)}) async-start(bf16[96,128,192]{1,2,0:T(8,128)(2,1)} %bitcast.310), calls=%async_computation | async-start | bytes 9437184 | tf_op jit(solution)/shard_map/all_to_all | solution.py:262
  214.3 491.2 %all-reduce.4.cloned.1.call-start = ((), (), s32[]{:S(2)}) async-start(), calls=%async_computation.1 | async-start | bytes 1474560
  307.7 2.9 copy-start.14
  315.3 9.8 %slice-start.2 = ((bf16[184320]{0:T(1024)(128)(2,1)}), bf16[73728]{0:T(1024)(128)(2,1)S(1)}, s32[]{:S(2)}) async-start(bf16[184320]{0:T(1024)(128)(2,1)} %copy-done.14), calls=%async_computation.4 | async-start | bytes 294912 | tf_op jit(solution)/shard_map/slice | solution.py:191
  315.3 9.9 %slice-start.3 = ((bf16[184320]{0:T(1024)(128)(2,1)}), bf16[27648]{0:T(1024)(128)(2,1)S(1)}, s32[]{:S(2)}) async-start(bf16[184320]{0:T(1024)(128)(2,1)} %copy-done.14), calls=%async_computation.5 | async-start | bytes 110592 | tf_op jit(solution)/shard_map/slice | solution.py:192
  315.3 10.2 %slice-start.4 = ((bf16[184320]{0:T(1024)(128)(2,1)}), bf16[9216]{0:T(1024)(128)(2,1)S(1)}, s32[]{:S(2)}) async-start(bf16[184320]{0:T(1024)(128)(2,1)} %copy-done.14), calls=%async_computation.6 | async-start | bytes 36864 | tf_op jit(solution)/shard_map/slice | solution.py:193
  315.3 10.3 %copy-start.15 = (bf16[184320]{0:T(1024)(128)(2,1)S(1)}, bf16[184320]{0:T(1024)(128)(2,1)}, u32[]{:S(2)}) copy-start(bf16[184320]{0:T(1024)(128)(2,1)} %copy-done.14) | copy-start | bytes 1105924
  315.3 10.5 %copy-start.43 = (f32[3,96]{1,0:T(4,128)S(1)}, f32[3,96]{1,0:T(4,128)}, u32[]{:S(2)}) copy-start(f32[3,96]{1,0:T(4,128)} %param.40) | copy-start | bytes 3460
  315.3 10.6 %copy-start.35 = (f32[32,12]{0,1:T(8,128)S(1)}, f32[32,12]{0,1:T(8,128)}, u32[]{:S(2)}) copy-start(f32[32,12]{0,1:T(8,128)} %param.43) | copy-start | bytes 4612
  325.4 62.1 %copy-start.19 = (bf16[96,288]{1,0:T(8,128)(2,1)}, bf16[96,288]{1,0:T(8,128)(2,1)S(1)}, u32[]{:S(2)}) copy-start(bf16[96,288]{1,0:T(8,128)(2,1)S(1)} %slice.122) | copy-start | bytes 165892
  325.8 116.2 %copy-start.29 = (bf16[384,96]{1,0:T(8,128)(2,1)}, bf16[384,96]{1,0:T(8,128)(2,1)S(1)}, u32[]{:S(2)}) copy-start(bf16[384,96]{1,0:T(8,128)(2,1)S(1)} %slice.129) | copy-start | bytes 221188
  325.8 57.2 %copy-start.38 = (f32[1,96]{1,0:T(1,128)}, f32[1,96]{1,0:T(1,128)S(1)}, u32[]{:S(2)}) copy-start(f32[1,96]{1,0:T(1,128)S(1)} %get-tuple-element.452) | copy-start | bytes 1156
  325.8 57.2 %copy-start.40 = (f32[96]{0:T(128)}, f32[96]{0:T(128)S(1)}, u32[]{:S(2)}) copy-start(f32[96]{0:T(128)S(1)} %get-tuple-element.451) | copy-start | bytes 1156
  325.9 123.2 %copy-start.33 = (f32[3072]{0:T(1024)}, f32[3072]{0:T(1024)S(1)}, u32[]{:S(2)}) copy-start(f32[3072]{0:T(1024)S(1)} %convert_bitcast_fusion.1) | copy-start | bytes 36868
  327.6 5.5 copy-start.9
  340.1 42.9 %copy-start.10 = (f32[24,128,96]{1,2,0:T(8,128)S(1)}, f32[24,128,96]{1,2,0:T(8,128)}, u32[]{:S(2)}) copy-start(f32[24,128,96]{1,2,0:T(8,128)} %param.35) | copy-start | bytes 3538948
  387.4 53.2 %copy-start.3 = (f32[3072,96]{0,1:T(8,128)}, f32[3072,96]{0,1:T(8,128)S(1)}, u32[]{:S(2)}) copy-start(f32[3072,96]{0,1:T(8,128)S(1)} %get-tuple-element.435) | copy-start | bytes 3538948
  441.0 8.1 %copy-start.5 = (f32[3072,96]{0,1:T(8,128)}, f32[3072,96]{0,1:T(8,128)S(1)}, u32[]{:S(2)}) copy-start(f32[3072,96]{0,1:T(8,128)S(1)} %get-tuple-element.457) | copy-start | bytes 3538948
  442.8 3.6 copy-start.11
  466.4 2.8 copy-start.13
  483.7 2.9 copy-start.13
  555.5 3.4 copy-start.4
  555.5 3.4 copy-start.20
  558.9 3.1 copy-start.18
  558.9 3.1 copy-start.34
  561.2 6.0 slice-start
  562.0 5.2 copy-start.6
  562.0 5.2 slice-start.1
  562.0 5.2 copy-start.30
  567.2 3.5 copy-start.21
  567.3 4.2 copy-start.27
  567.3 5.7 copy-start.8
  572.9 3.1 copy-start.41
  576.0 4.2 copy-start.26
  576.0 4.3 copy-start.23
  576.0 4.3 copy-start.28
  576.0 4.4 copy-start.22
  585.1 172.6 %copy-start.1 = (bf16[768,768]{1,0:T(8,128)(2,1)S(1)}, bf16[768,768]{1,0:T(8,128)(2,1)}, u32[]{:S(2)}) copy-start(bf16[768,768]{1,0:T(8,128)(2,1)} %param.31) | copy-start | bytes 3538948
  585.7 167.9 %copy-start.36 = (f32[32,12]{0,1:T(8,128)S(1)}, f32[32,12]{0,1:T(8,128)}, u32[]{:S(2)}) copy-start(f32[32,12]{0,1:T(8,128)} %param.43) | copy-start | bytes 4612
  585.8 167.9 %copy-start.42 = (f32[32,12]{0,1:T(8,128)S(1)}, f32[32,12]{0,1:T(8,128)}, u32[]{:S(2)}) copy-start(f32[32,12]{0,1:T(8,128)} %param.45) | copy-start | bytes 4612
  585.8 170.5 %copy-start.32 = (f32[5760]{0:T(1024)S(1)}, f32[5760]{0:T(1024)}, u32[]{:S(2)}) copy-start(f32[5760]{0:T(1024)} %param.37) | copy-start | bytes 69124
  585.8 170.5 %copy-start.37 = (f32[5760]{0:T(1024)S(1)}, f32[5760]{0:T(1024)}, u32[]{:S(2)}) copy-start(f32[5760]{0:T(1024)} %param.39) | copy-start | bytes 69124
  (31 other events, 46.3 us)
Sparse Core Ops, SparseCore 0:
  581.4 123.9 all-reduce.3
where the time goes:
time: 777 us; the launch traced here: 766 us
  local copies, waits for them, and re-layouts  227 us (29%)
  matrix products  191 us (25%)
  blocking collectives  131 us (17%)
  waiting for transfers between devices  118 us (15%)
  other arithmetic  73.6 us (9%)
  between operations  18.3 us (2%)
    unnamed x2, waiting for transfers between devices  118 us
    all_gather x1, blocking collectives, on_device(): lax.all_gather(side_weights.astype(jnp.bfloat16), ('batch', 'mp'), axis=0...  90.6 us
    dynamic_slice x48, local copies, waits for them, and re-layouts, base_attention(): return lax.map(one_block, shaped).reshape(count, L, heads * depth)  52.2 us
    dot_general x1, matrix products, on_device(): jnp.dot(base_hidden, base_down, preferred_element_type=jnp.float32)  42.9 us
    psum x1, blocking collectives, on_device(): lax.psum((gains_part, table_grad, jnp.sum(grad_shard * grad_shard)), ('ba...  40.5 us
    unnamed x1, matrix products  34.4 us
    dot_general x36, matrix products, masked_scores(): jnp.einsum('bqhe,bkhe->bhqk', query_blk, key_blk, preferred_element_type=...  29.4 us
    add x48, local copies, waits for them, and re-layouts, masked_scores(): jnp.einsum('bqhe,bkhe->bhqk', query_blk, key_blk, preferred_element_type=...  24.5 us
  transfers between devices with their start and end apart: 2, of which 1 were waited for; matrix products, arithmetic and copies ran while one was open for 4% of the time, Pallas kernels for 0%

commit v1 on v0

v1 whole, which is shorter than its diff:
```python
import functools
import math
import jax
import jax.numpy as jnp
import numpy as np
from jax import lax
from jax.experimental import pallas as pl
from jax.experimental.pallas import tpu as pltpu
from jax.sharding import PartitionSpec as P

D = 768
HD = 64
DS = 96
SH = 12
SHD = 8
SFF = 384
MAXD = 128
L = 128
ADAM_STEP = 10
PAIR = 2 * HD
SPAN = 2 * L

NORM_EPS = 1e-06
CLIP_NORM = 1.0
BETA_ONE = 0.9
BETA_TWO = 0.999
ADAM_EPS = 1e-08
RATE_MATRIX = 0.1
RATE_SMALL = 0.5
WEIGHT_DECAY = 0.01
MASKED = -1e30
PRECISE = lax.Precision.HIGHEST
MIB = 1 << 20
GELU_RATE = math.sqrt(2.0 / math.pi)
GELU_CUBE = 0.044715

NN = (((1,), (0,)), ((), ()))
NT = (((1,), (1,)), ((), ()))
TN = (((0,), (0,)), ((), ()))


def mm(left, right, dims=NN):
    return lax.dot_general(left, right, dims, preferred_element_type=jnp.float32)


def bucket_of(offset, buckets, reach):
    half_count = buckets // 2
    exact_count = half_count // 2
    distance = np.abs(offset)
    spread_part = (
        np.log(np.maximum(distance, 1) / exact_count)
        / np.log(reach / exact_count)
        * (half_count - exact_count)
    )
    far_bucket = np.minimum(exact_count + np.floor(spread_part).astype(np.int32), half_count - 1)
    near_side = np.where(distance < exact_count, distance, far_bucket)
    return (near_side + (offset > 0) * half_count).astype(np.int32)


def diagonal_onehot(buckets):
    column = np.arange(SPAN)
    offset = np.where(column < L, -column, SPAN - column)
    onehot = bucket_of(offset, buckets, MAXD)[None, :] == np.arange(buckets)[:, None]
    onehot = onehot & (column != L)[None, :]
    return onehot.astype(np.float32)


def gradient_onehot(buckets):
    column = np.arange(SPAN)
    onehot = bucket_of(L - 1 - column, buckets, MAXD)[None, :] == np.arange(buckets)[:, None]
    onehot = onehot & (column != SPAN - 1)[None, :]
    return onehot.astype(np.float32)


def rms_scale(values):
    return lax.rsqrt(jnp.mean(values * values, axis=-1, keepdims=True) + NORM_EPS)


def gelu(v):
    return 0.5 * v * (1.0 + jnp.tanh(GELU_RATE * (v + GELU_CUBE * (v * v * v))))


def spread_bias(row):
    full = jnp.broadcast_to(row, (L, SPAN))
    return pltpu.roll(full, 0, 1, stride=1, stride_axis=0)[:, :L]


def attention_kernel(seqs, meta_ref, len_ref, tok_ref, gain_ref, own_ref, mate_ref, diag_ref, ctx_ref, w_scr, bias_scr):
    step = pl.program_id(0)
    third = own_ref.shape[2]
    pairs = 2 * third // PAIR
    width = 2 * third

    def place(low_ref, high_ref):
        for part in range(3):
            w_scr[:, part * width : part * width + third] = low_ref[part]
            w_scr[:, part * width + third : (part + 1) * width] = high_ref[part]

    @pl.when(step == 0)
    def _():
        @pl.when(meta_ref[1] == 0)
        def _():
            place(own_ref, mate_ref)

        @pl.when(meta_ref[1] == 1)
        def _():
            place(mate_ref, own_ref)

        for head in range(2 * pairs):
            bias_scr[head * L : (head + 1) * L, :] = spread_bias(
                diag_ref[pl.ds(meta_ref[2] * 2 * pairs + head, 1), :]
            )

    rows = tok_ref[...].reshape(seqs * L, D).astype(jnp.float32)
    normed = (rows * rms_scale(rows) * gain_ref[0:1, :]).astype(jnp.bfloat16)
    qkv = mm(normed, w_scr[...]).astype(jnp.bfloat16)
    low_lane = lax.broadcasted_iota(jnp.int32, (L, PAIR), 1) < HD
    key_row = lax.broadcasted_iota(jnp.int32, (2 * L, L), 0) % L
    for s in range(seqs):
        length = len_ref[meta_ref[0] + step * seqs + s]
        seen = key_row < length
        for p in range(pairs):
            at = slice(s * L, (s + 1) * L)
            query = qkv[at, p * PAIR : (p + 1) * PAIR]
            key = qkv[at, width + p * PAIR : width + (p + 1) * PAIR]
            value = qkv[at, 2 * width + p * PAIR : 2 * width + (p + 1) * PAIR]
            zero = jnp.zeros_like(key)
            key_two = jnp.concatenate(
                [jnp.where(low_lane, key, zero), jnp.where(low_lane, zero, key)], axis=0
            )
            value_two = jnp.concatenate(
                [jnp.where(low_lane, value, zero), jnp.where(low_lane, zero, value)], axis=0
            )
            scores = mm(key_two, query, NT) + bias_scr[p * 2 * L : (p + 1) * 2 * L, :]
            scores = jnp.where(seen, scores, MASKED).reshape(2, L, L)
            shifted = jnp.exp(scores - jnp.max(scores, axis=1, keepdims=True))
            probs = shifted * (1.0 / jnp.sum(shifted, axis=1, keepdims=True))
            probs = probs.astype(jnp.bfloat16).reshape(2 * L, L)
            ctx_ref[at, p * PAIR : (p + 1) * PAIR] = mm(probs, value_two, TN).astype(jnp.bfloat16)


def attention_part(meta, lengths, tokens, gains, own, mate, diag, own_seqs, seqs):
    width = 2 * own.shape[2]
    grid = own_seqs // seqs
    fixed = lambda *dims: pl.BlockSpec(dims, lambda i, m, n: (0,) * len(dims))
    return pl.pallas_call(
        functools.partial(attention_kernel, seqs),
        name="attend",
        grid_spec=pltpu.PrefetchScalarGridSpec(
            num_scalar_prefetch=2,
            grid=(grid,),
            in_specs=[
                pl.BlockSpec((seqs, L, D), lambda i, m, n: (m[0] // seqs + i, 0, 0)),
                fixed(2, D),
                fixed(*own.shape),
                fixed(*mate.shape),
                fixed(*diag.shape),
            ],
            out_specs=pl.BlockSpec((seqs * L, width), lambda i, m, n: (i, 0)),
            scratch_shapes=[
                pltpu.VMEM((D, 3 * width), jnp.bfloat16),
                pltpu.VMEM((width // HD * L, L), jnp.float32),
            ],
        ),
        out_shape=jax.ShapeDtypeStruct((own_seqs * L, width), jnp.bfloat16),
        compiler_params=pltpu.CompilerParams(
            dimension_semantics=("arbitrary",), vmem_limit_bytes=56 * MIB
        ),
        cost_estimate=pl.CostEstimate(
            flops=2 * own_seqs * L * width * (3 * D + 2 * L),
            bytes_accessed=own_seqs * L * (D + width) * 2 + 6 * D * width,
            transcendentals=own_seqs * width // HD * L * L,
        ),
    )(meta, lengths, tokens, gains, own, mate, diag)


def ffn_kernel(seqs, chunk, meta_ref, ca_ref, cb_ref, tok_ref, gain_ref, wa_ref, wb_ref, up_ref, down_ref, taps_ref):
    rows = tok_ref[...].reshape(seqs * L, D).astype(jnp.float32)
    middle = rows + mm(ca_ref[...], wa_ref[...]) + mm(cb_ref[...], wb_ref[...])
    normed = (middle * rms_scale(middle) * gain_ref[1:2, :]).astype(jnp.bfloat16)
    total = jnp.zeros_like(middle)
    for c in range(0, up_ref.shape[1], chunk):
        hidden = gelu(mm(normed, up_ref[:, c : c + chunk])).astype(jnp.bfloat16)
        total = total + mm(hidden, down_ref[c : c + chunk, :])
    taps_ref[...] = (middle + total).astype(jnp.bfloat16)


def ffn_part(meta, ctx_a, ctx_b, tokens, gains, w_out, w_up, w_down, own_seqs, seqs, chunk):
    width = ctx_a.shape[1]
    grid = own_seqs // seqs
    ff = w_up.shape[1]
    fixed = lambda *dims: pl.BlockSpec(dims, lambda i, m: (0,) * len(dims))
    return pl.pallas_call(
        functools.partial(ffn_kernel, seqs, chunk),
        name="feed",
        grid_spec=pltpu.PrefetchScalarGridSpec(
            num_scalar_prefetch=1,
            grid=(grid,),
            in_specs=[
                pl.BlockSpec((seqs * L, width), lambda i, m: (i, 0)),
                pl.BlockSpec((seqs * L, width), lambda i, m: (i, 0)),
                pl.BlockSpec((seqs, L, D), lambda i, m: (m[0] // seqs + i, 0, 0)),
                fixed(2, D),
                pl.BlockSpec((width, D), lambda i, m: (m[2], 0)),
                pl.BlockSpec((width, D), lambda i, m: (1 - m[2], 0)),
                fixed(*w_up.shape),
                fixed(*w_down.shape),
            ],
            out_specs=pl.BlockSpec((seqs * L, D), lambda i, m: (i, 0)),
        ),
        out_shape=jax.ShapeDtypeStruct((own_seqs * L, D), jnp.bfloat16),
        compiler_params=pltpu.CompilerParams(
            dimension_semantics=("arbitrary",), vmem_limit_bytes=60 * MIB
        ),
        cost_estimate=pl.CostEstimate(
            flops=2 * own_seqs * L * D * (D + 2 * ff),
            bytes_accessed=own_seqs * L * 3 * D * 2 + 2 * D * (D + 2 * ff),
            transcendentals=own_seqs * L * ff,
        ),
    )(meta, ctx_a, ctx_b, tokens, gains, w_out, w_out, w_up, w_down)


def pick_rows(step, phase, count):
    row = lax.broadcasted_iota(jnp.int32, (count, step * count), 0)
    column = lax.broadcasted_iota(jnp.int32, (count, step * count), 1)
    return (column == step * row + phase).astype(jnp.bfloat16)


def by_head_rows(block):
    head = lax.broadcasted_iota(jnp.int32, block.shape, 1) // SHD
    zero = jnp.zeros_like(block)
    return jnp.concatenate([jnp.where(head == h, block, zero) for h in range(SH)], axis=0)


def by_head_lanes(block):
    head = lax.broadcasted_iota(jnp.int32, block.shape, 0) // SHD
    zero = jnp.zeros_like(block)
    return jnp.concatenate([jnp.where(head == h, block, zero) for h in range(SH)], axis=1)


def lanes_of(stacked):
    return jnp.concatenate([stacked[h * L : (h + 1) * L] for h in range(SH)], axis=1)


def norm_back(unit, scale, gain, grad):
    scaled = grad * gain
    back = scale * (scaled - unit * jnp.mean(scaled * unit, axis=-1, keepdims=True))
    return back, jnp.sum(grad * unit, axis=0, keepdims=True)


def side_kernel(
    seqs,
    meta_ref,
    len_ref,
    taps_ref,
    x_ref,
    go_ref,
    gain_ref,
    w_ref,
    diag_ref,
    onehot_ref,
    out_ref,
    ig_ref,
    grow_ref,
    gsmall_ref,
    wqkv_scr,
    wup_scr,
    bias_scr,
    gbias_scr,
    p_scr,
    plow_scr,
    gdown_scr,
    gqkv_scr,
    gproj_scr,
    gup_scr,
    gback_scr,
    ggain_scr,
):
    step = pl.program_id(0)
    at_qkv, at_out, at_up, at_back = D, D + 3 * DS, D + 4 * DS, D + 8 * DS

    @pl.when(step == 0)
    def _():
        for t in range(3):
            wqkv_scr[t] = mm(pick_rows(3, t, DS), w_ref[at_qkv:at_out, :]).astype(jnp.bfloat16)
        for t in range(4):
            wup_scr[:, t * DS : (t + 1) * DS] = mm(
                pick_rows(4, t, DS), w_ref[at_up:at_back, :]
            ).astype(jnp.bfloat16)
        for head in range(SH):
            bias_scr[head * L : (head + 1) * L, :] = spread_bias(diag_ref[head : head + 1, :])
        for ref in (gbias_scr, gdown_scr, gqkv_scr, gproj_scr, gup_scr, gback_scr, ggain_scr):
            ref[...] = jnp.zeros_like(ref)

    rows = seqs * L
    gain_one, gain_two = gain_ref[0:1, :], gain_ref[1:2, :]
    gate = jax.nn.sigmoid(gain_ref[2:3, :])
    w_out = w_ref[at_out:at_up, :]
    w_back = w_ref[at_back : at_back + SFF, :]
    lengths = [len_ref[meta_ref[0] + step * seqs + s] for s in range(seqs)]
    key_row = lax.broadcasted_iota(jnp.int32, (SH, L, L), 1)
    own_row = lax.broadcasted_iota(jnp.int32, (L, DS), 0)
    taps = taps_ref[...]
    x = x_ref[...].reshape(rows, DS)
    grad_out = jnp.concatenate(
        [jnp.where(own_row < lengths[s], go_ref[s], 0.0) for s in range(seqs)], axis=0
    )

    tapped = mm(taps, w_ref[0:D, :])
    mixed = gate * x + (1.0 - gate) * tapped
    scale_one = rms_scale(mixed)
    unit_one = mixed * scale_one
    normed_one = (unit_one * gain_one).astype(jnp.bfloat16)
    query = mm(normed_one, wqkv_scr[0]).astype(jnp.bfloat16)
    key = mm(normed_one, wqkv_scr[1]).astype(jnp.bfloat16)
    value = mm(normed_one, wqkv_scr[2]).astype(jnp.bfloat16)

    context = []
    for s in range(seqs):
        at = slice(s * L, (s + 1) * L)
        scores = mm(by_head_rows(key[at]), query[at], NT) + bias_scr[...]
        scores = scores.reshape(SH, L, L)
        scores = jnp.where(key_row < lengths[s], scores, MASKED)
        shifted = jnp.exp(scores - jnp.max(scores, axis=1, keepdims=True))
        probs = shifted * (1.0 / jnp.sum(shifted, axis=1, keepdims=True))
        p_scr[s] = probs
        probs_low = probs.astype(jnp.bfloat16).reshape(SH * L, L)
        plow_scr[s] = probs_low
        turned = mm(by_head_lanes(value[at].T), probs_low)
        context.append(turned.T.astype(jnp.bfloat16))
    context = jnp.concatenate(context, axis=0)

    middle = mixed + mm(context, w_out)
    scale_two = rms_scale(middle)
    unit_two = middle * scale_two
    normed_two = (unit_two * gain_two).astype(jnp.bfloat16)
    pre = mm(normed_two, wup_scr[...])
    square = pre * pre
    bend = jnp.tanh(GELU_RATE * pre * (1.0 + GELU_CUBE * square))
    half = 0.5 * (1.0 + bend)
    hidden = (pre * half).astype(jnp.bfloat16)
    slope = half + (0.5 * GELU_RATE) * pre * (1.0 - bend * bend) * (1.0 + 3.0 * GELU_CUBE * square)
    out_ref[...] = (middle + mm(hidden, w_back)).reshape(seqs, L, DS)

    grad_low = grad_out.astype(jnp.bfloat16)
    gback_scr[...] += mm(grad_low, hidden, TN)
    grad_pre = (mm(grad_low, w_back, NT) * slope).astype(jnp.bfloat16)
    gup_scr[...] += mm(normed_two, grad_pre, TN)
    back_two, gain_two_grad = norm_back(
        unit_two, scale_two, gain_two, mm(grad_pre, wup_scr[...], NT)
    )
    ggain_scr[1:2, :] += gain_two_grad
    grad_middle = grad_out + back_two
    grad_attended = grad_middle.astype(jnp.bfloat16)
    gproj_scr[...] += mm(context, grad_attended, TN)
    grad_context = mm(grad_attended, w_out, NT).astype(jnp.bfloat16)

    grad_query, grad_key, grad_value = [], [], []
    for s in range(seqs):
        at = slice(s * L, (s + 1) * L)
        grad_probs = mm(by_head_rows(value[at]), grad_context[at], NT).reshape(SH, L, L)
        probs = p_scr[s]
        row_dot = jnp.sum(probs * grad_probs, axis=1, keepdims=True)
        grad_scores = (probs * (grad_probs - row_dot)).astype(jnp.bfloat16).reshape(SH * L, L)
        gbias_scr[...] += grad_scores.astype(jnp.float32)
        turned = mm(by_head_lanes(key[at].T), grad_scores)
        grad_query.append(turned.T.astype(jnp.bfloat16))
        grad_key.append(mm(lanes_of(grad_scores), by_head_rows(query[at])).astype(jnp.bfloat16))
        grad_value.append(
            mm(lanes_of(plow_scr[s]), by_head_rows(grad_context[at])).astype(jnp.bfloat16)
        )
    grad_query = jnp.concatenate(grad_query, axis=0)
    grad_key = jnp.concatenate(grad_key, axis=0)
    grad_value = jnp.concatenate(grad_value, axis=0)

    grad_normed = mm(grad_query, wqkv_scr[0], NT)
    grad_normed += mm(grad_key, wqkv_scr[1], NT)
    grad_normed += mm(grad_value, wqkv_scr[2], NT)
    gqkv_scr[0] += mm(normed_one, grad_query, TN)
    gqkv_scr[1] += mm(normed_one, grad_key, TN)
    gqkv_scr[2] += mm(normed_one, grad_value, TN)
    back_one, gain_one_grad = norm_back(unit_one, scale_one, gain_one, grad_normed)
    ggain_scr[0:1, :] += gain_one_grad
    grad_mixed = grad_middle + back_one
    ig_ref[...] = (gate * grad_mixed).reshape(seqs, L, DS)
    grad_tap = ((1.0 - gate) * grad_mixed).astype(jnp.bfloat16)
    gdown_scr[...] += mm(grad_tap, taps, TN)
    ggain_scr[2:3, :] += jnp.sum(grad_mixed * (x - tapped), axis=0, keepdims=True)

    @pl.when(step == pl.num_programs(0) - 1)
    def _():
        low = lambda v: v.astype(jnp.bfloat16)
        pad = jnp.zeros((grow_ref.shape[0], grow_ref.shape[1] - DS), jnp.bfloat16)
        grow_ref[:, DS:] = pad
        grow_ref[0:D, 0:DS] = low(gdown_scr[...].T)
        spread = mm(pick_rows(3, 0, DS), low(gqkv_scr[0]), TN)
        for t in range(1, 3):
            spread = spread + mm(pick_rows(3, t, DS), low(gqkv_scr[t]), TN)
        grow_ref[at_qkv:at_out, 0:DS] = low(spread)
        grow_ref[at_out:at_up, 0:DS] = low(gproj_scr[...])
        spread = mm(pick_rows(4, 0, DS), low(gup_scr[:, 0:DS]), TN)
        for t in range(1, 4):
            spread = spread + mm(pick_rows(4, t, DS), low(gup_scr[:, t * DS : (t + 1) * DS]), TN)
        grow_ref[at_up:at_back, 0:DS] = low(spread)
        grow_ref[at_back : at_back + SFF, 0:DS] = low(gback_scr[...].T)
        flip_row = lax.broadcasted_iota(jnp.int32, (L, L), 0)
        flip_column = lax.broadcasted_iota(jnp.int32, (L, L), 1)
        flip = (flip_row + flip_column == L - 1).astype(jnp.float32)
        diagonals = []
        for head in range(SH):
            square = lax.dot_general(
                flip,
                gbias_scr[head * L : (head + 1) * L, :],
                NN,
                precision=PRECISE,
                preferred_element_type=jnp.float32,
            )
            full = jnp.concatenate([square, jnp.zeros_like(square)], axis=1)
            rolled = pltpu.roll(full, 0, 1, stride=1, stride_axis=0)
            diagonals.append(jnp.sum(rolled, axis=0, keepdims=True))
        diagonals = jnp.concatenate(diagonals, axis=0)
        gsmall_ref[...] = jnp.zeros_like(gsmall_ref)
        gsmall_ref[0:3, 0:DS] = ggain_scr[0:3, :] * jnp.concatenate(
            [jnp.ones((2, DS), jnp.float32), gate * (1.0 - gate)], axis=0
        )
        gsmall_ref[4 : 4 + SH, 0 : onehot_ref.shape[0]] = lax.dot_general(
            diagonals, onehot_ref[...], NT, precision=PRECISE, preferred_element_type=jnp.float32
        )


def side_part(meta, lengths, taps, side_input, output_grad, gains, w_rows, diag, onehot, seqs):
    own_seqs = side_input.shape[0]
    grid = own_seqs // seqs
    fixed = lambda *dims: pl.BlockSpec(dims, lambda i, m, n: (0,) * len(dims))
    block = pl.BlockSpec((seqs, L, DS), lambda i, m, n: (i, 0, 0))
    f32, bf16 = jnp.float32, jnp.bfloat16
    return pl.pallas_call(
        functools.partial(side_kernel, seqs),
        name="side",
        grid_spec=pltpu.PrefetchScalarGridSpec(
            num_scalar_prefetch=2,
            grid=(grid,),
            in_specs=[
                pl.BlockSpec((seqs * L, D), lambda i, m, n: (i, 0)),
                block,
                block,
                fixed(*gains.shape),
                fixed(*w_rows.shape),
                fixed(*diag.shape),
                fixed(*onehot.shape),
            ],
            out_specs=[block, block, fixed(w_rows.shape[0], L), fixed(16, L)],
            scratch_shapes=[
                pltpu.VMEM((3, DS, DS), bf16),
                pltpu.VMEM((DS, SFF), bf16),
                pltpu.VMEM((SH * L, L), f32),
                pltpu.VMEM((SH * L, L), f32),
                pltpu.VMEM((seqs, SH, L, L), f32),
                pltpu.VMEM((seqs, SH * L, L), bf16),
                pltpu.VMEM((DS, D), f32),
                pltpu.VMEM((3, DS, DS), f32),
                pltpu.VMEM((DS, DS), f32),
                pltpu.VMEM((DS, SFF), f32),
                pltpu.VMEM((DS, SFF), f32),
                pltpu.VMEM((8, DS), f32),
            ],
        ),
        out_shape=[
            jax.ShapeDtypeStruct(side_input.shape, f32),
            jax.ShapeDtypeStruct(side_input.shape, f32),
            jax.ShapeDtypeStruct((w_rows.shape[0], L), bf16),
            jax.ShapeDtypeStruct((16, L), f32),
        ],
        compiler_params=pltpu.CompilerParams(
            dimension_semantics=("arbitrary",), vmem_limit_bytes=56 * MIB
        ),
        cost_estimate=pl.CostEstimate(
            flops=own_seqs * 300_000_000,
            bytes_accessed=own_seqs * L * (2 * D + 16 * DS),
            transcendentals=own_seqs * L * (SH * L + SFF),
        ),
    )(meta, lengths, taps, side_input, output_grad, gains, w_rows, diag, onehot)


def adamw_update(weight_now, first_now, second_now, gradient, rate, decay_rate):
    first_new = BETA_ONE * first_now + (1.0 - BETA_ONE) * gradient
    second_new = BETA_TWO * second_now + (1.0 - BETA_TWO) * gradient * gradient
    first_hat = first_new / (1.0 - BETA_ONE**ADAM_STEP)
    second_hat = second_new / (1.0 - BETA_TWO**ADAM_STEP)
    weight_new = weight_now - rate * (
        first_hat / (jnp.sqrt(second_hat) + ADAM_EPS) + decay_rate * weight_now
    )
    return (first_new, second_new, weight_new)


def swap(values, distance):
    size = lax.axis_size("mp")
    return lax.ppermute(values, "mp", [(i, i ^ distance) for i in range(size)])


def exchange(values):
    return lax.all_to_all(values, ("batch", "mp"), split_axis=0, concat_axis=0, tiled=True)


def on_device(
    tokens,
    lengths,
    base_gains,
    base_qkv,
    base_out,
    base_up,
    base_down,
    base_table,
    side_input,
    output_grad,
    side_weights,
    weights_first,
    weights_second,
    side_gains,
    gains_first,
    gains_second,
    side_table,
    table_first,
    table_second,
):
    devices = lax.axis_size(("batch", "mp"))
    model_index = lax.axis_index("mp")
    own_seqs = side_input.shape[0]
    shard_rows = side_weights.shape[0] // DS
    buckets = side_table.shape[0]
    group = model_index // 2
    near = jnp.stack([model_index * own_seqs, model_index % 2, group]).astype(jnp.int32)
    far = jnp.stack([model_index * own_seqs, model_index % 2, 1 - group]).astype(jnp.int32)

    qkv_mate = swap(base_qkv, 1)
    qkv_far = swap(base_qkv, 2)
    qkv_far_mate = swap(qkv_far, 1)
    low_rows = side_weights.astype(jnp.bfloat16).reshape(1, shard_rows, DS)
    w_rows = exchange(jnp.broadcast_to(low_rows, (devices, shard_rows, DS)))
    w_rows = w_rows.reshape(devices * shard_rows, DS)

    onehot = jnp.asarray(diagonal_onehot(buckets))
    base_diag = jnp.dot(base_table.T, onehot, precision=PRECISE)
    side_diag = jnp.dot(side_table.T, onehot, precision=PRECISE)

    ctx_near = attention_part(
        near, lengths, tokens, base_gains, base_qkv, qkv_mate, base_diag, own_seqs, 2
    )
    ctx_far = attention_part(
        far, lengths, tokens, base_gains, qkv_far, qkv_far_mate, base_diag, own_seqs, 2
    )
    taps = ffn_part(
        near, ctx_near, ctx_far, tokens, base_gains, base_out, base_up, base_down, own_seqs, 4, 1024
    )
    side_output, input_grad, grad_rows, grad_small = side_part(
        near,
        lengths,
        taps,
        side_input,
        output_grad,
        side_gains,
        w_rows,
        side_diag,
        jnp.asarray(gradient_onehot(buckets)),
        2,
    )

    small_high = grad_small.astype(jnp.bfloat16)
    small_low = (grad_small - small_high.astype(jnp.float32)).astype(jnp.bfloat16)
    small = jnp.concatenate([small_high, small_low], axis=0)
    outgoing = jnp.concatenate(
        [
            grad_rows.reshape(devices, shard_rows, L),
            jnp.broadcast_to(small[None], (devices,) + small.shape),
        ],
        axis=1,
    )
    summed = jnp.sum(exchange(outgoing).astype(jnp.float32), axis=0)
    grad_shard = summed[:shard_rows, :DS]
    small_total = summed[shard_rows : shard_rows + 16] + summed[shard_rows + 16 :]
    gains_total = small_total[0:3, :DS]
    table_total = small_total[4 : 4 + SH, :buckets].T
    square = jnp.sum(grad_shard * grad_shard)
    squares = exchange(jnp.broadcast_to(square, (devices, L)))
    grad_norm = jnp.sqrt(
        jnp.sum(squares[:, 0])
        + jnp.sum(gains_total * gains_total)
        + jnp.sum(table_total * table_total)
    )
    factor = CLIP_NORM / jnp.maximum(grad_norm, CLIP_NORM)
    weights_moment, weights_square, weights_new = adamw_update(
        side_weights,
        weights_first,
        weights_second,
        factor * grad_shard.reshape(-1),
        RATE_MATRIX,
        WEIGHT_DECAY,
    )
    gains_moment, gains_square, gains_new = adamw_update(
        side_gains, gains_first, gains_second, factor * gains_total, RATE_SMALL, 0.0
    )
    table_moment, table_square, table_new = adamw_update(
        side_table, table_first, table_second, factor * table_total, RATE_SMALL, 0.0
    )
    return (
        side_output,
        input_grad,
        grad_norm,
        weights_moment,
        weights_square,
        weights_new,
        weights_new.astype(jnp.bfloat16),
        gains_moment,
        gains_square,
        gains_new,
        table_moment,
        table_square,
        table_new,
    )


def solution(mesh):
    return jax.shard_map(
        on_device,
        mesh=mesh,
        in_specs=(
            P("batch", None, None),
            P("batch"),
            P(),
            P(None, None, "mp"),
            P(),
            P(),
            P(),
            P(),
            P(("batch", "mp"), None, None),
            P(("batch", "mp"), None, None),
            P(("batch", "mp")),
            P(("batch", "mp")),
            P(("batch", "mp")),
            P(),
            P(),
            P(),
            P(),
            P(),
            P(),
        ),
        out_specs=(
            P(("batch", "mp"), None, None),
            P(("batch", "mp"), None, None),
            P(),
            P(("batch", "mp")),
            P(("batch", "mp")),
            P(("batch", "mp")),
            P(("batch", "mp")),
            P(),
            P(),
            P(),
            P(),
            P(),
            P(),
        ),
        check_vma=False,
    )
```

time: 777 us -> 228 us (0.29); the launches traced: 766 us -> 228 us
  local copies, waits for them, and re-layouts: 227 us -> 19.9 us
  matrix products: 191 us -> 1.49 us
  Pallas kernels: 0 us -> 142 us
  blocking collectives: 131 us -> 0 us
  waiting for transfers between devices: 118 us -> 35 us
  other arithmetic: 73.6 us -> 8.17 us
  between operations: 18.3 us -> 4 us
  starting transfers between devices: 5.1 us -> 17.3 us
    dot_general x109 -> x2, matrix products: 145 us -> 1.49 us  [the longest x1 0.75 us: on_device(): base_diag = jnp.dot(base_table.T, onehot, precision=PRECISE)]
    pallas_call x0 -> x4, Pallas kernels: none -> 142 us  [the longest x1 57.1 us: side_part(): pl.pallas_call(functools.partial(side_kernel, seqs), name='side', grid_sp...]
    unnamed x2 -> x0, waiting for transfers between devices: 118 us -> none
    all_gather x1 -> x0, blocking collectives: 90.6 us -> none  [on_device(): lax.all_gather(side_weights.astype(jnp.bfloat16), ('batch', 'mp'), axis=0...]
    dynamic_slice x56 -> x0, local copies, waits for them, and re-layouts: 55.3 us -> none  [the longest x48 52.2 us: base_attention(): return lax.map(one_block, shaped).reshape(count, L, heads * depth)]
    psum x1 -> x0, blocking collectives: 40.5 us -> none  [on_device(): lax.psum((gains_part, table_grad, jnp.sum(grad_shard * grad_shard)), ('ba...]
    unnamed x1 -> x0, matrix products: 34.4 us -> none
    dynamic_update_slice x42 -> x0, local copies, waits for them, and re-layouts: 32.3 us -> none  [the longest x24 16.8 us: base_attention(): return lax.map(one_block, shaped).reshape(count, L, heads * depth)]
  transfers between devices with their start and end apart: 2 -> 6, of which waited for: 1 -> 4; matrix products, arithmetic and copies ran while one was open for 4% -> 9% of each run, Pallas kernels for 0% -> 9%
where the time goes in v1:
time: 228 us
  Pallas kernels  142 us (62%)
  waiting for transfers between devices  35 us (15%)
  local copies, waits for them, and re-layouts  19.9 us (9%)
  starting transfers between devices  17.3 us (8%)
  other arithmetic  8.17 us (4%)
  between operations  4 us (2%)
    pallas_call x1, Pallas kernels, side_part(): pl.pallas_call(functools.partial(side_kernel, seqs), name='side', grid_sp...  57.1 us
    pallas_call x1, Pallas kernels, ffn_part(): pl.pallas_call(functools.partial(ffn_kernel, seqs, chunk), name='feed', g...  45.4 us
    pallas_call x2, Pallas kernels, attention_part(): pl.pallas_call(functools.partial(attention_kernel, seqs), name='attend',...  39.5 us
    all_to_all x3, waiting for transfers between devices, exchange(): lax.all_to_all(values, ('batch', 'mp'), split_axis=0, concat_axis=0, tile...  23 us
    all_to_all x3, starting transfers between devices, exchange(): lax.all_to_all(values, ('batch', 'mp'), split_axis=0, concat_axis=0, tile...  14.2 us
    ppermute x3, waiting for transfers between devices, swap(): return lax.ppermute(values, 'mp', [(i, i ^ distance) for i in range(size)])  12 us
    unnamed x35, local copies, waits for them, and re-layouts  9.24 us
    ppermute x3, local copies, waits for them, and re-layouts, swap(): return lax.ppermute(values, 'mp', [(i, i ^ distance) for i in range(size)])  6.13 us
  transfers between devices with their start and end apart: 6, of which 4 were waited for; matrix products, arithmetic and copies ran while one was open for 9% of the time, Pallas kernels for 9%

profile of v1, /device:TPU:0, one launch (start us, length us, event | category | flops | bytes accessed | tf_op | source)
XLA Modules:
  0.0 227.8 jit_solution(217896302890299872)
XLA Ops:
  0.6 0.0 copy-start
  0.7 3.0 %collective-permute-start.1 = (bf16[3,768,192]{1,2,0:T(8,128)(2,1)}, bf16[3,768,192]{1,2,0:T(8,128)(2,1)}, u32[]{:S(2)}, u32[]{:S(2)}) collective-permute-start(bf16[3,768,192]{1,2,0:T(8,128)(2,1)} %param.24), channel_id=1, source_target_pairs={{0,2},{1,3},{2,0},{3,1},{4,6},{5,7},{6,4},{7,5},{8,10},{9,11},{10,... | collective-permute-start | bytes 2654216 | tf_op jit(solution)/shard_map/ppermute | solution.py:498
  3.7 0.0 collective-permute-start
  3.7 0.7 convert_element_type.18
  4.4 0.1 broadcast_in_dim.16
  4.5 0.9 broadcast_in_dim.17
  5.4 5.0 %all-to-all-start = ((bf16[32,60,96]{2,1,0:T(8,128)(2,1)}), bf16[32,60,96]{2,1,0:T(8,128)(2,1)S(1)}, u32[]{:S(2)}, u32[]{:S(2)}) async-start(bf16[32,60,96]{2,1,0:T(8,128)(2,1)} %broadcast_in_dim.17), calls=%async_computation | async-start | bytes 1048576 | tf_op jit(solution)/shard_map/all_to_all | solution.py:502
  10.5 1.4 copy.64.own_ref
  11.9 1.6 copy.68.x_ref
  13.5 1.6 copy.69.go_ref
  15.2 0.6 pad_add_fusion.meta_ref
  15.8 0.7 convolution_bitcast_fusion.1.diag_ref
  16.5 12.0 %collective-permute-done.1 = bf16[3,768,192]{1,2,0:T(8,128)(2,1)} collective-permute-done((bf16[3,768,192]{1,2,0:T(8,128)(2,1)}, bf16[3,768,192]{1,2,0:T(8,128)(2,1)}, u32[]{:S(2)}, u32[]{:S(2)}) %collective-permute-start.1) | collective-permute-done | bytes 884768 | tf_op jit(solution)/shard_map/ppermute | solution.py:498
  28.6 0.6 pad_add_fusion.2.meta_ref
  29.1 0.7 convolution_bitcast_fusion.diag_ref
  29.9 0.5 all-to-all-done
  30.4 1.0 reshape.40.w_ref
  31.3 2.4 %copy.66.own_ref = bf16[3,768,192]{2,1,0:T(8,128)(2,1)} copy(bf16[3,768,192]{1,2,0:T(8,128)(2,1)} %collective-permute-done.1) | data formatting | bytes 1769472 | tf_op jit(solution)/shard_map/ppermute | solution.py:498
  33.7 2.3 %copy.65.mate_ref = bf16[3,768,192]{2,1,0:T(8,128)(2,1)} copy(bf16[3,768,192]{1,2,0:T(8,128)(2,1)} %collective-permute-done) | data formatting | bytes 1769472 | tf_op jit(solution)/shard_map/ppermute | solution.py:498
  36.1 19.7 %attend.2.ca_ref = bf16[3072,384]{1,0:T(8,128)(2,1)} custom-call(s32[3]{0:T(128)} %pad_add_fusion.meta_ref, s32[96]{0:T(128)} %len_ref.5, bf16[96,128,768]{2,1,0:T(8,128)(2,1)} %tok_ref.5, f32[2,768]{1,0:T(2,128)} %gain_ref.6, bf16[3,768,192]{2,1,0:T(8,128)(2,1)} %copy.64.own_ref, bf16[3,768,192]{2,1,0:T(8,128)(2,1)} %copy.65.mate_ref, ...), custom_call_target="tpu_custom_call" | custom-call | flops 6039797760 | bytes 8847360 | tf_op jit(solution)/shard_map/attend/pallas_call | solution.py:146
  55.8 1.4 copy.67.mate_ref
  57.2 19.7 %attend.3.cb_ref = bf16[3072,384]{1,0:T(8,128)(2,1)} custom-call(s32[3]{0:T(128)} %pad_add_fusion.2.meta_ref, s32[96]{0:T(128)} %len_ref.5, bf16[96,128,768]{2,1,0:T(8,128)(2,1)} %tok_ref.5, f32[2,768]{1,0:T(2,128)} %gain_ref.6, bf16[3,768,192]{2,1,0:T(8,128)(2,1)} %copy.66.own_ref, bf16[3,768,192]{2,1,0:T(8,128)(2,1)} %copy.67.mate_ref, ...), custom_call_target="tpu_custom_call" | custom-call | flops 6039797760 | bytes 8847360 | tf_op jit(solution)/shard_map/attend/pallas_call | solution.py:146
  76.9 45.4 %feed.1.taps_ref = bf16[3072,768]{1,0:T(8,128)(2,1)} custom-call(s32[3]{0:T(128)} %pad_add_fusion.meta_ref, bf16[3072,384]{1,0:T(8,128)(2,1)} %attend.2.ca_ref, bf16[3072,384]{1,0:T(8,128)(2,1)} %attend.3.cb_ref, bf16[96,128,768]{2,1,0:T(8,128)(2,1)} %tok_ref.5, f32[2,768]{1,0:T(2,128)} %gain_ref.6, bf16[768,768]{1,0:T(8,128)(2,1)} %wb_ref.1, ...), custom_call_target="tpu_custom_call" | custom-call | flops 32614907904 | bytes 24772608 | tf_op jit(solution)/shard_map/feed/pallas_call | solution.py:193
  122.4 57.1 %side.1 = (f32[24,128,96]{2,1,0:T(8,128)}, f32[24,128,96]{2,1,0:T(8,128)}, bf16[1920,128]{1,0:T(8,128)(2,1)}, f32[16,128]{1,0:T(8,128)}) custom-call(s32[3]{0:T(128)} %pad_add_fusion.meta_ref, s32[96]{0:T(128)} %len_ref.5, bf16[3072,768]{1,0:T(8,128)(2,1)} %feed.1.taps_ref, f32[24,128,96]{2,1,0:T(8,128)} %copy.68.x_ref, f32[24,128,96]{2,1,0:T(8,128)} %copy.69.go_ref, ...), custom_call_target="tpu_custom_call" | custom-call | flops 7200000000 | bytes 9437184 | tf_op jit(solution)/shard_map/side/pallas_call | solution.py:437
  179.5 0.8 subtract_convert_fusion
  180.3 1.1 reshape.41
  181.4 1.0 pad_maximum_fusion
  182.5 5.6 %all-to-all-start.1 = ((bf16[32,92,128]{2,1,0:T(8,128)(2,1)}), bf16[32,92,128]{2,1,0:T(8,128)(2,1)S(1)}, u32[]{:S(2)}, u32[]{:S(2)}) async-start(bf16[32,92,128]{2,1,0:T(8,128)(2,1)} %pad_maximum_fusion), calls=%async_computation.1 | async-start | bytes 1572864 | tf_op jit(solution)/shard_map/all_to_all | solution.py:502
  188.1 3.0 %copy.71 = f32[24,128,96]{1,2,0:T(8,128)} copy(f32[24,128,96]{2,1,0:T(8,128)} %get-tuple-element.73) | data formatting | bytes 2359296
  191.1 0.0 copy-start.10
  191.1 0.0 copy-start.11
  191.1 0.0 copy-start.6
  191.2 0.0 copy-start.8
  191.2 0.0 copy-start.9
  191.2 1.5 copy.72
  192.7 16.1 %all-to-all-done.1 = bf16[32,92,128]{2,1,0:T(8,128)(2,1)S(1)} async-done(((bf16[32,92,128]{2,1,0:T(8,128)(2,1)}), bf16[32,92,128]{2,1,0:T(8,128)(2,1)S(1)}, u32[]{:S(2)}, u32[]{:S(2)}) %all-to-all-start.1) | async-done | bytes 753696 | tf_op jit(solution)/shard_map/all_to_all | solution.py:502
  208.7 0.1 convert_reduce_fusion
  208.8 0.6 multiply_reduce_fusion
  209.4 0.6 multiply_reduce_fusion.1
  210.0 1.3 broadcast_in_dim.19
  211.3 3.6 %all-to-all-start.2 = ((f32[32,1,128]{2,1,0:T(1,128)}), f32[32,1,128]{2,1,0:T(1,128)S(1)}, u32[]{:S(2)}, u32[]{:S(2)}) async-start(f32[32,1,128]{2,1,0:T(1,128)} %broadcast_in_dim.19), calls=%async_computation.2 | async-start | bytes 32768 | tf_op jit(solution)/shard_map/all_to_all | solution.py:502
  214.9 0.6 multiply_reduce_fusion.2
  215.5 6.5 %all-to-all-done.2 = f32[32,1,128]{2,1,0:T(1,128)S(1)} async-done(((f32[32,1,128]{2,1,0:T(1,128)}), f32[32,1,128]{2,1,0:T(1,128)S(1)}, u32[]{:S(2)}, u32[]{:S(2)}) %all-to-all-start.2) | async-done | bytes 16416 | tf_op jit(solution)/shard_map/all_to_all | solution.py:502
  222.0 0.6 slice_reduce_fusion
  224.7 0.1 mul.157
  224.8 0.6 multiply_subtract_fusion.2
  225.4 0.6 multiply_subtract_fusion.1
  226.0 0.6 fusion.7
  (31 shorter events, 0.1 us)
Async XLA Ops:
  0.6 15.1 %copy-start = (f32[32,12]{0,1:T(8,128)S(1)}, f32[32,12]{0,1:T(8,128)}, u32[]{:S(2)}) copy-start(f32[32,12]{0,1:T(8,128)} %param.28) | copy-start | bytes 4612
  0.7 9.8 %copy-start.4 = (bf16[3,768,192]{1,2,0:T(8,128)(2,1)S(1)}, bf16[3,768,192]{1,2,0:T(8,128)(2,1)}, u32[]{:S(2)}) copy-start(bf16[3,768,192]{1,2,0:T(8,128)(2,1)} %param.24) | copy-start | bytes 2654212
  0.7 27.9 %collective-permute-start.1 = (bf16[3,768,192]{1,2,0:T(8,128)(2,1)}, bf16[3,768,192]{1,2,0:T(8,128)(2,1)}, u32[]{:S(2)}, u32[]{:S(2)}) collective-permute-start(bf16[3,768,192]{1,2,0:T(8,128)(2,1)} %param.24), channel_id=1, source_target_pairs={{0,2},{1,3},{2,0},{3,1},{4,6},{5,7},{6,4},{7,5},{8,10},{9,11},{10,... | collective-permute-start | bytes 2654216 | tf_op jit(solution)/shard_map/ppermute | solution.py:498
  3.7 30.1 %collective-permute-start = (bf16[3,768,192]{1,2,0:T(8,128)(2,1)}, bf16[3,768,192]{1,2,0:T(8,128)(2,1)}, u32[]{:S(2)}, u32[]{:S(2)}) collective-permute-start(bf16[3,768,192]{1,2,0:T(8,128)(2,1)} %param.24), channel_id=1, source_target_pairs={{0,1},{1,0},{2,3},{3,2},{4,5},{5,4},{6,7},{7,6},{8,9},{9,8},{10,11... | collective-permute-start | bytes 2654216 | tf_op jit(solution)/shard_map/ppermute | solution.py:498
  5.4 6.5 %copy-start.2 = (f32[24,128,96]{1,2,0:T(8,128)S(1)}, f32[24,128,96]{1,2,0:T(8,128)}, u32[]{:S(2)}) copy-start(f32[24,128,96]{1,2,0:T(8,128)} %param.29) | copy-start | bytes 3538948
  5.4 24.9 %all-to-all-start = ((bf16[32,60,96]{2,1,0:T(8,128)(2,1)}), bf16[32,60,96]{2,1,0:T(8,128)(2,1)S(1)}, u32[]{:S(2)}, u32[]{:S(2)}) async-start(bf16[32,60,96]{2,1,0:T(8,128)(2,1)} %broadcast_in_dim.17), calls=%async_computation | async-start | bytes 1048576 | tf_op jit(solution)/shard_map/all_to_all | solution.py:502
  11.9 1.6 copy-start.3
  13.5 2.2 copy-start.5
  13.5 15.6 %copy-start.7 = (f32[32,12]{0,1:T(8,128)S(1)}, f32[32,12]{0,1:T(8,128)}, u32[]{:S(2)}) copy-start(f32[32,12]{0,1:T(8,128)} %param.37) | copy-start | bytes 4612
  28.6 27.2 %collective-permute-start.2 = (bf16[3,768,192]{1,2,0:T(8,128)(2,1)}, bf16[3,768,192]{1,2,0:T(8,128)(2,1)S(1)}, u32[]{:S(2)}, u32[]{:S(2)}) collective-permute-start(bf16[3,768,192]{1,2,0:T(8,128)(2,1)} %collective-permute-done.1), channel_id=1, source_target_pairs={{0,1},{1,0},{2,3},{3,2},{4,5},{5,4},{6,7},{7,6},{8,9},{9,8},{10,11... | collective-permute-start | bytes 2654216 | tf_op jit(solution)/shard_map/ppermute | solution.py:498
  182.5 26.2 %all-to-all-start.1 = ((bf16[32,92,128]{2,1,0:T(8,128)(2,1)}), bf16[32,92,128]{2,1,0:T(8,128)(2,1)S(1)}, u32[]{:S(2)}, u32[]{:S(2)}) async-start(bf16[32,92,128]{2,1,0:T(8,128)(2,1)} %pad_maximum_fusion), calls=%async_computation.1 | async-start | bytes 1572864 | tf_op jit(solution)/shard_map/all_to_all | solution.py:502
  188.1 3.0 %copy-start.1 = (f32[24,128,96]{2,1,0:T(8,128)S(1)}, f32[24,128,96]{2,1,0:T(8,128)}, u32[]{:S(2)}) copy-start(f32[24,128,96]{2,1,0:T(8,128)} %get-tuple-element.74) | copy-start | bytes 3538948
  191.1 33.6 %copy-start.12 = (f32[3,96]{1,0:T(4,128)S(1)}, f32[3,96]{1,0:T(4,128)}, u32[]{:S(2)}) copy-start(f32[3,96]{1,0:T(4,128)} %gain_ref.7) | copy-start | bytes 3460
  191.1 33.6 %copy-start.13 = (f32[3,96]{1,0:T(4,128)S(1)}, f32[3,96]{1,0:T(4,128)}, u32[]{:S(2)}) copy-start(f32[3,96]{1,0:T(4,128)} %param.36) | copy-start | bytes 3460
  191.1 33.6 %copy-start.14 = (f32[3,96]{1,0:T(4,128)S(1)}, f32[3,96]{1,0:T(4,128)}, u32[]{:S(2)}) copy-start(f32[3,96]{1,0:T(4,128)} %param.35) | copy-start | bytes 3460
  191.1 34.3 %copy-start.10 = (f32[32,12]{0,1:T(8,128)S(1)}, f32[32,12]{0,1:T(8,128)}, u32[]{:S(2)}) copy-start(f32[32,12]{0,1:T(8,128)} %param.39) | copy-start | bytes 4612
  191.1 34.2 %copy-start.11 = (f32[32,12]{0,1:T(8,128)S(1)}, f32[32,12]{0,1:T(8,128)}, u32[]{:S(2)}) copy-start(f32[32,12]{0,1:T(8,128)} %param.38) | copy-start | bytes 4612
  191.1 34.9 %copy-start.6 = (f32[5760]{0:T(1024)S(1)}, f32[5760]{0:T(1024)}, u32[]{:S(2)}) copy-start(f32[5760]{0:T(1024)} %param.31) | copy-start | bytes 69124
  191.2 34.9 %copy-start.8 = (f32[5760]{0:T(1024)S(1)}, f32[5760]{0:T(1024)}, u32[]{:S(2)}) copy-start(f32[5760]{0:T(1024)} %param.33) | copy-start | bytes 69124
  191.2 34.8 %copy-start.9 = (f32[5760]{0:T(1024)S(1)}, f32[5760]{0:T(1024)}, u32[]{:S(2)}) copy-start(f32[5760]{0:T(1024)} %param.32) | copy-start | bytes 69124
  211.3 10.7 %all-to-all-start.2 = ((f32[32,1,128]{2,1,0:T(1,128)}), f32[32,1,128]{2,1,0:T(1,128)S(1)}, u32[]{:S(2)}, u32[]{:S(2)}) async-start(f32[32,1,128]{2,1,0:T(1,128)} %broadcast_in_dim.19), calls=%async_computation.2 | async-start | bytes 32768 | tf_op jit(solution)/shard_map/all_to_all | solution.py:502

commit v2 on v1

--- a/solution.py
+++ b/solution.py
@@ -87,14 +87,14 @@
 
 def attention_kernel(seqs, meta_ref, len_ref, tok_ref, gain_ref, own_ref, mate_ref, diag_ref, ctx_ref, w_scr, bias_scr):
     step = pl.program_id(0)
-    third = own_ref.shape[2]
-    pairs = 2 * third // PAIR
+    third = own_ref.shape[1]
     width = 2 * third
+    pairs = width // PAIR
 
     def place(low_ref, high_ref):
         for part in range(3):
-            w_scr[:, part * width : part * width + third] = low_ref[part]
-            w_scr[:, part * width + third : (part + 1) * width] = high_ref[part]
+            w_scr[part * width : part * width + third, :] = low_ref[part]
+            w_scr[part * width + third : (part + 1) * width, :] = high_ref[part]
 
     @pl.when(step == 0)
     def _():
@@ -113,42 +113,43 @@
 
     rows = tok_ref[...].reshape(seqs * L, D).astype(jnp.float32)
     normed = (rows * rms_scale(rows) * gain_ref[0:1, :]).astype(jnp.bfloat16)
-    qkv = mm(normed, w_scr[...]).astype(jnp.bfloat16)
+    query = mm(w_scr[0:width, :], normed, NT).astype(jnp.bfloat16)
+    key = mm(normed, w_scr[width : 2 * width, :], NT).astype(jnp.bfloat16)
+    value = mm(w_scr[2 * width :, :], normed, NT).astype(jnp.bfloat16)
     low_lane = lax.broadcasted_iota(jnp.int32, (L, PAIR), 1) < HD
-    key_row = lax.broadcasted_iota(jnp.int32, (2 * L, L), 0) % L
+    low_row = lax.broadcasted_iota(jnp.int32, (PAIR, L), 0) < HD
+    key_row = lax.broadcasted_iota(jnp.int32, (2, L, L), 1)
     for s in range(seqs):
-        length = len_ref[meta_ref[0] + step * seqs + s]
-        seen = key_row < length
+        at = slice(s * L, (s + 1) * L)
+        seen = key_row < len_ref[meta_ref[0] + step * seqs + s]
         for p in range(pairs):
-            at = slice(s * L, (s + 1) * L)
-            query = qkv[at, p * PAIR : (p + 1) * PAIR]
-            key = qkv[at, width + p * PAIR : width + (p + 1) * PAIR]
-            value = qkv[at, 2 * width + p * PAIR : 2 * width + (p + 1) * PAIR]
-            zero = jnp.zeros_like(key)
-            key_two = jnp.concatenate(
-                [jnp.where(low_lane, key, zero), jnp.where(low_lane, zero, key)], axis=0
+            head = slice(p * PAIR, (p + 1) * PAIR)
+            k_one, v_one = key[at, head], value[head, at]
+            zero = jnp.zeros_like(k_one)
+            k_two = jnp.concatenate(
+                [jnp.where(low_lane, k_one, zero), jnp.where(low_lane, zero, k_one)], axis=0
             )
-            value_two = jnp.concatenate(
-                [jnp.where(low_lane, value, zero), jnp.where(low_lane, zero, value)], axis=0
+            v_two = jnp.concatenate(
+                [jnp.where(low_row, v_one, zero), jnp.where(low_row, zero, v_one)], axis=1
             )
-            scores = mm(key_two, query, NT) + bias_scr[p * 2 * L : (p + 1) * 2 * L, :]
-            scores = jnp.where(seen, scores, MASKED).reshape(2, L, L)
+            scores = mm(k_two, query[head, at]) + bias_scr[p * 2 * L : (p + 1) * 2 * L, :]
+            scores = jnp.where(seen, scores.reshape(2, L, L), MASKED)
             shifted = jnp.exp(scores - jnp.max(scores, axis=1, keepdims=True))
-            probs = shifted * (1.0 / jnp.sum(shifted, axis=1, keepdims=True))
-            probs = probs.astype(jnp.bfloat16).reshape(2 * L, L)
-            ctx_ref[at, p * PAIR : (p + 1) * PAIR] = mm(probs, value_two, TN).astype(jnp.bfloat16)
+            scale = 1.0 / jnp.sum(shifted, axis=1, keepdims=True)
+            scale = jnp.broadcast_to(scale, (2, HD, L)).reshape(PAIR, L)
+            probs = shifted.astype(jnp.bfloat16).reshape(2 * L, L)
+            ctx_ref[head, at] = (mm(v_two, probs) * scale).astype(jnp.bfloat16)
 
 
 def attention_part(meta, lengths, tokens, gains, own, mate, diag, own_seqs, seqs):
-    width = 2 * own.shape[2]
-    grid = own_seqs // seqs
+    width = 2 * own.shape[1]
     fixed = lambda *dims: pl.BlockSpec(dims, lambda i, m, n: (0,) * len(dims))
     return pl.pallas_call(
         functools.partial(attention_kernel, seqs),
         name="attend",
         grid_spec=pltpu.PrefetchScalarGridSpec(
             num_scalar_prefetch=2,
-            grid=(grid,),
+            grid=(own_seqs // seqs,),
             in_specs=[
                 pl.BlockSpec((seqs, L, D), lambda i, m, n: (m[0] // seqs + i, 0, 0)),
                 fixed(2, D),
@@ -156,13 +157,13 @@
                 fixed(*mate.shape),
                 fixed(*diag.shape),
             ],
-            out_specs=pl.BlockSpec((seqs * L, width), lambda i, m, n: (i, 0)),
+            out_specs=pl.BlockSpec((width, seqs * L), lambda i, m, n: (0, i)),
             scratch_shapes=[
-                pltpu.VMEM((D, 3 * width), jnp.bfloat16),
+                pltpu.VMEM((3 * width, D), jnp.bfloat16),
                 pltpu.VMEM((width // HD * L, L), jnp.float32),
             ],
         ),
-        out_shape=jax.ShapeDtypeStruct((own_seqs * L, width), jnp.bfloat16),
+        out_shape=jax.ShapeDtypeStruct((width, own_seqs * L), jnp.bfloat16),
         compiler_params=pltpu.CompilerParams(
             dimension_semantics=("arbitrary",), vmem_limit_bytes=56 * MIB
         ),
@@ -176,7 +177,7 @@
 
 def ffn_kernel(seqs, chunk, meta_ref, ca_ref, cb_ref, tok_ref, gain_ref, wa_ref, wb_ref, up_ref, down_ref, taps_ref):
     rows = tok_ref[...].reshape(seqs * L, D).astype(jnp.float32)
-    middle = rows + mm(ca_ref[...], wa_ref[...]) + mm(cb_ref[...], wb_ref[...])
+    middle = rows + mm(ca_ref[...], wa_ref[...], TN) + mm(cb_ref[...], wb_ref[...], TN)
     normed = (middle * rms_scale(middle) * gain_ref[1:2, :]).astype(jnp.bfloat16)
     total = jnp.zeros_like(middle)
     for c in range(0, up_ref.shape[1], chunk):
@@ -186,7 +187,7 @@
 
 
 def ffn_part(meta, ctx_a, ctx_b, tokens, gains, w_out, w_up, w_down, own_seqs, seqs, chunk):
-    width = ctx_a.shape[1]
+    width = ctx_a.shape[0]
     grid = own_seqs // seqs
     ff = w_up.shape[1]
     fixed = lambda *dims: pl.BlockSpec(dims, lambda i, m: (0,) * len(dims))
@@ -197,8 +198,8 @@
             num_scalar_prefetch=1,
             grid=(grid,),
             in_specs=[
-                pl.BlockSpec((seqs * L, width), lambda i, m: (i, 0)),
-                pl.BlockSpec((seqs * L, width), lambda i, m: (i, 0)),
+                pl.BlockSpec((width, seqs * L), lambda i, m: (0, i)),
+                pl.BlockSpec((width, seqs * L), lambda i, m: (0, i)),
                 pl.BlockSpec((seqs, L, D), lambda i, m: (m[0] // seqs + i, 0, 0)),
                 fixed(2, D),
                 pl.BlockSpec((width, D), lambda i, m: (m[2], 0)),
@@ -244,8 +245,31 @@
 
 def norm_back(unit, scale, gain, grad):
     scaled = grad * gain
-    back = scale * (scaled - unit * jnp.mean(scaled * unit, axis=-1, keepdims=True))
-    return back, jnp.sum(grad * unit, axis=0, keepdims=True)
+    return scale * (scaled - unit * jnp.mean(scaled * unit, axis=0, keepdims=True))
+
+
+def two_by_head(turned, first):
+    blocks = [by_head_rows(turned[:, s * L : (s + 1) * L].T) for s in (first, first + 1)]
+    return jnp.concatenate(blocks, axis=1)
+
+
+def two_apart(turned, first):
+    zero = jnp.zeros((L, L), turned.dtype)
+    one, two = turned[:, first * L : (first + 1) * L], turned[:, (first + 1) * L : (first + 2) * L]
+    return jnp.concatenate(
+        [jnp.concatenate([one, zero], axis=1), jnp.concatenate([zero, two], axis=1)], axis=0
+    )
+
+
+def column_scale(values):
+    return lax.rsqrt(jnp.mean(values * values, axis=0, keepdims=True) + NORM_EPS)
+
+
+def fold_lanes(values):
+    total = values[:, 0:L]
+    for s in range(1, values.shape[1] // L):
+        total = total + values[:, s * L : (s + 1) * L]
+    return total
 
 
 def side_kernel(
@@ -263,12 +287,18 @@
     ig_ref,
     grow_ref,
     gsmall_ref,
+    gain_scr,
+    wdown_scr,
     wqkv_scr,
+    wqkv_turn_scr,
+    wout_turn_scr,
     wup_scr,
+    wup_turn_scr,
+    wback_turn_scr,
     bias_scr,
     gbias_scr,
-    p_scr,
-    plow_scr,
+    e_scr,
+    elow_scr,
     gdown_scr,
     gqkv_scr,
     gproj_scr,
@@ -278,120 +308,133 @@
 ):
     step = pl.program_id(0)
     at_qkv, at_out, at_up, at_back = D, D + 3 * DS, D + 4 * DS, D + 8 * DS
+    low = lambda v: v.astype(jnp.bfloat16)
 
     @pl.when(step == 0)
     def _():
+        wdown_scr[...] = w_ref[0:D, :].T
         for t in range(3):
-            wqkv_scr[t] = mm(pick_rows(3, t, DS), w_ref[at_qkv:at_out, :]).astype(jnp.bfloat16)
+            part = mm(pick_rows(3, t, DS), w_ref[at_qkv:at_out, :])
+            wqkv_scr[t] = low(part)
+            wqkv_turn_scr[t * L : t * L + DS, :] = low(part.T)
+            wqkv_turn_scr[t * L + DS : (t + 1) * L, :] = jnp.zeros((L - DS, DS), jnp.bfloat16)
+        wout_turn_scr[...] = w_ref[at_out:at_up, :].T
         for t in range(4):
-            wup_scr[:, t * DS : (t + 1) * DS] = mm(
-                pick_rows(4, t, DS), w_ref[at_up:at_back, :]
-            ).astype(jnp.bfloat16)
+            part = mm(pick_rows(4, t, DS), w_ref[at_up:at_back, :])
+            wup_scr[:, t * DS : (t + 1) * DS] = low(part)
+            wup_turn_scr[t * DS : (t + 1) * DS, :] = low(part.T)
+        wback_turn_scr[...] = w_ref[at_back : at_back + SFF, :].T
+        for row in range(3):
+            wide = jnp.broadcast_to(gain_ref[row : row + 1, :], (L, DS)).T
+            gain_scr[row] = jax.nn.sigmoid(wide) if row == 2 else wide
         for head in range(SH):
             bias_scr[head * L : (head + 1) * L, :] = spread_bias(diag_ref[head : head + 1, :])
         for ref in (gbias_scr, gdown_scr, gqkv_scr, gproj_scr, gup_scr, gback_scr, ggain_scr):
             ref[...] = jnp.zeros_like(ref)
 
-    rows = seqs * L
-    gain_one, gain_two = gain_ref[0:1, :], gain_ref[1:2, :]
-    gate = jax.nn.sigmoid(gain_ref[2:3, :])
+    wide = lambda row: jnp.concatenate([gain_scr[row]] * seqs, axis=1)
+    gain_one, gain_two, gate = wide(0), wide(1), wide(2)
     w_out = w_ref[at_out:at_up, :]
     w_back = w_ref[at_back : at_back + SFF, :]
     lengths = [len_ref[meta_ref[0] + step * seqs + s] for s in range(seqs)]
     key_row = lax.broadcasted_iota(jnp.int32, (SH, L, L), 1)
-    own_row = lax.broadcasted_iota(jnp.int32, (L, DS), 0)
+    token = lax.broadcasted_iota(jnp.int32, (DS, L), 1)
     taps = taps_ref[...]
-    x = x_ref[...].reshape(rows, DS)
+    x = jnp.concatenate([x_ref[s] for s in range(seqs)], axis=1)
     grad_out = jnp.concatenate(
-        [jnp.where(own_row < lengths[s], go_ref[s], 0.0) for s in range(seqs)], axis=0
-    )
-
-    tapped = mm(taps, w_ref[0:D, :])
+        [jnp.where(token < lengths[s], go_ref[s], 0.0) for s in range(seqs)], axis=1
+    )
+
+    tapped = mm(wdown_scr[...], taps, NT)
     mixed = gate * x + (1.0 - gate) * tapped
-    scale_one = rms_scale(mixed)
+    scale_one = column_scale(mixed)
     unit_one = mixed * scale_one
-    normed_one = (unit_one * gain_one).astype(jnp.bfloat16)
-    query = mm(normed_one, wqkv_scr[0]).astype(jnp.bfloat16)
-    key = mm(normed_one, wqkv_scr[1]).astype(jnp.bfloat16)
-    value = mm(normed_one, wqkv_scr[2]).astype(jnp.bfloat16)
-
-    context = []
-    for s in range(seqs):
-        at = slice(s * L, (s + 1) * L)
-        scores = mm(by_head_rows(key[at]), query[at], NT) + bias_scr[...]
-        scores = scores.reshape(SH, L, L)
-        scores = jnp.where(key_row < lengths[s], scores, MASKED)
-        shifted = jnp.exp(scores - jnp.max(scores, axis=1, keepdims=True))
-        probs = shifted * (1.0 / jnp.sum(shifted, axis=1, keepdims=True))
-        p_scr[s] = probs
-        probs_low = probs.astype(jnp.bfloat16).reshape(SH * L, L)
-        plow_scr[s] = probs_low
-        turned = mm(by_head_lanes(value[at].T), probs_low)
-        context.append(turned.T.astype(jnp.bfloat16))
-    context = jnp.concatenate(context, axis=0)
-
-    middle = mixed + mm(context, w_out)
-    scale_two = rms_scale(middle)
+    normed_one = low(unit_one * gain_one)
+    qkv = low(mm(wqkv_turn_scr[...], normed_one))
+
+    query, key, value = qkv[0:L], qkv[L : 2 * L], qkv[2 * L :]
+    context, inverse = [], []
+    for s in range(0, seqs, 2):
+        score_two = mm(two_by_head(key, s), two_apart(query, s))
+        for side in range(2):
+            at = slice((s + side) * L, (s + side + 1) * L)
+            scores = score_two[:, side * L : (side + 1) * L] + bias_scr[...]
+            scores = jnp.where(key_row < lengths[s + side], scores.reshape(SH, L, L), MASKED)
+            shifted = jnp.exp(scores - jnp.max(scores, axis=1, keepdims=True))
+            e_scr[s + side] = shifted
+            e_low = low(shifted).reshape(SH * L, L)
+            elow_scr[s + side] = e_low
+            total = 1.0 / jnp.sum(shifted, axis=1, keepdims=True)
+            inverse.append(jnp.broadcast_to(total, (SH, SHD, L)).reshape(DS, L))
+            context.append(mm(by_head_lanes(value[0:DS, at]), e_low) * inverse[-1])
+    context = jnp.concatenate(context, axis=1)
+    inverse = jnp.concatenate(inverse, axis=1)
+    context_low = low(context)
+
+    middle = mixed + mm(wout_turn_scr[...], context_low)
+    scale_two = column_scale(middle)
     unit_two = middle * scale_two
-    normed_two = (unit_two * gain_two).astype(jnp.bfloat16)
-    pre = mm(normed_two, wup_scr[...])
+    normed_two = low(unit_two * gain_two)
+    pre = mm(wup_turn_scr[...], normed_two)
     square = pre * pre
     bend = jnp.tanh(GELU_RATE * pre * (1.0 + GELU_CUBE * square))
     half = 0.5 * (1.0 + bend)
-    hidden = (pre * half).astype(jnp.bfloat16)
+    hidden = low(pre * half)
     slope = half + (0.5 * GELU_RATE) * pre * (1.0 - bend * bend) * (1.0 + 3.0 * GELU_CUBE * square)
-    out_ref[...] = (middle + mm(hidden, w_back)).reshape(seqs, L, DS)
-
-    grad_low = grad_out.astype(jnp.bfloat16)
-    gback_scr[...] += mm(grad_low, hidden, TN)
-    grad_pre = (mm(grad_low, w_back, NT) * slope).astype(jnp.bfloat16)
-    gup_scr[...] += mm(normed_two, grad_pre, TN)
-    back_two, gain_two_grad = norm_back(
-        unit_two, scale_two, gain_two, mm(grad_pre, wup_scr[...], NT)
-    )
-    ggain_scr[1:2, :] += gain_two_grad
-    grad_middle = grad_out + back_two
-    grad_attended = grad_middle.astype(jnp.bfloat16)
-    gproj_scr[...] += mm(context, grad_attended, TN)
-    grad_context = mm(grad_attended, w_out, NT).astype(jnp.bfloat16)
-
+    side_out = middle + mm(wback_turn_scr[...], hidden)
+
+    grad_low = low(grad_out)
+    gback_scr[...] += mm(hidden, grad_low, NT)
+    grad_pre = low(mm(w_back, grad_low) * slope)
+    gup_scr[...] += mm(normed_two, grad_pre, NT)
+    grad_normed_two = mm(wup_scr[...], grad_pre)
+    ggain_scr[1] += fold_lanes(grad_normed_two * unit_two)
+    grad_middle = grad_out + norm_back(unit_two, scale_two, gain_two, grad_normed_two)
+    grad_attended = low(grad_middle)
+    gproj_scr[...] += mm(context_low, grad_attended, NT)
+    grad_context = low(mm(w_out, grad_attended) * inverse)
+    pad = jnp.zeros((L - DS, seqs * L), jnp.bfloat16)
+    dots = (grad_context.astype(jnp.float32) * context).reshape(SH, SHD, seqs * L)
+    dots = jnp.sum(dots, axis=1, keepdims=True)
+
+    grad_context = jnp.concatenate([grad_context, pad], axis=0)
     grad_query, grad_key, grad_value = [], [], []
-    for s in range(seqs):
-        at = slice(s * L, (s + 1) * L)
-        grad_probs = mm(by_head_rows(value[at]), grad_context[at], NT).reshape(SH, L, L)
-        probs = p_scr[s]
-        row_dot = jnp.sum(probs * grad_probs, axis=1, keepdims=True)
-        grad_scores = (probs * (grad_probs - row_dot)).astype(jnp.bfloat16).reshape(SH * L, L)
-        gbias_scr[...] += grad_scores.astype(jnp.float32)
-        turned = mm(by_head_lanes(key[at].T), grad_scores)
-        grad_query.append(turned.T.astype(jnp.bfloat16))
-        grad_key.append(mm(lanes_of(grad_scores), by_head_rows(query[at])).astype(jnp.bfloat16))
-        grad_value.append(
-            mm(lanes_of(plow_scr[s]), by_head_rows(grad_context[at])).astype(jnp.bfloat16)
-        )
-    grad_query = jnp.concatenate(grad_query, axis=0)
+    for s in range(0, seqs, 2):
+        prob_two = mm(two_by_head(value, s), two_apart(grad_context, s))
+        for side in range(2):
+            at = slice((s + side) * L, (s + side + 1) * L)
+            grad_probs = prob_two[:, side * L : (side + 1) * L].reshape(SH, L, L)
+            grad_scores = e_scr[s + side] * (grad_probs - dots[:, :, at])
+            gbias_scr[...] += grad_scores.reshape(SH * L, L)
+            grad_scores = low(grad_scores).reshape(SH * L, L)
+            grad_query.append(low(mm(by_head_lanes(key[0:DS, at]), grad_scores)))
+            grad_key.append(low(mm(lanes_of(grad_scores), by_head_rows(query[0:DS, at].T))))
+            grad_value.append(
+                low(mm(lanes_of(elow_scr[s + side]), by_head_rows(grad_context[0:DS, at].T)))
+            )
+    grad_query = jnp.concatenate(grad_query, axis=1)
     grad_key = jnp.concatenate(grad_key, axis=0)
     grad_value = jnp.concatenate(grad_value, axis=0)
 
-    grad_normed = mm(grad_query, wqkv_scr[0], NT)
-    grad_normed += mm(grad_key, wqkv_scr[1], NT)
-    grad_normed += mm(grad_value, wqkv_scr[2], NT)
-    gqkv_scr[0] += mm(normed_one, grad_query, TN)
-    gqkv_scr[1] += mm(normed_one, grad_key, TN)
-    gqkv_scr[2] += mm(normed_one, grad_value, TN)
-    back_one, gain_one_grad = norm_back(unit_one, scale_one, gain_one, grad_normed)
-    ggain_scr[0:1, :] += gain_one_grad
-    grad_mixed = grad_middle + back_one
-    ig_ref[...] = (gate * grad_mixed).reshape(seqs, L, DS)
-    grad_tap = ((1.0 - gate) * grad_mixed).astype(jnp.bfloat16)
-    gdown_scr[...] += mm(grad_tap, taps, TN)
-    ggain_scr[2:3, :] += jnp.sum(grad_mixed * (x - tapped), axis=0, keepdims=True)
+    grad_normed = mm(wqkv_scr[0], grad_query)
+    grad_normed += mm(wqkv_scr[1], grad_key, NT)
+    grad_normed += mm(wqkv_scr[2], grad_value, NT)
+    gqkv_scr[0] += mm(normed_one, grad_query, NT)
+    gqkv_scr[1] += mm(normed_one, grad_key)
+    gqkv_scr[2] += mm(normed_one, grad_value)
+    ggain_scr[0] += fold_lanes(grad_normed * unit_one)
+    grad_mixed = grad_middle + norm_back(unit_one, scale_one, gain_one, grad_normed)
+    input_grad = gate * grad_mixed
+    grad_tap = low((1.0 - gate) * grad_mixed)
+    gdown_scr[...] += mm(grad_tap, taps)
+    ggain_scr[2] += fold_lanes(grad_mixed * (x - tapped))
+    for s in range(seqs):
+        out_ref[s] = side_out[:, s * L : (s + 1) * L]
+        ig_ref[s] = input_grad[:, s * L : (s + 1) * L]
 
     @pl.when(step == pl.num_programs(0) - 1)
     def _():
-        low = lambda v: v.astype(jnp.bfloat16)
-        pad = jnp.zeros((grow_ref.shape[0], grow_ref.shape[1] - DS), jnp.bfloat16)
-        grow_ref[:, DS:] = pad
+        grow_ref[:, DS:] = jnp.zeros((grow_ref.shape[0], grow_ref.shape[1] - DS), jnp.bfloat16)
         grow_ref[0:D, 0:DS] = low(gdown_scr[...].T)
         spread = mm(pick_rows(3, 0, DS), low(gqkv_scr[0]), TN)
         for t in range(1, 3):
@@ -402,7 +445,7 @@
         for t in range(1, 4):
             spread = spread + mm(pick_rows(4, t, DS), low(gup_scr[:, t * DS : (t + 1) * DS]), TN)
         grow_ref[at_up:at_back, 0:DS] = low(spread)
-        grow_ref[at_back : at_back + SFF, 0:DS] = low(gback_scr[...].T)
+        grow_ref[at_back : at_back + SFF, 0:DS] = low(gback_scr[...])
         flip_row = lax.broadcasted_iota(jnp.int32, (L, L), 0)
         flip_column = lax.broadcasted_iota(jnp.int32, (L, L), 1)
         flip = (flip_row + flip_column == L - 1).astype(jnp.float32)
@@ -420,9 +463,11 @@
             diagonals.append(jnp.sum(rolled, axis=0, keepdims=True))
         diagonals = jnp.concatenate(diagonals, axis=0)
         gsmall_ref[...] = jnp.zeros_like(gsmall_ref)
-        gsmall_ref[0:3, 0:DS] = ggain_scr[0:3, :] * jnp.concatenate(
-            [jnp.ones((2, DS), jnp.float32), gate * (1.0 - gate)], axis=0
-        )
+        for row in range(3):
+            total = ggain_scr[row]
+            if row == 2:
+                total = total * (gain_scr[2] * (1.0 - gain_scr[2]))
+            gsmall_ref[row : row + 1, 0:DS] = jnp.sum(total.T, axis=0, keepdims=True)
         gsmall_ref[4 : 4 + SH, 0 : onehot_ref.shape[0]] = lax.dot_general(
             diagonals, onehot_ref[...], NT, precision=PRECISE, preferred_element_type=jnp.float32
         )
@@ -432,7 +477,7 @@
     own_seqs = side_input.shape[0]
     grid = own_seqs // seqs
     fixed = lambda *dims: pl.BlockSpec(dims, lambda i, m, n: (0,) * len(dims))
-    block = pl.BlockSpec((seqs, L, DS), lambda i, m, n: (i, 0, 0))
+    block = pl.BlockSpec((seqs, DS, L), lambda i, m, n: (i, 0, 0))
     f32, bf16 = jnp.float32, jnp.bfloat16
     return pl.pallas_call(
         functools.partial(side_kernel, seqs),
@@ -451,7 +496,13 @@
             ],
             out_specs=[block, block, fixed(w_rows.shape[0], L), fixed(16, L)],
             scratch_shapes=[
+                pltpu.VMEM((3, DS, L), f32),
+                pltpu.VMEM((DS, D), bf16),
                 pltpu.VMEM((3, DS, DS), bf16),
+                pltpu.VMEM((3 * L, DS), bf16),
+                pltpu.VMEM((DS, DS), bf16),
+                pltpu.VMEM((DS, SFF), bf16),
+                pltpu.VMEM((SFF, DS), bf16),
                 pltpu.VMEM((DS, SFF), bf16),
                 pltpu.VMEM((SH * L, L), f32),
                 pltpu.VMEM((SH * L, L), f32),
@@ -461,8 +512,8 @@
                 pltpu.VMEM((3, DS, DS), f32),
                 pltpu.VMEM((DS, DS), f32),
                 pltpu.VMEM((DS, SFF), f32),
-                pltpu.VMEM((DS, SFF), f32),
-                pltpu.VMEM((8, DS), f32),
+                pltpu.VMEM((SFF, DS), f32),
+                pltpu.VMEM((3, DS, L), f32),
             ],
         ),
         out_shape=[
@@ -532,37 +583,42 @@
     near = jnp.stack([model_index * own_seqs, model_index % 2, group]).astype(jnp.int32)
     far = jnp.stack([model_index * own_seqs, model_index % 2, 1 - group]).astype(jnp.int32)
 
-    qkv_mate = swap(base_qkv, 1)
-    qkv_far = swap(base_qkv, 2)
-    qkv_far_mate = swap(qkv_far, 1)
-    low_rows = side_weights.astype(jnp.bfloat16).reshape(1, shard_rows, DS)
-    w_rows = exchange(jnp.broadcast_to(low_rows, (devices, shard_rows, DS)))
-    w_rows = w_rows.reshape(devices * shard_rows, DS)
+    turn = lambda values: jnp.transpose(values, (0, 2, 1))
+    qkv_own = turn(base_qkv)
+    qkv_far = swap(qkv_own, 2)
+    qkv_mate = swap(qkv_own, 1)
 
     onehot = jnp.asarray(diagonal_onehot(buckets))
     base_diag = jnp.dot(base_table.T, onehot, precision=PRECISE)
     side_diag = jnp.dot(side_table.T, onehot, precision=PRECISE)
 
     ctx_near = attention_part(
-        near, lengths, tokens, base_gains, base_qkv, qkv_mate, base_diag, own_seqs, 2
-    )
+        near, lengths, tokens, base_gains, qkv_own, qkv_mate, base_diag, own_seqs, 8
+    )
+    ctx_near, qkv_far, low_rows = lax.optimization_barrier(
+        (ctx_near, qkv_far, side_weights.astype(jnp.bfloat16).reshape(1, shard_rows, DS))
+    )
+    qkv_far_mate = swap(qkv_far, 1)
+    w_rows = exchange(jnp.broadcast_to(low_rows, (devices, shard_rows, DS)))
     ctx_far = attention_part(
-        far, lengths, tokens, base_gains, qkv_far, qkv_far_mate, base_diag, own_seqs, 2
+        far, lengths, tokens, base_gains, qkv_far, qkv_far_mate, base_diag, own_seqs, 8
     )
     taps = ffn_part(
-        near, ctx_near, ctx_far, tokens, base_gains, base_out, base_up, base_down, own_seqs, 4, 1024
-    )
+        near, ctx_near, ctx_far, tokens, base_gains, base_out, base_up, base_down, own_seqs, 8, 1024
+    )
+    taps, w_rows = lax.optimization_barrier((taps, w_rows))
+    w_rows = w_rows.reshape(devices * shard_rows, DS)
     side_output, input_grad, grad_rows, grad_small = side_part(
         near,
         lengths,
         taps,
-        side_input,
-        output_grad,
+        turn(side_input),
+        turn(output_grad),
         side_gains,
         w_rows,
         side_diag,
         jnp.asarray(gradient_onehot(buckets)),
-        2,
+        8,
     )
 
     small_high = grad_small.astype(jnp.bfloat16)
@@ -576,7 +632,7 @@
         axis=1,
     )
     summed = jnp.sum(exchange(outgoing).astype(jnp.float32), axis=0)
-    grad_shard = summed[:shard_rows, :DS]
+    grad_shard = lax.optimization_barrier(summed[:shard_rows, :DS].reshape(-1))
     small_total = summed[shard_rows : shard_rows + 16] + summed[shard_rows + 16 :]
     gains_total = small_total[0:3, :DS]
     table_total = small_total[4 : 4 + SH, :buckets].T
@@ -592,7 +648,7 @@
         side_weights,
         weights_first,
         weights_second,
-        factor * grad_shard.reshape(-1),
+        factor * grad_shard,
         RATE_MATRIX,
         WEIGHT_DECAY,
     )
@@ -603,8 +659,8 @@
         side_table, table_first, table_second, factor * table_total, RATE_SMALL, 0.0
     )
     return (
-        side_output,
-        input_grad,
+        turn(side_output),
+        turn(input_grad),
         grad_norm,
         weights_moment,
         weights_square,

time: 228 us -> 179 us (0.79)
  Pallas kernels: 142 us -> 112 us
  waiting for transfers between devices: 35 us -> 7.21 us
  blocking collectives: 0 us -> 26.3 us
  local copies, waits for them, and re-layouts: 19.9 us -> 6.35 us
  starting transfers between devices: 17.3 us -> 12.9 us
    all_to_all x0 -> x1, blocking collectives: none -> 26.3 us  [exchange(): lax.all_to_all(values, ('batch', 'mp'), split_axis=0, concat_axis=0, tile...]
    pallas_call x1, Pallas kernels: 57.1 us -> 36.8 us  [side_part(): pl.pallas_call(functools.partial(side_kernel, seqs), name='side', grid_sp...]
    all_to_all x3 -> x2, waiting for transfers between devices: 23 us -> 5.87 us  [exchange(): lax.all_to_all(values, ('batch', 'mp'), split_axis=0, concat_axis=0, tile...]
    ppermute x3, waiting for transfers between devices: 12 us -> 1.34 us  [swap(): return lax.ppermute(values, 'mp', [(i, i ^ distance) for i in range(size)])]
    pallas_call x2, Pallas kernels: 39.5 us -> 30.6 us  [attention_part(): pl.pallas_call(functools.partial(attention_kernel, seqs), name='attend',...]
    unnamed x35 -> x28, local copies, waits for them, and re-layouts: 9.24 us -> 1.88 us
    ppermute x3 -> x0, local copies, waits for them, and re-layouts: 6.13 us -> none  [swap(): return lax.ppermute(values, 'mp', [(i, i ^ distance) for i in range(size)])]
    all_to_all x3 -> x2, starting transfers between devices: 14.2 us -> 9.77 us  [exchange(): lax.all_to_all(values, ('batch', 'mp'), split_axis=0, concat_axis=0, tile...]
  transfers between devices with their start and end apart: 6 -> 5, of which waited for: 4 -> 2; matrix products, arithmetic and copies ran while one was open for 9% -> 4% of each run, Pallas kernels for 9% -> 42%
where the time goes in v2:
time: 179 us; the launch traced here: 178 us
  Pallas kernels  112 us (63%)
  blocking collectives  26.3 us (15%)
  starting transfers between devices  12.9 us (7%)
  other arithmetic  7.34 us (4%)
  waiting for transfers between devices  7.21 us (4%)
  local copies, waits for them, and re-layouts  6.35 us (4%)
  between operations  4 us (2%)
  matrix products  2.25 us (1%)
    pallas_call x1, Pallas kernels, ffn_part(): pl.pallas_call(functools.partial(ffn_kernel, seqs, chunk), name='feed', g...  44.6 us
    pallas_call x1, Pallas kernels, side_part(): pl.pallas_call(functools.partial(side_kernel, seqs), name='side', grid_sp...  36.8 us
    pallas_call x2, Pallas kernels, attention_part(): pl.pallas_call(functools.partial(attention_kernel, seqs), name='attend',...  30.6 us
    all_to_all x1, blocking collectives, exchange(): lax.all_to_all(values, ('batch', 'mp'), split_axis=0, concat_axis=0, tile...  26.3 us
    all_to_all x2, starting transfers between devices, exchange(): lax.all_to_all(values, ('batch', 'mp'), split_axis=0, concat_axis=0, tile...  9.77 us
    all_to_all x2, waiting for transfers between devices, exchange(): lax.all_to_all(values, ('batch', 'mp'), split_axis=0, concat_axis=0, tile...  5.87 us
  transfers between devices with their start and end apart: 5, of which 2 were waited for; matrix products, arithmetic and copies ran while one was open for 4% of the time, Pallas kernels for 42%

profile of v2, /device:TPU:0, one launch (start us, length us, event | category | flops | bytes accessed | tf_op | source)
XLA Modules:
  0.0 178.2 jit_solution(14555013402720470828)
XLA Ops:
  0.6 0.0 copy-start
  0.7 0.5 collective-permute-start
  1.2 2.6 %collective-permute-start.1 = (bf16[3,192,768]{2,1,0:T(8,128)(2,1)}, bf16[3,192,768]{2,1,0:T(8,128)(2,1)S(1)}, u32[]{:S(2)}, u32[]{:S(2)}) collective-permute-start(bf16[3,192,768]{2,1,0:T(8,128)(2,1)} %bitcast.27), channel_id=1, source_target_pairs={{0,2},{1,3},{2,0},{3,1},{4,6},{5,7},{6,4},{7,5},{8,10},{9,11},{10,... | collective-permute-start | bytes 2654216 | tf_op jit(solution)/shard_map/ppermute | solution.py:549
  3.7 0.7 convert_element_type.18
  4.5 0.1 reshape.41
  4.6 0.6 pad_add_fusion.meta_ref
  5.2 1.5 convolution_bitcast_fusion.1.diag_ref
  6.7 0.0 collective-permute-done.mate_ref
  6.7 0.9 copy-done.2
  7.6 15.3 %attend.2.ca_ref = bf16[384,3072]{1,0:T(8,128)(2,1)} custom-call(s32[3]{0:T(128)} %pad_add_fusion.meta_ref, s32[96]{0:T(128)} %len_ref.5, bf16[96,128,768]{2,1,0:T(8,128)(2,1)} %tok_ref.5, f32[2,768]{1,0:T(2,128)} %gain_ref.6, bf16[3,192,768]{2,1,0:T(8,128)(2,1)} %bitcast.28, bf16[3,192,768]{2,1,0:T(8,128)(2,1)} %copy-done.2, ...), custom_call_target="tpu_custom_call" | custom-call | flops 6039797760 | bytes 8847360 | tf_op jit(solution)/shard_map/attend/pallas_call | solution.py:147
  22.9 1.3 collective-permute-done.1.own_ref
  24.2 0.0 collective-permute-start.2
  24.2 0.7 pad_add_fusion.2.meta_ref
  24.9 0.7 convolution_bitcast_fusion.diag_ref
  25.6 0.9 broadcast_in_dim.17
  26.6 6.2 %all-to-all-start = ((bf16[32,60,96]{2,1,0:T(8,128)(2,1)}), bf16[32,60,96]{2,1,0:T(8,128)(2,1)S(1)}, u32[]{:S(2)}, u32[]{:S(2)}) async-start(bf16[32,60,96]{2,1,0:T(8,128)(2,1)} %broadcast_in_dim.17), calls=%async_computation | async-start | bytes 1048576 | tf_op jit(solution)/shard_map/all_to_all | solution.py:553
  32.7 0.0 collective-permute-done.2.mate_ref
  32.7 0.0 copy-start.3
  32.7 0.9 copy-done.3
  33.6 15.3 %attend.3.cb_ref = bf16[384,3072]{1,0:T(8,128)(2,1)} custom-call(s32[3]{0:T(128)} %pad_add_fusion.2.meta_ref, s32[96]{0:T(128)} %len_ref.5, bf16[96,128,768]{2,1,0:T(8,128)(2,1)} %tok_ref.5, f32[2,768]{1,0:T(2,128)} %gain_ref.6, bf16[3,192,768]{2,1,0:T(8,128)(2,1)} %copy-done.1, bf16[3,192,768]{2,1,0:T(8,128)(2,1)} %copy-done.3, ...), custom_call_target="tpu_custom_call" | custom-call | flops 6039797760 | bytes 8847360 | tf_op jit(solution)/shard_map/attend/pallas_call | solution.py:147
  49.0 44.6 %feed.1.taps_ref = bf16[3072,768]{1,0:T(8,128)(2,1)} custom-call(s32[3]{0:T(128)} %pad_add_fusion.meta_ref, bf16[384,3072]{1,0:T(8,128)(2,1)} %attend.2.ca_ref, bf16[384,3072]{1,0:T(8,128)(2,1)} %attend.3.cb_ref, bf16[96,128,768]{2,1,0:T(8,128)(2,1)} %tok_ref.5, f32[2,768]{1,0:T(2,128)} %gain_ref.6, bf16[768,768]{1,0:T(8,128)(2,1)} %wb_ref.1, ...), custom_call_target="tpu_custom_call" | custom-call | flops 32614907904 | bytes 24772608 | tf_op jit(solution)/shard_map/feed/pallas_call | solution.py:194
  93.5 0.0 all-to-all-done
  93.5 1.0 reshape.42.w_ref
  94.5 36.8 %side.1 = (f32[24,96,128]{2,1,0:T(8,128)}, f32[24,96,128]{2,1,0:T(8,128)}, bf16[1920,128]{1,0:T(8,128)(2,1)}, f32[16,128]{1,0:T(8,128)}) custom-call(s32[3]{0:T(128)} %pad_add_fusion.meta_ref, s32[96]{0:T(128)} %len_ref.5, bf16[3072,768]{1,0:T(8,128)(2,1)} %feed.1.taps_ref, f32[24,96,128]{2,1,0:T(8,128)} %bitcast.31, f32[24,96,128]{2,1,0:T(8,128)} %bitcast.32, ...), custom_call_target="tpu_custom_call" | custom-call | flops 7200000000 | bytes 9437184 | tf_op jit(solution)/shard_map/side/pallas_call | solution.py:482
  131.3 1.1 reshape.43
  132.4 0.8 subtract_convert_fusion
  133.2 0.1 pad_maximum_fusion
  133.4 0.0 copy-start.9
  133.4 0.0 copy-start.10
  133.4 0.0 copy-start.11
  133.4 0.0 copy-start.12
  133.4 0.0 copy-start.13
  133.4 0.0 copy-start.5
  133.4 0.0 copy-start.7
  133.4 0.0 copy-start.8
  133.5 26.3 %all_to_all.19 = bf16[32,92,128]{2,1,0:T(8,128)(2,1)S(1)} all-to-all(bf16[32,92,128]{2,1,0:T(8,128)(2,1)S(1)} %pad_maximum_fusion), channel_id=1, replica_groups=mesh['batch'=8,'mp'=4] {'batch','mp'}, dimensions={0} | all-to-all | bytes 1507328 | tf_op jit(solution)/shard_map/all_to_all | solution.py:553
  159.7 0.1 convert_reduce_fusion
  159.9 0.1 reshape.44
  159.9 0.6 multiply_reduce_fusion
  160.5 1.3 broadcast_in_dim.19
  161.8 3.6 %all-to-all-start.2 = ((f32[32,1,128]{2,1,0:T(1,128)}), f32[32,1,128]{2,1,0:T(1,128)S(1)}, u32[]{:S(2)}, u32[]{:S(2)}) async-start(f32[32,1,128]{2,1,0:T(1,128)} %broadcast_in_dim.19), calls=%async_computation.2 | async-start | bytes 32768 | tf_op jit(solution)/shard_map/all_to_all | solution.py:553
  165.4 0.6 multiply_reduce_fusion.1
  166.0 0.6 multiply_reduce_fusion.2
  166.6 5.9 %all-to-all-done.2 = f32[32,1,128]{2,1,0:T(1,128)S(1)} async-done(((f32[32,1,128]{2,1,0:T(1,128)}), f32[32,1,128]{2,1,0:T(1,128)S(1)}, u32[]{:S(2)}, u32[]{:S(2)}) %all-to-all-start.2) | async-done | bytes 16416 | tf_op jit(solution)/shard_map/all_to_all | solution.py:553
  172.5 0.6 slice_reduce_fusion
  175.2 0.6 multiply_subtract_fusion.1
  175.8 0.6 multiply_subtract_fusion.2
  176.4 0.6 fusion.7
  (20 shorter events, 0.1 us)
Async XLA Ops:
  0.6 4.5 %copy-start = (f32[32,12]{0,1:T(8,128)S(1)}, f32[32,12]{0,1:T(8,128)}, u32[]{:S(2)}) copy-start(f32[32,12]{0,1:T(8,128)} %param.28) | copy-start | bytes 4612
  0.7 6.0 %collective-permute-start = (bf16[3,192,768]{2,1,0:T(8,128)(2,1)}, bf16[3,192,768]{2,1,0:T(8,128)(2,1)S(1)}, u32[]{:S(2)}, u32[]{:S(2)}) collective-permute-start(bf16[3,192,768]{2,1,0:T(8,128)(2,1)} %bitcast.26), channel_id=1, source_target_pairs={{0,1},{1,0},{2,3},{3,2},{4,5},{5,4},{6,7},{7,6},{8,9},{9,8},{10,11... | collective-permute-start | bytes 2654216 | tf_op jit(solution)/shard_map/ppermute | solution.py:549
  1.2 23.0 %collective-permute-start.1 = (bf16[3,192,768]{2,1,0:T(8,128)(2,1)}, bf16[3,192,768]{2,1,0:T(8,128)(2,1)S(1)}, u32[]{:S(2)}, u32[]{:S(2)}) collective-permute-start(bf16[3,192,768]{2,1,0:T(8,128)(2,1)} %bitcast.27), channel_id=1, source_target_pairs={{0,2},{1,3},{2,0},{3,1},{4,6},{5,7},{6,4},{7,5},{8,10},{9,11},{10,... | collective-permute-start | bytes 2654216 | tf_op jit(solution)/shard_map/ppermute | solution.py:549
  6.7 18.2 %copy-start.4 = (f32[32,256]{1,0:T(8,128)S(1)}, f32[32,256]{1,0:T(8,128)}, u32[]{:S(2)}) copy-start(f32[32,256]{1,0:T(8,128)} %constant.82.clone) | copy-start | bytes 98308
  6.7 18.2 %copy-start.6 = (f32[32,12]{0,1:T(8,128)S(1)}, f32[32,12]{0,1:T(8,128)}, u32[]{:S(2)}) copy-start(f32[32,12]{0,1:T(8,128)} %param.37) | copy-start | bytes 4612
  6.7 0.9 copy-start.2
  24.2 8.5 %copy-start.1 = (bf16[3,192,768]{2,1,0:T(8,128)(2,1)}, bf16[3,192,768]{2,1,0:T(8,128)(2,1)S(1)}, u32[]{:S(2)}) copy-start(bf16[3,192,768]{2,1,0:T(8,128)(2,1)S(1)} %collective-permute-done.1.own_ref) | copy-start | bytes 2654212
  24.2 8.5 %collective-permute-start.2 = (bf16[3,192,768]{2,1,0:T(8,128)(2,1)S(1)}, bf16[3,192,768]{2,1,0:T(8,128)(2,1)S(1)}, u32[]{:S(2)}, u32[]{:S(2)}) collective-permute-start(bf16[3,192,768]{2,1,0:T(8,128)(2,1)S(1)} %collective-permute-done.1.own_ref), channel_id=1, source_target_pairs={{0,1},{1,0},{2,3},{3,2},{4,5},{5,4},{6,7},{7,6},{8,9},{9,8},{10,11... | collective-permute-start | bytes 2654216 | tf_op jit(solution)/shard_map/ppermute | solution.py:549
  26.6 67.0 %all-to-all-start = ((bf16[32,60,96]{2,1,0:T(8,128)(2,1)}), bf16[32,60,96]{2,1,0:T(8,128)(2,1)S(1)}, u32[]{:S(2)}, u32[]{:S(2)}) async-start(bf16[32,60,96]{2,1,0:T(8,128)(2,1)} %broadcast_in_dim.17), calls=%async_computation | async-start | bytes 1048576 | tf_op jit(solution)/shard_map/all_to_all | solution.py:553
  32.7 0.9 copy-start.3
  133.4 41.8 %copy-start.9 = (f32[32,12]{0,1:T(8,128)S(1)}, f32[32,12]{0,1:T(8,128)}, u32[]{:S(2)}) copy-start(f32[32,12]{0,1:T(8,128)} %param.39) | copy-start | bytes 4612
  133.4 41.8 %copy-start.10 = (f32[32,12]{0,1:T(8,128)S(1)}, f32[32,12]{0,1:T(8,128)}, u32[]{:S(2)}) copy-start(f32[32,12]{0,1:T(8,128)} %param.38) | copy-start | bytes 4612
  133.4 42.4 %copy-start.11 = (f32[3,96]{1,0:T(4,128)S(1)}, f32[3,96]{1,0:T(4,128)}, u32[]{:S(2)}) copy-start(f32[3,96]{1,0:T(4,128)} %gain_ref.7) | copy-start | bytes 3460
  133.4 42.4 %copy-start.12 = (f32[3,96]{1,0:T(4,128)S(1)}, f32[3,96]{1,0:T(4,128)}, u32[]{:S(2)}) copy-start(f32[3,96]{1,0:T(4,128)} %param.36) | copy-start | bytes 3460
  133.4 42.4 %copy-start.13 = (f32[3,96]{1,0:T(4,128)S(1)}, f32[3,96]{1,0:T(4,128)}, u32[]{:S(2)}) copy-start(f32[3,96]{1,0:T(4,128)} %param.35) | copy-start | bytes 3460
  133.4 43.0 %copy-start.5 = (f32[5760]{0:T(1024)S(1)}, f32[5760]{0:T(1024)}, u32[]{:S(2)}) copy-start(f32[5760]{0:T(1024)} %param.31) | copy-start | bytes 69124
  133.4 43.0 %copy-start.7 = (f32[5760]{0:T(1024)S(1)}, f32[5760]{0:T(1024)}, u32[]{:S(2)}) copy-start(f32[5760]{0:T(1024)} %param.33) | copy-start | bytes 69124
  133.4 43.0 %copy-start.8 = (f32[5760]{0:T(1024)S(1)}, f32[5760]{0:T(1024)}, u32[]{:S(2)}) copy-start(f32[5760]{0:T(1024)} %param.32) | copy-start | bytes 69124
  161.8 10.7 %all-to-all-start.2 = ((f32[32,1,128]{2,1,0:T(1,128)}), f32[32,1,128]{2,1,0:T(1,128)S(1)}, u32[]{:S(2)}, u32[]{:S(2)}) async-start(f32[32,1,128]{2,1,0:T(1,128)} %broadcast_in_dim.19), calls=%async_computation.2 | async-start | bytes 32768 | tf_op jit(solution)/shard_map/all_to_all | solution.py:553

commit v3 on v2

--- a/solution.py
+++ b/solution.py
@@ -31,6 +31,7 @@
 MASKED = -1e30
 PRECISE = lax.Precision.HIGHEST
 MIB = 1 << 20
+VMEM_MAIN = 60
 GELU_RATE = math.sqrt(2.0 / math.pi)
 GELU_CUBE = 0.044715
 
@@ -85,44 +86,43 @@
     return pltpu.roll(full, 0, 1, stride=1, stride_axis=0)[:, :L]
 
 
-def attention_kernel(seqs, meta_ref, len_ref, tok_ref, gain_ref, own_ref, mate_ref, diag_ref, ctx_ref, w_scr, bias_scr):
-    step = pl.program_id(0)
+def attention_setup(parity, group, own_ref, mate_ref, diag_ref, w_scr, bias_scr):
     third = own_ref.shape[1]
     width = 2 * third
-    pairs = width // PAIR
+    heads = width // HD
 
     def place(low_ref, high_ref):
         for part in range(3):
             w_scr[part * width : part * width + third, :] = low_ref[part]
             w_scr[part * width + third : (part + 1) * width, :] = high_ref[part]
 
-    @pl.when(step == 0)
+    @pl.when(parity == 0)
     def _():
-        @pl.when(meta_ref[1] == 0)
-        def _():
-            place(own_ref, mate_ref)
-
-        @pl.when(meta_ref[1] == 1)
-        def _():
-            place(mate_ref, own_ref)
-
-        for head in range(2 * pairs):
-            bias_scr[head * L : (head + 1) * L, :] = spread_bias(
-                diag_ref[pl.ds(meta_ref[2] * 2 * pairs + head, 1), :]
-            )
-
-    rows = tok_ref[...].reshape(seqs * L, D).astype(jnp.float32)
-    normed = (rows * rms_scale(rows) * gain_ref[0:1, :]).astype(jnp.bfloat16)
+        place(own_ref, mate_ref)
+
+    @pl.when(parity == 1)
+    def _():
+        place(mate_ref, own_ref)
+
+    for head in range(heads):
+        bias_scr[head * L : (head + 1) * L, :] = spread_bias(
+            diag_ref[pl.ds(group * heads + head, 1), :]
+        )
+
+
+def attention_block(lengths, rows, gain, w_scr, bias_scr, ctx_ref):
+    width = w_scr.shape[0] // 3
+    normed = (rows * rms_scale(rows) * gain).astype(jnp.bfloat16)
     query = mm(w_scr[0:width, :], normed, NT).astype(jnp.bfloat16)
     key = mm(normed, w_scr[width : 2 * width, :], NT).astype(jnp.bfloat16)
     value = mm(w_scr[2 * width :, :], normed, NT).astype(jnp.bfloat16)
     low_lane = lax.broadcasted_iota(jnp.int32, (L, PAIR), 1) < HD
     low_row = lax.broadcasted_iota(jnp.int32, (PAIR, L), 0) < HD
     key_row = lax.broadcasted_iota(jnp.int32, (2, L, L), 1)
-    for s in range(seqs):
+    for s, length in enumerate(lengths):
         at = slice(s * L, (s + 1) * L)
-        seen = key_row < len_ref[meta_ref[0] + step * seqs + s]
-        for p in range(pairs):
+        seen = key_row < length
+        for p in range(width // PAIR):
             head = slice(p * PAIR, (p + 1) * PAIR)
             k_one, v_one = key[at, head], value[head, at]
             zero = jnp.zeros_like(k_one)
@@ -141,12 +141,24 @@
             ctx_ref[head, at] = (mm(v_two, probs) * scale).astype(jnp.bfloat16)
 
 
-def attention_part(meta, lengths, tokens, gains, own, mate, diag, own_seqs, seqs):
+def near_kernel(seqs, meta_ref, len_ref, tok_ref, gain_ref, own_ref, mate_ref, diag_ref, ctx_ref, w_scr, bias_scr):
+    step = pl.program_id(0)
+
+    @pl.when(step == 0)
+    def _():
+        attention_setup(meta_ref[1], meta_ref[2], own_ref, mate_ref, diag_ref, w_scr, bias_scr)
+
+    lengths = [len_ref[meta_ref[0] + step * seqs + s] for s in range(seqs)]
+    rows = tok_ref[...].reshape(seqs * L, D).astype(jnp.float32)
+    attention_block(lengths, rows, gain_ref[0:1, :], w_scr, bias_scr, ctx_ref)
+
+
+def near_part(meta, lengths, tokens, gains, own, mate, diag, own_seqs, seqs):
     width = 2 * own.shape[1]
     fixed = lambda *dims: pl.BlockSpec(dims, lambda i, m, n: (0,) * len(dims))
     return pl.pallas_call(
-        functools.partial(attention_kernel, seqs),
-        name="attend",
+        functools.partial(near_kernel, seqs),
+        name="near",
         grid_spec=pltpu.PrefetchScalarGridSpec(
             num_scalar_prefetch=2,
             grid=(own_seqs // seqs,),
@@ -175,50 +187,15 @@
     )(meta, lengths, tokens, gains, own, mate, diag)
 
 
-def ffn_kernel(seqs, chunk, meta_ref, ca_ref, cb_ref, tok_ref, gain_ref, wa_ref, wb_ref, up_ref, down_ref, taps_ref):
-    rows = tok_ref[...].reshape(seqs * L, D).astype(jnp.float32)
-    middle = rows + mm(ca_ref[...], wa_ref[...], TN) + mm(cb_ref[...], wb_ref[...], TN)
-    normed = (middle * rms_scale(middle) * gain_ref[1:2, :]).astype(jnp.bfloat16)
+def feed_block(chunk, rows, near, far, gain, wo_scr, up_scr, down_scr, taps_scr):
+    width = near.shape[0]
+    middle = rows + mm(near, wo_scr[0:width, :], TN) + mm(far, wo_scr[width:, :], TN)
+    normed = (middle * rms_scale(middle) * gain).astype(jnp.bfloat16)
     total = jnp.zeros_like(middle)
-    for c in range(0, up_ref.shape[1], chunk):
-        hidden = gelu(mm(normed, up_ref[:, c : c + chunk])).astype(jnp.bfloat16)
-        total = total + mm(hidden, down_ref[c : c + chunk, :])
-    taps_ref[...] = (middle + total).astype(jnp.bfloat16)
-
-
-def ffn_part(meta, ctx_a, ctx_b, tokens, gains, w_out, w_up, w_down, own_seqs, seqs, chunk):
-    width = ctx_a.shape[0]
-    grid = own_seqs // seqs
-    ff = w_up.shape[1]
-    fixed = lambda *dims: pl.BlockSpec(dims, lambda i, m: (0,) * len(dims))
-    return pl.pallas_call(
-        functools.partial(ffn_kernel, seqs, chunk),
-        name="feed",
-        grid_spec=pltpu.PrefetchScalarGridSpec(
-            num_scalar_prefetch=1,
-            grid=(grid,),
-            in_specs=[
-                pl.BlockSpec((width, seqs * L), lambda i, m: (0, i)),
-                pl.BlockSpec((width, seqs * L), lambda i, m: (0, i)),
-                pl.BlockSpec((seqs, L, D), lambda i, m: (m[0] // seqs + i, 0, 0)),
-                fixed(2, D),
-                pl.BlockSpec((width, D), lambda i, m: (m[2], 0)),
-                pl.BlockSpec((width, D), lambda i, m: (1 - m[2], 0)),
-                fixed(*w_up.shape),
-                fixed(*w_down.shape),
-            ],
-            out_specs=pl.BlockSpec((seqs * L, D), lambda i, m: (i, 0)),
-        ),
-        out_shape=jax.ShapeDtypeStruct((own_seqs * L, D), jnp.bfloat16),
-        compiler_params=pltpu.CompilerParams(
-            dimension_semantics=("arbitrary",), vmem_limit_bytes=60 * MIB
-        ),
-        cost_estimate=pl.CostEstimate(
-            flops=2 * own_seqs * L * D * (D + 2 * ff),
-            bytes_accessed=own_seqs * L * 3 * D * 2 + 2 * D * (D + 2 * ff),
-            transcendentals=own_seqs * L * ff,
-        ),
-    )(meta, ctx_a, ctx_b, tokens, gains, w_out, w_out, w_up, w_down)
+    for c in range(0, up_scr.shape[1], chunk):
+        hidden = gelu(mm(normed, up_scr[:, c : c + chunk])).astype(jnp.bfloat16)
+        total = total + mm(hidden, down_scr[c : c + chunk, :])
+    taps_scr[...] = (middle + total).astype(jnp.bfloat16)
 
 
 def pick_rows(step, phase, count):
@@ -272,74 +249,82 @@
     return total
 
 
-def side_kernel(
-    seqs,
-    meta_ref,
-    len_ref,
-    taps_ref,
-    x_ref,
-    go_ref,
-    gain_ref,
-    w_ref,
-    diag_ref,
-    onehot_ref,
-    out_ref,
-    ig_ref,
-    grow_ref,
-    gsmall_ref,
-    gain_scr,
-    wdown_scr,
-    wqkv_scr,
-    wqkv_turn_scr,
-    wout_turn_scr,
-    wup_scr,
-    wup_turn_scr,
-    wback_turn_scr,
-    bias_scr,
-    gbias_scr,
-    e_scr,
-    elow_scr,
-    gdown_scr,
-    gqkv_scr,
-    gproj_scr,
-    gup_scr,
-    gback_scr,
-    ggain_scr,
-):
-    step = pl.program_id(0)
-    at_qkv, at_out, at_up, at_back = D, D + 3 * DS, D + 4 * DS, D + 8 * DS
-    low = lambda v: v.astype(jnp.bfloat16)
-
-    @pl.when(step == 0)
-    def _():
-        wdown_scr[...] = w_ref[0:D, :].T
-        for t in range(3):
-            part = mm(pick_rows(3, t, DS), w_ref[at_qkv:at_out, :])
-            wqkv_scr[t] = low(part)
-            wqkv_turn_scr[t * L : t * L + DS, :] = low(part.T)
-            wqkv_turn_scr[t * L + DS : (t + 1) * L, :] = jnp.zeros((L - DS, DS), jnp.bfloat16)
-        wout_turn_scr[...] = w_ref[at_out:at_up, :].T
-        for t in range(4):
-            part = mm(pick_rows(4, t, DS), w_ref[at_up:at_back, :])
-            wup_scr[:, t * DS : (t + 1) * DS] = low(part)
-            wup_turn_scr[t * DS : (t + 1) * DS, :] = low(part.T)
-        wback_turn_scr[...] = w_ref[at_back : at_back + SFF, :].T
-        for row in range(3):
-            wide = jnp.broadcast_to(gain_ref[row : row + 1, :], (L, DS)).T
-            gain_scr[row] = jax.nn.sigmoid(wide) if row == 2 else wide
-        for head in range(SH):
-            bias_scr[head * L : (head + 1) * L, :] = spread_bias(diag_ref[head : head + 1, :])
-        for ref in (gbias_scr, gdown_scr, gqkv_scr, gproj_scr, gup_scr, gback_scr, ggain_scr):
-            ref[...] = jnp.zeros_like(ref)
-
+AT_QKV, AT_OUT, AT_UP, AT_BACK, AT_END = D, D + 3 * DS, D + 4 * DS, D + 8 * DS, D + 8 * DS + SFF
+
+
+def low(values):
+    return values.astype(jnp.bfloat16)
+
+
+def side_setup(gain_ref, w_ref, diag_ref, scratch):
+    (
+        gain_scr,
+        wdown_scr,
+        wqkv_scr,
+        wqkv_turn_scr,
+        wout_turn_scr,
+        wup_scr,
+        wup_turn_scr,
+        wback_turn_scr,
+        bias_scr,
+        gbias_scr,
+        elow_scr,
+        gdown_scr,
+        gqkv_scr,
+        gproj_scr,
+        gup_scr,
+        gback_scr,
+        ggain_scr,
+    ) = scratch
+    wdown_scr[...] = w_ref[0:D, :].T
+    for t in range(3):
+        part = mm(pick_rows(3, t, DS), w_ref[AT_QKV:AT_OUT, :])
+        wqkv_scr[t] = low(part)
+        wqkv_turn_scr[t * L : t * L + DS, :] = low(part.T)
+        wqkv_turn_scr[t * L + DS : (t + 1) * L, :] = jnp.zeros((L - DS, DS), jnp.bfloat16)
+    wout_turn_scr[...] = w_ref[AT_OUT:AT_UP, :].T
+    for t in range(4):
+        part = mm(pick_rows(4, t, DS), w_ref[AT_UP:AT_BACK, :])
+        wup_scr[:, t * DS : (t + 1) * DS] = low(part)
+        wup_turn_scr[t * DS : (t + 1) * DS, :] = low(part.T)
+    wback_turn_scr[...] = w_ref[AT_BACK : AT_END, :].T
+    for row in range(3):
+        wide = jnp.broadcast_to(gain_ref[row : row + 1, :], (L, DS)).T
+        gain_scr[row] = jax.nn.sigmoid(wide) if row == 2 else wide
+    for head in range(SH):
+        bias_scr[head * L : (head + 1) * L, :] = spread_bias(diag_ref[head : head + 1, :])
+    for ref in (gbias_scr, gdown_scr, gqkv_scr, gproj_scr, gup_scr, gback_scr, ggain_scr):
+        ref[...] = jnp.zeros_like(ref)
+
+
+def side_block(lengths, taps_scr, x_ref, go_ref, w_ref, out_ref, ig_ref, scratch):
+    (
+        gain_scr,
+        wdown_scr,
+        wqkv_scr,
+        wqkv_turn_scr,
+        wout_turn_scr,
+        wup_scr,
+        wup_turn_scr,
+        wback_turn_scr,
+        bias_scr,
+        gbias_scr,
+        elow_scr,
+        gdown_scr,
+        gqkv_scr,
+        gproj_scr,
+        gup_scr,
+        gback_scr,
+        ggain_scr,
+    ) = scratch
+    seqs = len(lengths)
     wide = lambda row: jnp.concatenate([gain_scr[row]] * seqs, axis=1)
     gain_one, gain_two, gate = wide(0), wide(1), wide(2)
-    w_out = w_ref[at_out:at_up, :]
-    w_back = w_ref[at_back : at_back + SFF, :]
-    lengths = [len_ref[meta_ref[0] + step * seqs + s] for s in range(seqs)]
+    w_out = w_ref[AT_OUT:AT_UP, :]
+    w_back = w_ref[AT_BACK : AT_END, :]
     key_row = lax.broadcasted_iota(jnp.int32, (SH, L, L), 1)
     token = lax.broadcasted_iota(jnp.int32, (DS, L), 1)
-    taps = taps_ref[...]
+    taps = taps_scr[...]
     x = jnp.concatenate([x_ref[s] for s in range(seqs)], axis=1)
     grad_out = jnp.concatenate(
         [jnp.where(token < lengths[s], go_ref[s], 0.0) for s in range(seqs)], axis=1
@@ -361,7 +346,6 @@
             scores = score_two[:, side * L : (side + 1) * L] + bias_scr[...]
             scores = jnp.where(key_row < lengths[s + side], scores.reshape(SH, L, L), MASKED)
             shifted = jnp.exp(scores - jnp.max(scores, axis=1, keepdims=True))
-            e_scr[s + side] = shifted
             e_low = low(shifted).reshape(SH * L, L)
             elow_scr[s + side] = e_low
             total = 1.0 / jnp.sum(shifted, axis=1, keepdims=True)
@@ -404,7 +388,9 @@
         for side in range(2):
             at = slice((s + side) * L, (s + side + 1) * L)
             grad_probs = prob_two[:, side * L : (side + 1) * L].reshape(SH, L, L)
-            grad_scores = e_scr[s + side] * (grad_probs - dots[:, :, at])
+            grad_scores = elow_scr[s + side].astype(jnp.float32).reshape(SH, L, L) * (
+                grad_probs - dots[:, :, at]
+            )
             gbias_scr[...] += grad_scores.reshape(SH * L, L)
             grad_scores = low(grad_scores).reshape(SH * L, L)
             grad_query.append(low(mm(by_head_lanes(key[0:DS, at]), grad_scores)))
@@ -432,70 +418,223 @@
         out_ref[s] = side_out[:, s * L : (s + 1) * L]
         ig_ref[s] = input_grad[:, s * L : (s + 1) * L]
 
+
+def side_finish(onehot_ref, send_ref, grow_scr, scratch):
+    (
+        gain_scr,
+        wdown_scr,
+        wqkv_scr,
+        wqkv_turn_scr,
+        wout_turn_scr,
+        wup_scr,
+        wup_turn_scr,
+        wback_turn_scr,
+        bias_scr,
+        gbias_scr,
+        elow_scr,
+        gdown_scr,
+        gqkv_scr,
+        gproj_scr,
+        gup_scr,
+        gback_scr,
+        ggain_scr,
+    ) = scratch
+    grow_scr[:, DS:] = jnp.zeros((grow_scr.shape[0], grow_scr.shape[1] - DS), jnp.bfloat16)
+    grow_scr[0:D, 0:DS] = low(gdown_scr[...].T)
+    spread = mm(pick_rows(3, 0, DS), low(gqkv_scr[0]), TN)
+    for t in range(1, 3):
+        spread = spread + mm(pick_rows(3, t, DS), low(gqkv_scr[t]), TN)
+    grow_scr[AT_QKV:AT_OUT, 0:DS] = low(spread)
+    grow_scr[AT_OUT:AT_UP, 0:DS] = low(gproj_scr[...])
+    spread = mm(pick_rows(4, 0, DS), low(gup_scr[:, 0:DS]), TN)
+    for t in range(1, 4):
+        spread = spread + mm(pick_rows(4, t, DS), low(gup_scr[:, t * DS : (t + 1) * DS]), TN)
+    grow_scr[AT_UP:AT_BACK, 0:DS] = low(spread)
+    grow_scr[AT_BACK : AT_END, 0:DS] = low(gback_scr[...])
+    flip_row = lax.broadcasted_iota(jnp.int32, (L, L), 0)
+    flip_column = lax.broadcasted_iota(jnp.int32, (L, L), 1)
+    flip = (flip_row + flip_column == L - 1).astype(jnp.float32)
+    diagonals = []
+    for head in range(SH):
+        square = lax.dot_general(
+            flip,
+            gbias_scr[head * L : (head + 1) * L, :],
+            NN,
+            precision=PRECISE,
+            preferred_element_type=jnp.float32,
+        )
+        full = jnp.concatenate([square, jnp.zeros_like(square)], axis=1)
+        rolled = pltpu.roll(full, 0, 1, stride=1, stride_axis=0)
+        diagonals.append(jnp.sum(rolled, axis=0, keepdims=True))
+    diagonals = jnp.concatenate(diagonals, axis=0)
+    shard_rows = AT_END // send_ref.shape[0]
+    small = shard_rows + SH
+    for device in range(send_ref.shape[0]):
+        send_ref[device, 0:shard_rows, :] = grow_scr[
+            device * shard_rows : (device + 1) * shard_rows, :
+        ]
+    gains = []
+    for row in range(3):
+        total = ggain_scr[row]
+        if row == 2:
+            total = total * (gain_scr[2] * (1.0 - gain_scr[2]))
+        gains.append(jnp.sum(total.T, axis=0, keepdims=True))
+    gains.append(jnp.zeros((SH - 3, DS), jnp.float32))
+    table = lax.dot_general(
+        diagonals, onehot_ref[...], NT, precision=PRECISE, preferred_element_type=jnp.float32
+    )
+    extra = low(jnp.concatenate([jnp.concatenate(gains, axis=0), table], axis=1))
+    blank = jnp.zeros((send_ref.shape[1] - small, L), jnp.bfloat16)
+    for device in range(send_ref.shape[0]):
+        send_ref[device, shard_rows:small, :] = extra
+        if small < send_ref.shape[1]:
+            send_ref[device, small:, :] = blank
+
+
+def main_kernel(
+    seqs,
+    chunk,
+    meta_ref,
+    len_ref,
+    tok_ref,
+    gain_ref,
+    far_ref,
+    mate_ref,
+    diag_ref,
+    near_ref,
+    x_ref,
+    go_ref,
+    side_gain_ref,
+    side_diag_ref,
+    onehot_ref,
+    wo_hbm,
+    up_hbm,
+    down_hbm,
+    w_hbm,
+    out_ref,
+    ig_ref,
+    send_ref,
+    w_scr,
+    bias_scr,
+    ctx_scr,
+    taps_scr,
+    wo_scr,
+    up_scr,
+    down_scr,
+    wrow_scr,
+    grow_scr,
+    sems,
+    *scratch,
+):
+    step = pl.program_id(0)
+    group = meta_ref[2]
+    width = near_ref.shape[0]
+    copies = [
+        pltpu.make_async_copy(
+            wo_hbm.at[pl.ds(group * width, width), :], wo_scr.at[pl.ds(0, width), :], sems.at[0]
+        ),
+        pltpu.make_async_copy(
+            wo_hbm.at[pl.ds((1 - group) * width, width), :],
+            wo_scr.at[pl.ds(width, width), :],
+            sems.at[1],
+        ),
+        pltpu.make_async_copy(up_hbm, up_scr, sems.at[2]),
+        pltpu.make_async_copy(down_hbm, down_scr, sems.at[3]),
+        pltpu.make_async_copy(w_hbm, wrow_scr, sems.at[4]),
+    ]
+
+    @pl.when(step == 0)
+    def _():
+        for copy in copies:
+            copy.start()
+        attention_setup(meta_ref[1], 1 - group, far_ref, mate_ref, diag_ref, w_scr, bias_scr)
+
+    lengths = [len_ref[meta_ref[0] + step * seqs + s] for s in range(seqs)]
+    rows = tok_ref[...].reshape(seqs * L, D).astype(jnp.float32)
+    attention_block(lengths, rows, gain_ref[0:1, :], w_scr, bias_scr, ctx_scr)
+
+    @pl.when(step == 0)
+    def _():
+        for copy in copies:
+            copy.wait()
+        side_setup(side_gain_ref, wrow_scr, side_diag_ref, scratch)
+
+    rows = tok_ref[...].reshape(seqs * L, D).astype(jnp.float32)
+    feed_block(
+        chunk, rows, near_ref[...], ctx_scr[...], gain_ref[1:2, :], wo_scr, up_scr, down_scr, taps_scr
+    )
+    side_block(lengths, taps_scr, x_ref, go_ref, wrow_scr, out_ref, ig_ref, scratch)
+
     @pl.when(step == pl.num_programs(0) - 1)
     def _():
-        grow_ref[:, DS:] = jnp.zeros((grow_ref.shape[0], grow_ref.shape[1] - DS), jnp.bfloat16)
-        grow_ref[0:D, 0:DS] = low(gdown_scr[...].T)
-        spread = mm(pick_rows(3, 0, DS), low(gqkv_scr[0]), TN)
-        for t in range(1, 3):
-            spread = spread + mm(pick_rows(3, t, DS), low(gqkv_scr[t]), TN)
-        grow_ref[at_qkv:at_out, 0:DS] = low(spread)
-        grow_ref[at_out:at_up, 0:DS] = low(gproj_scr[...])
-        spread = mm(pick_rows(4, 0, DS), low(gup_scr[:, 0:DS]), TN)
-        for t in range(1, 4):
-            spread = spread + mm(pick_rows(4, t, DS), low(gup_scr[:, t * DS : (t + 1) * DS]), TN)
-        grow_ref[at_up:at_back, 0:DS] = low(spread)
-        grow_ref[at_back : at_back + SFF, 0:DS] = low(gback_scr[...])
-        flip_row = lax.broadcasted_iota(jnp.int32, (L, L), 0)
-        flip_column = lax.broadcasted_iota(jnp.int32, (L, L), 1)
-        flip = (flip_row + flip_column == L - 1).astype(jnp.float32)
-        diagonals = []
-        for head in range(SH):
-            square = lax.dot_general(
-                flip,
-                gbias_scr[head * L : (head + 1) * L, :],
-                NN,
-                precision=PRECISE,
-                preferred_element_type=jnp.float32,
-            )
-            full = jnp.concatenate([square, jnp.zeros_like(square)], axis=1)
-            rolled = pltpu.roll(full, 0, 1, stride=1, stride_axis=0)
-            diagonals.append(jnp.sum(rolled, axis=0, keepdims=True))
-        diagonals = jnp.concatenate(diagonals, axis=0)
-        gsmall_ref[...] = jnp.zeros_like(gsmall_ref)
-        for row in range(3):
-            total = ggain_scr[row]
-            if row == 2:
-                total = total * (gain_scr[2] * (1.0 - gain_scr[2]))
-            gsmall_ref[row : row + 1, 0:DS] = jnp.sum(total.T, axis=0, keepdims=True)
-        gsmall_ref[4 : 4 + SH, 0 : onehot_ref.shape[0]] = lax.dot_general(
-            diagonals, onehot_ref[...], NT, precision=PRECISE, preferred_element_type=jnp.float32
-        )
-
-
-def side_part(meta, lengths, taps, side_input, output_grad, gains, w_rows, diag, onehot, seqs):
+        side_finish(onehot_ref, send_ref, grow_scr, scratch)
+
+
+def main_part(
+    meta,
+    lengths,
+    tokens,
+    gains,
+    far,
+    mate,
+    diag,
+    ctx_near,
+    side_input,
+    output_grad,
+    side_gains,
+    side_diag,
+    onehot,
+    w_out,
+    w_up,
+    w_down,
+    w_rows,
+    devices,
+    seqs,
+    chunk,
+):
     own_seqs = side_input.shape[0]
-    grid = own_seqs // seqs
+    width = ctx_near.shape[0]
+    ff = w_up.shape[1]
+    send_rows = -(-(w_rows.shape[0] // devices + SH) // 8) * 8
     fixed = lambda *dims: pl.BlockSpec(dims, lambda i, m, n: (0,) * len(dims))
     block = pl.BlockSpec((seqs, DS, L), lambda i, m, n: (i, 0, 0))
+    hbm = pl.BlockSpec(memory_space=pl.ANY)
     f32, bf16 = jnp.float32, jnp.bfloat16
     return pl.pallas_call(
-        functools.partial(side_kernel, seqs),
-        name="side",
+        functools.partial(main_kernel, seqs, chunk),
+        name="main",
         grid_spec=pltpu.PrefetchScalarGridSpec(
             num_scalar_prefetch=2,
-            grid=(grid,),
+            grid=(own_seqs // seqs,),
             in_specs=[
-                pl.BlockSpec((seqs * L, D), lambda i, m, n: (i, 0)),
+                pl.BlockSpec((seqs, L, D), lambda i, m, n: (m[0] // seqs + i, 0, 0)),
+                fixed(2, D),
+                fixed(*far.shape),
+                fixed(*mate.shape),
+                fixed(*diag.shape),
+                pl.BlockSpec((width, seqs * L), lambda i, m, n: (0, i)),
                 block,
                 block,
-                fixed(*gains.shape),
-                fixed(*w_rows.shape),
-                fixed(*diag.shape),
+                fixed(*side_gains.shape),
+                fixed(*side_diag.shape),
                 fixed(*onehot.shape),
+                hbm,
+                hbm,
+                hbm,
+                hbm,
             ],
-            out_specs=[block, block, fixed(w_rows.shape[0], L), fixed(16, L)],
+            out_specs=[block, block, fixed(devices, send_rows, L)],
             scratch_shapes=[
+                pltpu.VMEM((3 * width, D), bf16),
+                pltpu.VMEM((width // HD * L, L), f32),
+                pltpu.VMEM((width, seqs * L), bf16),
+                pltpu.VMEM((seqs * L, D), bf16),
+                pltpu.VMEM(w_out.shape, bf16),
+                pltpu.VMEM(w_up.shape, bf16),
+                pltpu.VMEM(w_down.shape, bf16),
+                pltpu.VMEM(w_rows.shape, bf16),
+                pltpu.VMEM((w_rows.shape[0], L), bf16),
+                pltpu.SemaphoreType.DMA((5,)),
                 pltpu.VMEM((3, DS, L), f32),
                 pltpu.VMEM((DS, D), bf16),
                 pltpu.VMEM((3, DS, DS), bf16),
@@ -506,7 +645,6 @@
                 pltpu.VMEM((DS, SFF), bf16),
                 pltpu.VMEM((SH * L, L), f32),
                 pltpu.VMEM((SH * L, L), f32),
-                pltpu.VMEM((seqs, SH, L, L), f32),
                 pltpu.VMEM((seqs, SH * L, L), bf16),
                 pltpu.VMEM((DS, D), f32),
                 pltpu.VMEM((3, DS, DS), f32),
@@ -519,18 +657,36 @@
         out_shape=[
             jax.ShapeDtypeStruct(side_input.shape, f32),
             jax.ShapeDtypeStruct(side_input.shape, f32),
-            jax.ShapeDtypeStruct((w_rows.shape[0], L), bf16),
-            jax.ShapeDtypeStruct((16, L), f32),
+            jax.ShapeDtypeStruct((devices, send_rows, L), bf16),
         ],
         compiler_params=pltpu.CompilerParams(
-            dimension_semantics=("arbitrary",), vmem_limit_bytes=56 * MIB
+            dimension_semantics=("arbitrary",), vmem_limit_bytes=VMEM_MAIN * MIB
         ),
         cost_estimate=pl.CostEstimate(
-            flops=own_seqs * 300_000_000,
-            bytes_accessed=own_seqs * L * (2 * D + 16 * DS),
-            transcendentals=own_seqs * L * (SH * L + SFF),
-        ),
-    )(meta, lengths, taps, side_input, output_grad, gains, w_rows, diag, onehot)
+            flops=2 * own_seqs * L * (D * (D + 2 * ff) + width * (3 * D + 2 * L))
+            + own_seqs * 300_000_000,
+            bytes_accessed=own_seqs * L * (3 * D + 16 * DS) + 2 * D * (D + 2 * ff),
+            transcendentals=own_seqs * L * (ff + 2 * SH * L + SFF),
+        ),
+    )(
+        meta,
+        lengths,
+        tokens,
+        gains,
+        far,
+        mate,
+        diag,
+        ctx_near,
+        side_input,
+        output_grad,
+        side_gains,
+        side_diag,
+        onehot,
+        w_out,
+        w_up,
+        w_down,
+        w_rows,
+    )
 
 
 def adamw_update(weight_now, first_now, second_now, gradient, rate, decay_rate):
@@ -579,63 +735,51 @@
     own_seqs = side_input.shape[0]
     shard_rows = side_weights.shape[0] // DS
     buckets = side_table.shape[0]
-    group = model_index // 2
-    near = jnp.stack([model_index * own_seqs, model_index % 2, group]).astype(jnp.int32)
-    far = jnp.stack([model_index * own_seqs, model_index % 2, 1 - group]).astype(jnp.int32)
+    meta = jnp.stack([model_index * own_seqs, model_index % 2, model_index // 2]).astype(jnp.int32)
 
     turn = lambda values: jnp.transpose(values, (0, 2, 1))
     qkv_own = turn(base_qkv)
     qkv_far = swap(qkv_own, 2)
     qkv_mate = swap(qkv_own, 1)
+    low_rows = side_weights.astype(jnp.bfloat16).reshape(1, shard_rows, DS)
+    w_rows = exchange(jnp.broadcast_to(low_rows, (devices, shard_rows, DS)))
 
     onehot = jnp.asarray(diagonal_onehot(buckets))
     base_diag = jnp.dot(base_table.T, onehot, precision=PRECISE)
     side_diag = jnp.dot(side_table.T, onehot, precision=PRECISE)
 
-    ctx_near = attention_part(
-        near, lengths, tokens, base_gains, qkv_own, qkv_mate, base_diag, own_seqs, 8
-    )
-    ctx_near, qkv_far, low_rows = lax.optimization_barrier(
-        (ctx_near, qkv_far, side_weights.astype(jnp.bfloat16).reshape(1, shard_rows, DS))
-    )
-    qkv_far_mate = swap(qkv_far, 1)
-    w_rows = exchange(jnp.broadcast_to(low_rows, (devices, shard_rows, DS)))
-    ctx_far = attention_part(
-        far, lengths, tokens, base_gains, qkv_far, qkv_far_mate, base_diag, own_seqs, 8
-    )
-    taps = ffn_part(
-        near, ctx_near, ctx_far, tokens, base_gains, base_out, base_up, base_down, own_seqs, 8, 1024
-    )
-    taps, w_rows = lax.optimization_barrier((taps, w_rows))
-    w_rows = w_rows.reshape(devices * shard_rows, DS)
-    side_output, input_grad, grad_rows, grad_small = side_part(
-        near,
+    ctx_near = near_part(
+        meta, lengths, tokens, base_gains, qkv_own, qkv_mate, base_diag, own_seqs, 8
+    )
+    ctx_near, qkv_far, w_rows = lax.optimization_barrier((ctx_near, qkv_far, w_rows))
+    side_output, input_grad, outgoing = main_part(
+        meta,
         lengths,
-        taps,
+        tokens,
+        base_gains,
+        qkv_far,
+        swap(qkv_far, 1),
+        base_diag,
+        ctx_near,
         turn(side_input),
         turn(output_grad),
         side_gains,
-        w_rows,
         side_diag,
         jnp.asarray(gradient_onehot(buckets)),
+        base_out,
+        base_up,
+        base_down,
+        w_rows.reshape(devices * shard_rows, DS),
+        devices,
         8,
-    )
-
-    small_high = grad_small.astype(jnp.bfloat16)
-    small_low = (grad_small - small_high.astype(jnp.float32)).astype(jnp.bfloat16)
-    small = jnp.concatenate([small_high, small_low], axis=0)
-    outgoing = jnp.concatenate(
-        [
-            grad_rows.reshape(devices, shard_rows, L),
-            jnp.broadcast_to(small[None], (devices,) + small.shape),
-        ],
-        axis=1,
-    )
+        1024,
+    )
+
     summed = jnp.sum(exchange(outgoing).astype(jnp.float32), axis=0)
     grad_shard = lax.optimization_barrier(summed[:shard_rows, :DS].reshape(-1))
-    small_total = summed[shard_rows : shard_rows + 16] + summed[shard_rows + 16 :]
+    small_total = summed[shard_rows : shard_rows + SH]
     gains_total = small_total[0:3, :DS]
-    table_total = small_total[4 : 4 + SH, :buckets].T
+    table_total = small_total[:, DS : DS + buckets].T
     square = jnp.sum(grad_shard * grad_shard)
     squares = exchange(jnp.broadcast_to(square, (devices, L)))
     grad_norm = jnp.sqrt(

time: 179 us -> 164 us (0.916)
  Pallas kernels: 112 us -> 104 us
  blocking collectives: 26.3 us -> 21.3 us
  waiting for transfers between devices: 7.21 us -> 10.2 us
    pallas_call x4 -> x2, Pallas kernels: 112 us -> 104 us  [the longest x1 88.9 us: main_part(): pl.pallas_call(functools.partial(main_kernel, seqs, chunk), name='main',...]
    all_to_all x1, blocking collectives: 26.3 us -> 21.3 us  [exchange(): lax.all_to_all(values, ('batch', 'mp'), split_axis=0, concat_axis=0, tile...]
    all_to_all x2, waiting for transfers between devices: 5.87 us -> 9.56 us  [exchange(): lax.all_to_all(values, ('batch', 'mp'), split_axis=0, concat_axis=0, tile...]
  transfers between devices with their start and end apart: 5 -> 5, of which waited for: 2 -> 3; matrix products, arithmetic and copies ran while one was open for 4% -> 3% of each run, Pallas kernels for 42% -> 9%
where the time goes in v3:
time: 164 us
  Pallas kernels  104 us (63%)
  blocking collectives  21.3 us (13%)
  starting transfers between devices  11.3 us (7%)
  waiting for transfers between devices  10.2 us (6%)
  other arithmetic  5.86 us (4%)
  local copies, waits for them, and re-layouts  5.22 us (3%)
  between operations  3.98 us (2%)
    pallas_call x1, Pallas kernels, main_part(): pl.pallas_call(functools.partial(main_kernel, seqs, chunk), name='main',...  88.9 us
    all_to_all x1, blocking collectives, exchange(): lax.all_to_all(values, ('batch', 'mp'), split_axis=0, concat_axis=0, tile...  21.3 us
    pallas_call x1, Pallas kernels, near_part(): pl.pallas_call(functools.partial(near_kernel, seqs), name='near', grid_sp...  15.2 us
    all_to_all x2, waiting for transfers between devices, exchange(): lax.all_to_all(values, ('batch', 'mp'), split_axis=0, concat_axis=0, tile...  9.56 us
    all_to_all x2, starting transfers between devices, exchange(): lax.all_to_all(values, ('batch', 'mp'), split_axis=0, concat_axis=0, tile...  8.22 us
  transfers between devices with their start and end apart: 5, of which 3 were waited for; matrix products, arithmetic and copies ran while one was open for 3% of the time, Pallas kernels for 9%

profile of v3, /device:TPU:0, one launch (start us, length us, event | category | flops | bytes accessed | tf_op | source)
XLA Modules:
  0.0 163.6 jit_solution(8018510248014673522)
XLA Ops:
  0.6 0.0 copy-start
  0.7 0.0 copy-start.2
  0.7 0.5 collective-permute-start
  1.2 2.6 %collective-permute-start.1 = (bf16[3,192,768]{2,1,0:T(8,128)(2,1)}, bf16[3,192,768]{2,1,0:T(8,128)(2,1)S(1)}, u32[]{:S(2)}, u32[]{:S(2)}) collective-permute-start(bf16[3,192,768]{2,1,0:T(8,128)(2,1)} %bitcast.25), channel_id=1, source_target_pairs={{0,2},{1,3},{2,0},{3,1},{4,6},{5,7},{6,4},{7,5},{8,10},{9,11},{10,... | collective-permute-start | bytes 2654216 | tf_op jit(solution)/shard_map/ppermute | solution.py:705
  3.8 0.7 convert_element_type.9
  4.5 0.1 broadcast_in_dim.10
  4.6 0.9 broadcast_in_dim.11
  5.5 4.9 %all-to-all-start = ((bf16[32,60,96]{2,1,0:T(8,128)(2,1)}), bf16[32,60,96]{2,1,0:T(8,128)(2,1)S(1)}, u32[]{:S(2)}, u32[]{:S(2)}) async-start(bf16[32,60,96]{2,1,0:T(8,128)(2,1)} %broadcast_in_dim.11), calls=%async_computation | async-start | bytes 1048576 | tf_op jit(solution)/shard_map/all_to_all | solution.py:709
  10.4 0.0 copy-done
  10.4 0.0 copy-done.2
  10.5 0.7 convolution_bitcast_fusion.1.diag_ref
  11.2 0.6 pad_add_fusion.meta_ref
  11.8 0.0 collective-permute-done.mate_ref
  11.8 0.9 copy-done.1
  12.7 15.2 %near.1.near_ref = bf16[384,3072]{1,0:T(8,128)(2,1)} custom-call(s32[3]{0:T(128)} %pad_add_fusion.meta_ref, s32[96]{0:T(128)} %len_ref.3, bf16[96,128,768]{2,1,0:T(8,128)(2,1)} %tok_ref.3, f32[2,768]{1,0:T(2,128)} %gain_ref.3, bf16[3,192,768]{2,1,0:T(8,128)(2,1)} %bitcast.26, bf16[3,192,768]{2,1,0:T(8,128)(2,1)} %copy-done.1, ...), custom_call_target="tpu_custom_call" | custom-call | flops 6039797760 | bytes 8847360 | tf_op jit(solution)/shard_map/near/pallas_call | solution.py:159
  28.0 3.1 %all-to-all-done = bf16[32,60,96]{2,1,0:T(8,128)(2,1)S(1)} async-done(((bf16[32,60,96]{2,1,0:T(8,128)(2,1)}), bf16[32,60,96]{2,1,0:T(8,128)(2,1)S(1)}, u32[]{:S(2)}, u32[]{:S(2)}) %all-to-all-start) | async-done | bytes 368672 | tf_op jit(solution)/shard_map/all_to_all | solution.py:709
  31.0 0.0 collective-permute-done.1.far_ref
  31.1 0.0 collective-permute-start.2
  31.1 0.0 copy-done.4
  31.1 0.9 convolution_bitcast_fusion.side_diag_ref
  31.9 0.9 reshape.36.w_hbm
  32.9 0.6 collective-permute-done.2.mate_ref
  33.5 0.0 copy-done.12
  33.5 0.9 copy-done.13
  34.4 88.9 %main.1 = (f32[24,96,128]{2,1,0:T(8,128)}, f32[24,96,128]{2,1,0:T(8,128)}, bf16[32,72,128]{2,1,0:T(8,128)(2,1)}) custom-call(s32[3]{0:T(128)} %pad_add_fusion.meta_ref, s32[96]{0:T(128)} %len_ref.3, bf16[96,128,768]{2,1,0:T(8,128)(2,1)} %tok_ref.3, f32[2,768]{1,0:T(2,128)} %gain_ref.3, bf16[3,192,768]{2,1,0:T(8,128)(2,1)} %copy-done.12, ...), custom_call_target="tpu_custom_call" | custom-call | flops 45854703616 | bytes 22413312 | tf_op jit(solution)/shard_map/main/pallas_call | solution.py:603
  123.3 0.0 copy-start.9
  123.3 0.0 copy-start.10
  123.4 0.0 copy-start.11
  123.4 0.0 copy-start.7
  123.4 0.0 copy-start.8
  123.4 0.0 copy-start.3
  123.4 0.0 copy-start.5
  123.4 0.0 copy-start.6
  123.4 21.3 %all_to_all.19 = bf16[32,72,128]{2,1,0:T(8,128)(2,1)S(1)} all-to-all(bf16[32,72,128]{2,1,0:T(8,128)(2,1)} %get-tuple-element.24), channel_id=1, replica_groups=mesh['batch'=8,'mp'=4] {'batch','mp'}, dimensions={0} | all-to-all | bytes 1179648 | tf_op jit(solution)/shard_map/all_to_all | solution.py:709
  144.7 0.1 convert_reduce_fusion
  144.8 0.7 multiply_reduce_fusion.1
  145.5 0.1 reshape.37
  145.6 0.6 multiply_reduce_fusion
  146.2 1.3 broadcast_in_dim.12
  147.4 3.3 %all-to-all-start.2 = ((f32[32,1,128]{2,1,0:T(1,128)}), f32[32,1,128]{2,1,0:T(1,128)S(1)}, u32[]{:S(2)}, u32[]{:S(2)}) async-start(f32[32,1,128]{2,1,0:T(1,128)} %broadcast_in_dim.12), calls=%async_computation.2 | async-start | bytes 32768 | tf_op jit(solution)/shard_map/all_to_all | solution.py:709
  150.7 0.6 multiply_reduce_fusion.2
  151.3 6.5 %all-to-all-done.2 = f32[32,1,128]{2,1,0:T(1,128)S(1)} async-done(((f32[32,1,128]{2,1,0:T(1,128)}), f32[32,1,128]{2,1,0:T(1,128)S(1)}, u32[]{:S(2)}, u32[]{:S(2)}) %all-to-all-start.2) | async-done | bytes 16416 | tf_op jit(solution)/shard_map/all_to_all | solution.py:709
  157.8 0.6 slice_reduce_fusion
  160.4 0.0 copy-done.9
  160.5 0.6 multiply_subtract_fusion.2
  161.1 0.7 multiply_subtract_fusion.1
  161.8 0.0 copy-done.5
  161.8 0.6 fusion.7
  (11 shorter events, 0.0 us)
Async XLA Ops:
  0.6 9.8 %copy-start = (f32[32,12]{0,1:T(8,128)S(1)}, f32[32,12]{0,1:T(8,128)}, u32[]{:S(2)}) copy-start(f32[32,12]{0,1:T(8,128)} %param.28) | copy-start | bytes 4612
  0.7 9.8 %copy-start.2 = (f32[32,256]{1,0:T(8,128)S(1)}, f32[32,256]{1,0:T(8,128)}, u32[]{:S(2)}) copy-start(f32[32,256]{1,0:T(8,128)} %constant.79.clone) | copy-start | bytes 98308
  0.7 11.1 %collective-permute-start = (bf16[3,192,768]{2,1,0:T(8,128)(2,1)}, bf16[3,192,768]{2,1,0:T(8,128)(2,1)S(1)}, u32[]{:S(2)}, u32[]{:S(2)}) collective-permute-start(bf16[3,192,768]{2,1,0:T(8,128)(2,1)} %bitcast.24), channel_id=1, source_target_pairs={{0,1},{1,0},{2,3},{3,2},{4,5},{5,4},{6,7},{7,6},{8,9},{9,8},{10,11... | collective-permute-start | bytes 2654216 | tf_op jit(solution)/shard_map/ppermute | solution.py:705
  1.2 29.9 %collective-permute-start.1 = (bf16[3,192,768]{2,1,0:T(8,128)(2,1)}, bf16[3,192,768]{2,1,0:T(8,128)(2,1)S(1)}, u32[]{:S(2)}, u32[]{:S(2)}) collective-permute-start(bf16[3,192,768]{2,1,0:T(8,128)(2,1)} %bitcast.25), channel_id=1, source_target_pairs={{0,2},{1,3},{2,0},{3,1},{4,6},{5,7},{6,4},{7,5},{8,10},{9,11},{10,... | collective-permute-start | bytes 2654216 | tf_op jit(solution)/shard_map/ppermute | solution.py:705
  5.5 25.5 %all-to-all-start = ((bf16[32,60,96]{2,1,0:T(8,128)(2,1)}), bf16[32,60,96]{2,1,0:T(8,128)(2,1)S(1)}, u32[]{:S(2)}, u32[]{:S(2)}) async-start(bf16[32,60,96]{2,1,0:T(8,128)(2,1)} %broadcast_in_dim.11), calls=%async_computation | async-start | bytes 1048576 | tf_op jit(solution)/shard_map/all_to_all | solution.py:709
  11.8 19.3 %copy-start.4 = (f32[32,12]{0,1:T(8,128)S(1)}, f32[32,12]{0,1:T(8,128)}, u32[]{:S(2)}) copy-start(f32[32,12]{0,1:T(8,128)} %param.37) | copy-start | bytes 4612
  11.8 0.9 copy-start.1
  31.0 2.4 %copy-start.12 = (bf16[3,192,768]{2,1,0:T(8,128)(2,1)}, bf16[3,192,768]{2,1,0:T(8,128)(2,1)S(1)}, u32[]{:S(2)}) copy-start(bf16[3,192,768]{2,1,0:T(8,128)(2,1)S(1)} %collective-permute-done.1.far_ref) | copy-start | bytes 2654212
  31.1 2.4 %collective-permute-start.2 = (bf16[3,192,768]{2,1,0:T(8,128)(2,1)S(1)}, bf16[3,192,768]{2,1,0:T(8,128)(2,1)S(1)}, u32[]{:S(2)}, u32[]{:S(2)}) collective-permute-start(bf16[3,192,768]{2,1,0:T(8,128)(2,1)S(1)} %collective-permute-done.1.far_ref), channel_id=1, source_target_pairs={{0,1},{1,0},{2,3},{3,2},{4,5},{5,4},{6,7},{7,6},{8,9},{9,8},{10,11... | collective-permute-start | bytes 2654216 | tf_op jit(solution)/shard_map/ppermute | solution.py:705
  33.5 0.9 copy-start.13
  123.3 37.1 %copy-start.9 = (f32[3,96]{1,0:T(4,128)S(1)}, f32[3,96]{1,0:T(4,128)}, u32[]{:S(2)}) copy-start(f32[3,96]{1,0:T(4,128)} %side_gain_ref.1) | copy-start | bytes 3460
  123.3 37.1 %copy-start.10 = (f32[3,96]{1,0:T(4,128)S(1)}, f32[3,96]{1,0:T(4,128)}, u32[]{:S(2)}) copy-start(f32[3,96]{1,0:T(4,128)} %param.36) | copy-start | bytes 3460
  123.4 37.1 %copy-start.11 = (f32[3,96]{1,0:T(4,128)S(1)}, f32[3,96]{1,0:T(4,128)}, u32[]{:S(2)}) copy-start(f32[3,96]{1,0:T(4,128)} %param.35) | copy-start | bytes 3460
  123.4 37.7 %copy-start.7 = (f32[32,12]{0,1:T(8,128)S(1)}, f32[32,12]{0,1:T(8,128)}, u32[]{:S(2)}) copy-start(f32[32,12]{0,1:T(8,128)} %param.39) | copy-start | bytes 4612
  123.4 37.7 %copy-start.8 = (f32[32,12]{0,1:T(8,128)S(1)}, f32[32,12]{0,1:T(8,128)}, u32[]{:S(2)}) copy-start(f32[32,12]{0,1:T(8,128)} %param.38) | copy-start | bytes 4612
  123.4 38.4 %copy-start.3 = (f32[5760]{0:T(1024)S(1)}, f32[5760]{0:T(1024)}, u32[]{:S(2)}) copy-start(f32[5760]{0:T(1024)} %param.31) | copy-start | bytes 69124
  123.4 38.4 %copy-start.5 = (f32[5760]{0:T(1024)S(1)}, f32[5760]{0:T(1024)}, u32[]{:S(2)}) copy-start(f32[5760]{0:T(1024)} %param.33) | copy-start | bytes 69124
  123.4 38.4 %copy-start.6 = (f32[5760]{0:T(1024)S(1)}, f32[5760]{0:T(1024)}, u32[]{:S(2)}) copy-start(f32[5760]{0:T(1024)} %param.32) | copy-start | bytes 69124
  147.4 10.4 %all-to-all-start.2 = ((f32[32,1,128]{2,1,0:T(1,128)}), f32[32,1,128]{2,1,0:T(1,128)S(1)}, u32[]{:S(2)}, u32[]{:S(2)}) async-start(f32[32,1,128]{2,1,0:T(1,128)} %broadcast_in_dim.12), calls=%async_computation.2 | async-start | bytes 32768 | tf_op jit(solution)/shard_map/all_to_all | solution.py:709

commit v4 on v3

--- a/solution.py
+++ b/solution.py
@@ -81,12 +81,24 @@
     return 0.5 * v * (1.0 + jnp.tanh(GELU_RATE * (v + GELU_CUBE * (v * v * v))))
 
 
+def diagonals_of(table_ref, onehot_ref):
+    return lax.dot_general(
+        table_ref[...],
+        onehot_ref[...],
+        NN,
+        precision=PRECISE,
+        preferred_element_type=jnp.float32,
+    )
+
+
 def spread_bias(row):
     full = jnp.broadcast_to(row, (L, SPAN))
     return pltpu.roll(full, 0, 1, stride=1, stride_axis=0)[:, :L]
 
 
-def attention_setup(parity, group, own_ref, mate_ref, diag_ref, w_scr, bias_scr):
+def attention_setup(
+    parity, group, own_ref, mate_ref, table_ref, onehot_ref, diag_scr, w_scr, bias_scr
+):
     third = own_ref.shape[1]
     width = 2 * third
     heads = width // HD
@@ -104,18 +116,18 @@
     def _():
         place(mate_ref, own_ref)
 
+    diag_scr[...] = diagonals_of(table_ref, onehot_ref)
     for head in range(heads):
         bias_scr[head * L : (head + 1) * L, :] = spread_bias(
-            diag_ref[pl.ds(group * heads + head, 1), :]
+            diag_scr[pl.ds(group * heads + head, 1), :]
         )
 
 
 def attention_block(lengths, rows, gain, w_scr, bias_scr, ctx_ref):
     width = w_scr.shape[0] // 3
     normed = (rows * rms_scale(rows) * gain).astype(jnp.bfloat16)
-    query = mm(w_scr[0:width, :], normed, NT).astype(jnp.bfloat16)
-    key = mm(normed, w_scr[width : 2 * width, :], NT).astype(jnp.bfloat16)
-    value = mm(w_scr[2 * width :, :], normed, NT).astype(jnp.bfloat16)
+    turned = mm(w_scr[...], normed, NT).astype(jnp.bfloat16)
+    query, key, value = turned[0:width], turned[width : 2 * width], turned[2 * width :]
     low_lane = lax.broadcasted_iota(jnp.int32, (L, PAIR), 1) < HD
     low_row = lax.broadcasted_iota(jnp.int32, (PAIR, L), 0) < HD
     key_row = lax.broadcasted_iota(jnp.int32, (2, L, L), 1)
@@ -124,7 +136,7 @@
         seen = key_row < length
         for p in range(width // PAIR):
             head = slice(p * PAIR, (p + 1) * PAIR)
-            k_one, v_one = key[at, head], value[head, at]
+            k_one, v_one = key[head, at].T, value[head, at]
             zero = jnp.zeros_like(k_one)
             k_two = jnp.concatenate(
                 [jnp.where(low_lane, k_one, zero), jnp.where(low_lane, zero, k_one)], axis=0
@@ -141,19 +153,43 @@
             ctx_ref[head, at] = (mm(v_two, probs) * scale).astype(jnp.bfloat16)
 
 
-def near_kernel(seqs, meta_ref, len_ref, tok_ref, gain_ref, own_ref, mate_ref, diag_ref, ctx_ref, w_scr, bias_scr):
+def near_kernel(
+    seqs,
+    meta_ref,
+    len_ref,
+    tok_ref,
+    gain_ref,
+    own_ref,
+    mate_ref,
+    table_ref,
+    onehot_ref,
+    ctx_ref,
+    diag_scr,
+    w_scr,
+    bias_scr,
+):
     step = pl.program_id(0)
 
     @pl.when(step == 0)
     def _():
-        attention_setup(meta_ref[1], meta_ref[2], own_ref, mate_ref, diag_ref, w_scr, bias_scr)
+        attention_setup(
+            meta_ref[1],
+            meta_ref[2],
+            own_ref,
+            mate_ref,
+            table_ref,
+            onehot_ref,
+            diag_scr,
+            w_scr,
+            bias_scr,
+        )
 
     lengths = [len_ref[meta_ref[0] + step * seqs + s] for s in range(seqs)]
     rows = tok_ref[...].reshape(seqs * L, D).astype(jnp.float32)
     attention_block(lengths, rows, gain_ref[0:1, :], w_scr, bias_scr, ctx_ref)
 
 
-def near_part(meta, lengths, tokens, gains, own, mate, diag, own_seqs, seqs):
+def near_part(meta, lengths, tokens, gains, own, mate, table, onehot, own_seqs, seqs):
     width = 2 * own.shape[1]
     fixed = lambda *dims: pl.BlockSpec(dims, lambda i, m, n: (0,) * len(dims))
     return pl.pallas_call(
@@ -167,10 +203,12 @@
                 fixed(2, D),
                 fixed(*own.shape),
                 fixed(*mate.shape),
-                fixed(*diag.shape),
+                fixed(*table.shape),
+                fixed(*onehot.shape),
             ],
             out_specs=pl.BlockSpec((width, seqs * L), lambda i, m, n: (0, i)),
             scratch_shapes=[
+                pltpu.VMEM((table.shape[0], SPAN), jnp.float32),
                 pltpu.VMEM((3 * width, D), jnp.bfloat16),
                 pltpu.VMEM((width // HD * L, L), jnp.float32),
             ],
@@ -184,18 +222,26 @@
             bytes_accessed=own_seqs * L * (D + width) * 2 + 6 * D * width,
             transcendentals=own_seqs * width // HD * L * L,
         ),
-    )(meta, lengths, tokens, gains, own, mate, diag)
+    )(meta, lengths, tokens, gains, own, mate, table, onehot)
 
 
 def feed_block(chunk, rows, near, far, gain, wo_scr, up_scr, down_scr, taps_scr):
     width = near.shape[0]
-    middle = rows + mm(near, wo_scr[0:width, :], TN) + mm(far, wo_scr[width:, :], TN)
-    normed = (middle * rms_scale(middle) * gain).astype(jnp.bfloat16)
-    total = jnp.zeros_like(middle)
-    for c in range(0, up_scr.shape[1], chunk):
-        hidden = gelu(mm(normed, up_scr[:, c : c + chunk])).astype(jnp.bfloat16)
-        total = total + mm(hidden, down_scr[c : c + chunk, :])
-    taps_scr[...] = (middle + total).astype(jnp.bfloat16)
+    size = rows.shape[0] // 2
+    halves = [slice(0, size), slice(size, 2 * size)]
+    middle = [
+        rows[at]
+        + mm(near[:, at], wo_scr[0:width, :], TN)
+        + mm(far[:, at], wo_scr[width:, :], TN)
+        for at in halves
+    ]
+    normed = [(part * rms_scale(part) * gain).astype(jnp.bfloat16) for part in middle]
+    for at, part, unit in zip(halves, middle, normed):
+        total = jnp.zeros_like(part)
+        for c in range(0, up_scr.shape[1], chunk):
+            hidden = gelu(mm(unit, up_scr[:, c : c + chunk])).astype(jnp.bfloat16)
+            total = total + mm(hidden, down_scr[c : c + chunk, :])
+        taps_scr[at, :] = (part + total).astype(jnp.bfloat16)
 
 
 def pick_rows(step, phase, count):
@@ -256,7 +302,7 @@
     return values.astype(jnp.bfloat16)
 
 
-def side_setup(gain_ref, w_ref, diag_ref, scratch):
+def side_setup(gain_ref, w_ref, table_ref, onehot_ref, scratch):
     (
         gain_scr,
         wdown_scr,
@@ -291,8 +337,9 @@
     for row in range(3):
         wide = jnp.broadcast_to(gain_ref[row : row + 1, :], (L, DS)).T
         gain_scr[row] = jax.nn.sigmoid(wide) if row == 2 else wide
+    diagonals = diagonals_of(table_ref, onehot_ref)
     for head in range(SH):
-        bias_scr[head * L : (head + 1) * L, :] = spread_bias(diag_ref[head : head + 1, :])
+        bias_scr[head * L : (head + 1) * L, :] = spread_bias(diagonals[head : head + 1, :])
     for ref in (gbias_scr, gdown_scr, gqkv_scr, gproj_scr, gup_scr, gback_scr, ggain_scr):
         ref[...] = jnp.zeros_like(ref)
 
@@ -500,13 +547,14 @@
     gain_ref,
     far_ref,
     mate_ref,
-    diag_ref,
+    table_ref,
     near_ref,
     x_ref,
     go_ref,
     side_gain_ref,
-    side_diag_ref,
+    side_table_ref,
     onehot_ref,
+    turn_onehot_ref,
     wo_hbm,
     up_hbm,
     down_hbm,
@@ -514,6 +562,7 @@
     out_ref,
     ig_ref,
     send_ref,
+    diag_scr,
     w_scr,
     bias_scr,
     ctx_scr,
@@ -547,7 +596,17 @@
     def _():
         for copy in copies:
             copy.start()
-        attention_setup(meta_ref[1], 1 - group, far_ref, mate_ref, diag_ref, w_scr, bias_scr)
+        attention_setup(
+            meta_ref[1],
+            1 - group,
+            far_ref,
+            mate_ref,
+            table_ref,
+            onehot_ref,
+            diag_scr,
+            w_scr,
+            bias_scr,
+        )
 
     lengths = [len_ref[meta_ref[0] + step * seqs + s] for s in range(seqs)]
     rows = tok_ref[...].reshape(seqs * L, D).astype(jnp.float32)
@@ -557,7 +616,7 @@
     def _():
         for copy in copies:
             copy.wait()
-        side_setup(side_gain_ref, wrow_scr, side_diag_ref, scratch)
+        side_setup(side_gain_ref, wrow_scr, side_table_ref, onehot_ref, scratch)
 
     rows = tok_ref[...].reshape(seqs * L, D).astype(jnp.float32)
     feed_block(
@@ -567,7 +626,7 @@
 
     @pl.when(step == pl.num_programs(0) - 1)
     def _():
-        side_finish(onehot_ref, send_ref, grow_scr, scratch)
+        side_finish(turn_onehot_ref, send_ref, grow_scr, scratch)
 
 
 def main_part(
@@ -577,13 +636,14 @@
     gains,
     far,
     mate,
-    diag,
+    table,
     ctx_near,
     side_input,
     output_grad,
     side_gains,
-    side_diag,
+    side_table,
     onehot,
+    turn_onehot,
     w_out,
     w_up,
     w_down,
@@ -611,13 +671,14 @@
                 fixed(2, D),
                 fixed(*far.shape),
                 fixed(*mate.shape),
-                fixed(*diag.shape),
+                fixed(*table.shape),
                 pl.BlockSpec((width, seqs * L), lambda i, m, n: (0, i)),
                 block,
                 block,
                 fixed(*side_gains.shape),
-                fixed(*side_diag.shape),
+                fixed(*side_table.shape),
                 fixed(*onehot.shape),
+                fixed(*turn_onehot.shape),
                 hbm,
                 hbm,
                 hbm,
@@ -625,6 +686,7 @@
             ],
             out_specs=[block, block, fixed(devices, send_rows, L)],
             scratch_shapes=[
+                pltpu.VMEM((table.shape[0], SPAN), f32),
                 pltpu.VMEM((3 * width, D), bf16),
                 pltpu.VMEM((width // HD * L, L), f32),
                 pltpu.VMEM((width, seqs * L), bf16),
@@ -675,13 +737,14 @@
         gains,
         far,
         mate,
-        diag,
+        table,
         ctx_near,
         side_input,
         output_grad,
         side_gains,
-        side_diag,
+        side_table,
         onehot,
+        turn_onehot,
         w_out,
         w_up,
         w_down,
@@ -698,6 +761,79 @@
         first_hat / (jnp.sqrt(second_hat) + ADAM_EPS) + decay_rate * weight_now
     )
     return (first_new, second_new, weight_new)
+
+
+def collect_kernel(shard_rows, got_ref, shard_ref, small_ref, square_ref):
+    total = got_ref[0].astype(jnp.float32)
+    for device in range(1, got_ref.shape[0]):
+        total = total + got_ref[device].astype(jnp.float32)
+    shard = total[0:shard_rows, 0:DS]
+    shard_ref[...] = shard
+    small_ref[...] = total[shard_rows : shard_rows + SH, :]
+    square = jnp.sum(jnp.sum(shard * shard, axis=1, keepdims=True), axis=0, keepdims=True)
+    square_ref[...] = jnp.broadcast_to(square, square_ref.shape)
+
+
+def collect_part(got, shard_rows):
+    devices = got.shape[0]
+    return pl.pallas_call(
+        functools.partial(collect_kernel, shard_rows),
+        name="collect",
+        out_shape=[
+            jax.ShapeDtypeStruct((shard_rows, DS), jnp.float32),
+            jax.ShapeDtypeStruct((SH, L), jnp.float32),
+            jax.ShapeDtypeStruct((devices, L), jnp.float32),
+        ],
+        in_specs=[pl.BlockSpec(memory_space=pltpu.VMEM)],
+        out_specs=[pl.BlockSpec(memory_space=pltpu.VMEM)] * 3,
+    )(got)
+
+
+def update_kernel(square_ref, small_ref, shard_ref, *refs):
+    weights, gains, table = refs[0:3], refs[3:6], refs[6:9]
+    norm_ref, copy_ref = refs[9], refs[13]
+    gains_total = small_ref[0:3, 0:DS]
+    table_total = small_ref[:, DS:]
+    whole = lambda values: jnp.sum(
+        jnp.sum(values, axis=1, keepdims=True), axis=0, keepdims=True
+    )
+    norm = jnp.sqrt(
+        jnp.sum(square_ref[:, 0:1], axis=0, keepdims=True)
+        + whole(gains_total * gains_total)
+        + whole(table_total * table_total)
+    )
+    norm_ref[...] = norm
+    factor = CLIP_NORM / jnp.maximum(norm, CLIP_NORM)
+
+    def update(state, gradient, outs, rate, decay):
+        results = adamw_update(*[ref[...] for ref in state], factor * gradient, rate, decay)
+        for ref, value in zip(outs, results):
+            ref[...] = value
+        return results[2]
+
+    new = update(weights, shard_ref[...], refs[10:13], RATE_MATRIX, WEIGHT_DECAY)
+    copy_ref[...] = new.astype(jnp.bfloat16)
+    update(gains, gains_total, refs[14:17], RATE_SMALL, 0.0)
+    update(table, table_total, refs[17:20], RATE_SMALL, 0.0)
+
+
+def update_part(squares, small, shard, weights, gains, table):
+    f32 = jnp.float32
+    like = lambda values, dtype=f32: jax.ShapeDtypeStruct(values.shape, dtype)
+    operands = (squares, small, shard, *weights, *gains, *table)
+    return pl.pallas_call(
+        update_kernel,
+        name="update",
+        out_shape=[
+            jax.ShapeDtypeStruct((1, 1), f32),
+            *[like(values) for values in weights],
+            like(shard, jnp.bfloat16),
+            *[like(values) for values in gains],
+            *[like(values) for values in table],
+        ],
+        in_specs=[pl.BlockSpec(memory_space=pltpu.VMEM)] * len(operands),
+        out_specs=[pl.BlockSpec(memory_space=pltpu.VMEM)] * 11,
+    )(*operands)
 
 
 def swap(values, distance):
@@ -740,31 +876,33 @@
     turn = lambda values: jnp.transpose(values, (0, 2, 1))
     qkv_own = turn(base_qkv)
     qkv_far = swap(qkv_own, 2)
+    lanes = L if side_weights.shape[0] % L == 0 else DS
+    flat = lambda values: values.reshape(-1, lanes)
+    low_rows = flat(side_weights.astype(jnp.bfloat16))
+    low_rows = jnp.broadcast_to(low_rows[None], (devices,) + low_rows.shape)
+    w_rows = exchange(low_rows)
     qkv_mate = swap(qkv_own, 1)
-    low_rows = side_weights.astype(jnp.bfloat16).reshape(1, shard_rows, DS)
-    w_rows = exchange(jnp.broadcast_to(low_rows, (devices, shard_rows, DS)))
 
     onehot = jnp.asarray(diagonal_onehot(buckets))
-    base_diag = jnp.dot(base_table.T, onehot, precision=PRECISE)
-    side_diag = jnp.dot(side_table.T, onehot, precision=PRECISE)
-
     ctx_near = near_part(
-        meta, lengths, tokens, base_gains, qkv_own, qkv_mate, base_diag, own_seqs, 8
+        meta, lengths, tokens, base_gains, qkv_own, qkv_mate, base_table.T, onehot, own_seqs, 8
     )
     ctx_near, qkv_far, w_rows = lax.optimization_barrier((ctx_near, qkv_far, w_rows))
+    qkv_far_mate = swap(qkv_far, 1)
     side_output, input_grad, outgoing = main_part(
         meta,
         lengths,
         tokens,
         base_gains,
         qkv_far,
-        swap(qkv_far, 1),
-        base_diag,
+        qkv_far_mate,
+        base_table.T,
         ctx_near,
         turn(side_input),
         turn(output_grad),
         side_gains,
-        side_diag,
+        side_table.T,
+        onehot,
         jnp.asarray(gradient_onehot(buckets)),
         base_out,
         base_up,
@@ -775,47 +913,41 @@
         1024,
     )
 
-    summed = jnp.sum(exchange(outgoing).astype(jnp.float32), axis=0)
-    grad_shard = lax.optimization_barrier(summed[:shard_rows, :DS].reshape(-1))
-    small_total = summed[shard_rows : shard_rows + SH]
-    gains_total = small_total[0:3, :DS]
-    table_total = small_total[:, DS : DS + buckets].T
-    square = jnp.sum(grad_shard * grad_shard)
-    squares = exchange(jnp.broadcast_to(square, (devices, L)))
-    grad_norm = jnp.sqrt(
-        jnp.sum(squares[:, 0])
-        + jnp.sum(gains_total * gains_total)
-        + jnp.sum(table_total * table_total)
-    )
-    factor = CLIP_NORM / jnp.maximum(grad_norm, CLIP_NORM)
-    weights_moment, weights_square, weights_new = adamw_update(
-        side_weights,
-        weights_first,
-        weights_second,
-        factor * grad_shard,
-        RATE_MATRIX,
-        WEIGHT_DECAY,
-    )
-    gains_moment, gains_square, gains_new = adamw_update(
-        side_gains, gains_first, gains_second, factor * gains_total, RATE_SMALL, 0.0
-    )
-    table_moment, table_square, table_new = adamw_update(
-        side_table, table_first, table_second, factor * table_total, RATE_SMALL, 0.0
-    )
-    return (
-        turn(side_output),
-        turn(input_grad),
+    grad_shard, small, squares = collect_part(exchange(outgoing), shard_rows)
+    (
         grad_norm,
         weights_moment,
         weights_square,
         weights_new,
-        weights_new.astype(jnp.bfloat16),
+        weights_copy,
         gains_moment,
         gains_square,
         gains_new,
         table_moment,
         table_square,
         table_new,
+    ) = update_part(
+        exchange(squares),
+        small,
+        flat(grad_shard),
+        [flat(side_weights), flat(weights_first), flat(weights_second)],
+        [side_gains, gains_first, gains_second],
+        [side_table.T, table_first.T, table_second.T],
+    )
+    return (
+        turn(side_output),
+        turn(input_grad),
+        grad_norm.reshape(()),
+        weights_moment.reshape(-1),
+        weights_square.reshape(-1),
+        weights_new.reshape(-1),
+        weights_copy.reshape(-1),
+        gains_moment,
+        gains_square,
+        gains_new,
+        table_moment.T,
+        table_square.T,
+        table_new.T,
     )
 
 

time: 164 us -> 157 us (0.957)
  other arithmetic: 5.86 us -> 1.33 us
  between operations: 3.98 us -> 0.83 us
  Pallas kernels: 104 us -> 106 us
    pallas_call x0 -> x2, Pallas kernels: none -> 3.68 us  [the longest x1 1.84 us: collect_part(): pl.pallas_call(functools.partial(collect_kernel, shard_rows), name='colle...]
    reduce_sum x5 -> x0, other arithmetic: 2.58 us -> none  [the longest x1 0.68 us: on_device(): jnp.sum(table_total * table_total)]
    pallas_call x1, Pallas kernels: 88.9 us -> 87.2 us  [main_part(): pl.pallas_call(functools.partial(main_kernel, seqs, chunk), name='main',...]
where the time goes in v4:
time: 157 us; the launch traced here: 156 us
  Pallas kernels  106 us (68%)
  blocking collectives  21.5 us (14%)
  starting transfers between devices  11.3 us (7%)
  waiting for transfers between devices  10.1 us (6%)
  local copies, waits for them, and re-layouts  5.81 us (4%)
    pallas_call x1, Pallas kernels, main_part(): pl.pallas_call(functools.partial(main_kernel, seqs, chunk), name='main',...  87.2 us
    all_to_all x1, blocking collectives, exchange(): lax.all_to_all(values, ('batch', 'mp'), split_axis=0, concat_axis=0, tile...  21.5 us
    pallas_call x1, Pallas kernels, near_part(): pl.pallas_call(functools.partial(near_kernel, seqs), name='near', grid_sp...  14.7 us
    all_to_all x2, waiting for transfers between devices, exchange(): lax.all_to_all(values, ('batch', 'mp'), split_axis=0, concat_axis=0, tile...  8.83 us
    all_to_all x2, starting transfers between devices, exchange(): lax.all_to_all(values, ('batch', 'mp'), split_axis=0, concat_axis=0, tile...  8.22 us
  transfers between devices with their start and end apart: 5, of which 3 were waited for; matrix products, arithmetic and copies ran while one was open for 3% of the time, Pallas kernels for 9%

profile of v4, /device:TPU:0, one launch (start us, length us, event | category | flops | bytes accessed | tf_op | source)
XLA Modules:
  0.0 156.4 jit_solution(16113159446229824265)
XLA Ops:
  0.6 0.5 collective-permute-start
  1.2 2.6 %collective-permute-start.1 = (bf16[3,192,768]{2,1,0:T(8,128)(2,1)}, bf16[3,192,768]{2,1,0:T(8,128)(2,1)S(1)}, u32[]{:S(2)}, u32[]{:S(2)}) collective-permute-start(bf16[3,192,768]{2,1,0:T(8,128)(2,1)} %bitcast.30), channel_id=1, source_target_pairs={{0,2},{1,3},{2,0},{3,1},{4,6},{5,7},{6,4},{7,5},{8,10},{9,11},{10,... | collective-permute-start | bytes 2654216 | tf_op jit(solution)/shard_map/ppermute | solution.py:841
  3.7 0.7 convert_bitcast_fusion
  4.5 0.8 broadcast_in_dim.8
  5.3 4.9 %all-to-all-start = ((bf16[32,45,128]{2,1,0:T(8,128)(2,1)}), bf16[32,45,128]{2,1,0:T(8,128)(2,1)S(1)}, u32[]{:S(2)}, u32[]{:S(2)}) async-start(bf16[32,45,128]{2,1,0:T(8,128)(2,1)} %broadcast_in_dim.8), calls=%async_computation | async-start | bytes 786432 | tf_op jit(solution)/shard_map/all_to_all | solution.py:845
  10.2 0.6 pad_add_fusion.meta_ref
  10.8 0.0 collective-permute-done.mate_ref
  10.8 0.0 copy-start
  10.8 0.9 copy-done
  11.7 14.7 %near.1.near_ref = bf16[384,3072]{1,0:T(8,128)(2,1)} custom-call(s32[3]{0:T(128)} %pad_add_fusion.meta_ref, s32[96]{0:T(128)} %len_ref.3, bf16[96,128,768]{2,1,0:T(8,128)(2,1)} %tok_ref.3, f32[2,768]{1,0:T(2,128)} %gain_ref.3, bf16[3,192,768]{2,1,0:T(8,128)(2,1)} %bitcast.31, bf16[3,192,768]{2,1,0:T(8,128)(2,1)} %copy-done, f32[12,32]{1,0:T(8,128)} %bitcast.37, ...), custom_call_target="tpu_custom_call" | custom-call | flops 6039797760 | bytes 8847360 | tf_op jit(solution)/shard_map/near/pallas_call | solution.py:195
  26.4 3.2 %all-to-all-done = bf16[32,45,128]{2,1,0:T(8,128)(2,1)S(1)} async-done(((bf16[32,45,128]{2,1,0:T(8,128)(2,1)}), bf16[32,45,128]{2,1,0:T(8,128)(2,1)S(1)}, u32[]{:S(2)}, u32[]{:S(2)}) %all-to-all-start) | async-done | bytes 368672 | tf_op jit(solution)/shard_map/all_to_all | solution.py:845
  29.6 0.0 collective-permute-done.1.far_ref
  29.6 0.0 copy-start.2
  29.6 0.0 collective-permute-start.2
  29.6 1.1 reshape.59.w_hbm
  30.7 1.3 collective-permute-done.2.mate_ref
  32.0 0.0 copy-start.3
  32.0 0.0 copy-done.2
  32.1 0.9 copy-done.3
  33.0 87.2 %main.1 = (f32[24,96,128]{2,1,0:T(8,128)}, f32[24,96,128]{2,1,0:T(8,128)}, bf16[32,72,128]{2,1,0:T(8,128)(2,1)}) custom-call(s32[3]{0:T(128)} %pad_add_fusion.meta_ref, s32[96]{0:T(128)} %len_ref.3, bf16[96,128,768]{2,1,0:T(8,128)(2,1)} %tok_ref.3, f32[2,768]{1,0:T(2,128)} %gain_ref.3, bf16[3,192,768]{2,1,0:T(8,128)(2,1)} %copy-done.2, ...), custom_call_target="tpu_custom_call" | custom-call | flops 45854703616 | bytes 22413312 | tf_op jit(solution)/shard_map/main/pallas_call | solution.py:663
  120.2 21.5 %all_to_all.21.got_ref = bf16[32,72,128]{2,1,0:T(8,128)(2,1)} all-to-all(bf16[32,72,128]{2,1,0:T(8,128)(2,1)} %get-tuple-element.38), channel_id=1, replica_groups=mesh['batch'=8,'mp'=4] {'batch','mp'}, dimensions={0} | all-to-all | bytes 1179648 | tf_op jit(solution)/shard_map/all_to_all | solution.py:845
  141.7 1.8 %collect.1 = (f32[60,96]{1,0:T(8,128)}, f32[12,128]{1,0:T(8,128)}, f32[32,128]{1,0:T(8,128)}) custom-call(bf16[32,72,128]{2,1,0:T(8,128)(2,1)} %all_to_all.21.got_ref), custom_call_target="tpu_custom_call" | custom-call | tf_op jit(solution)/shard_map/collect/pallas_call | solution.py:779
  143.5 3.3 %all-to-all-start.2 = ((f32[32,1,128]{2,1,0:T(1,128)}), f32[32,1,128]{2,1,0:T(1,128)S(1)}, u32[]{:S(2)}, u32[]{:S(2)}) async-start(f32[32,1,128]{2,1,0:T(1,128)} %bitcast.36), calls=%async_computation.2 | async-start | bytes 32768 | tf_op jit(solution)/shard_map/all_to_all | solution.py:845
  146.8 1.4 reshape.60.shard_ref
  148.3 5.6 %all-to-all-done.2 = f32[32,1,128]{2,1,0:T(1,128)S(1)} async-done(((f32[32,1,128]{2,1,0:T(1,128)}), f32[32,1,128]{2,1,0:T(1,128)S(1)}, u32[]{:S(2)}, u32[]{:S(2)}) %all-to-all-start.2) | async-done | bytes 16416 | tf_op jit(solution)/shard_map/all_to_all | solution.py:845
  153.9 0.0 copy-start.1
  153.9 0.6 copy-done.1
  154.5 1.8 %update.1 = (f32[1,1]{1,0:T(1,128)}, f32[45,128]{1,0:T(8,128)}, f32[45,128]{1,0:T(8,128)}, f32[45,128]{1,0:T(8,128)}, bf16[45,128]{1,0:T(8,128)(2,1)}, /*index=5...) custom-call(f32[32,128]{1,0:T(8,128)} %bitcast.33, ...), custom_call_target="tpu_custom_call" | custom-call | tf_op jit(solution)/shard_map/update/pallas_call | solution.py:824
Async XLA Ops:
  0.6 10.2 %collective-permute-start = (bf16[3,192,768]{2,1,0:T(8,128)(2,1)}, bf16[3,192,768]{2,1,0:T(8,128)(2,1)S(1)}, u32[]{:S(2)}, u32[]{:S(2)}) collective-permute-start(bf16[3,192,768]{2,1,0:T(8,128)(2,1)} %bitcast.29), channel_id=1, source_target_pairs={{0,1},{1,0},{2,3},{3,2},{4,5},{5,4},{6,7},{7,6},{8,9},{9,8},{10,11... | collective-permute-start | bytes 2654216 | tf_op jit(solution)/shard_map/ppermute | solution.py:841
  1.2 28.5 %collective-permute-start.1 = (bf16[3,192,768]{2,1,0:T(8,128)(2,1)}, bf16[3,192,768]{2,1,0:T(8,128)(2,1)S(1)}, u32[]{:S(2)}, u32[]{:S(2)}) collective-permute-start(bf16[3,192,768]{2,1,0:T(8,128)(2,1)} %bitcast.30), channel_id=1, source_target_pairs={{0,2},{1,3},{2,0},{3,1},{4,6},{5,7},{6,4},{7,5},{8,10},{9,11},{10,... | collective-permute-start | bytes 2654216 | tf_op jit(solution)/shard_map/ppermute | solution.py:841
  5.3 24.3 %all-to-all-start = ((bf16[32,45,128]{2,1,0:T(8,128)(2,1)}), bf16[32,45,128]{2,1,0:T(8,128)(2,1)S(1)}, u32[]{:S(2)}, u32[]{:S(2)}) async-start(bf16[32,45,128]{2,1,0:T(8,128)(2,1)} %broadcast_in_dim.8), calls=%async_computation | async-start | bytes 786432 | tf_op jit(solution)/shard_map/all_to_all | solution.py:845
  10.8 0.9 copy-start
  29.6 2.4 %copy-start.2 = (bf16[3,192,768]{2,1,0:T(8,128)(2,1)}, bf16[3,192,768]{2,1,0:T(8,128)(2,1)S(1)}, u32[]{:S(2)}) copy-start(bf16[3,192,768]{2,1,0:T(8,128)(2,1)S(1)} %collective-permute-done.1.far_ref) | copy-start | bytes 2654212
  29.6 2.4 %collective-permute-start.2 = (bf16[3,192,768]{2,1,0:T(8,128)(2,1)S(1)}, bf16[3,192,768]{2,1,0:T(8,128)(2,1)S(1)}, u32[]{:S(2)}, u32[]{:S(2)}) collective-permute-start(bf16[3,192,768]{2,1,0:T(8,128)(2,1)S(1)} %collective-permute-done.1.far_ref), channel_id=1, source_target_pairs={{0,1},{1,0},{2,3},{3,2},{4,5},{5,4},{6,7},{7,6},{8,9},{9,8},{10,11... | collective-permute-start | bytes 2654216 | tf_op jit(solution)/shard_map/ppermute | solution.py:841
  32.0 0.9 copy-start.3
  143.5 10.4 %all-to-all-start.2 = ((f32[32,1,128]{2,1,0:T(1,128)}), f32[32,1,128]{2,1,0:T(1,128)S(1)}, u32[]{:S(2)}, u32[]{:S(2)}) async-start(f32[32,1,128]{2,1,0:T(1,128)} %bitcast.36), calls=%async_computation.2 | async-start | bytes 32768 | tf_op jit(solution)/shard_map/all_to_all | solution.py:845
  153.9 0.6 copy-start.1

commit v5 on v4

--- a/solution.py
+++ b/solution.py
@@ -19,6 +19,8 @@
 ADAM_STEP = 10
 PAIR = 2 * HD
 SPAN = 2 * L
+NARROW = L - DS
+SMALL_ROWS = SH + 9
 
 NORM_EPS = 1e-06
 CLIP_NORM = 1.0
@@ -123,11 +125,20 @@
         )
 
 
-def attention_block(lengths, rows, gain, w_scr, bias_scr, ctx_ref):
+def together(*steps):
+    waiting = list(steps)
+    while waiting:
+        for stage in list(waiting):
+            if next(stage, StopIteration) is StopIteration:
+                waiting.remove(stage)
+
+
+def attention_steps(lengths, rows, gain, w_scr, bias_scr, ctx_ref, base):
     width = w_scr.shape[0] // 3
     normed = (rows * rms_scale(rows) * gain).astype(jnp.bfloat16)
     turned = mm(w_scr[...], normed, NT).astype(jnp.bfloat16)
     query, key, value = turned[0:width], turned[width : 2 * width], turned[2 * width :]
+    yield
     low_lane = lax.broadcasted_iota(jnp.int32, (L, PAIR), 1) < HD
     low_row = lax.broadcasted_iota(jnp.int32, (PAIR, L), 0) < HD
     key_row = lax.broadcasted_iota(jnp.int32, (2, L, L), 1)
@@ -150,7 +161,9 @@
             scale = 1.0 / jnp.sum(shifted, axis=1, keepdims=True)
             scale = jnp.broadcast_to(scale, (2, HD, L)).reshape(PAIR, L)
             probs = shifted.astype(jnp.bfloat16).reshape(2 * L, L)
-            ctx_ref[head, at] = (mm(v_two, probs) * scale).astype(jnp.bfloat16)
+            into = slice(base + s * L, base + (s + 1) * L)
+            ctx_ref[head, into] = (mm(v_two, probs) * scale).astype(jnp.bfloat16)
+        yield
 
 
 def near_kernel(
@@ -186,7 +199,7 @@
 
     lengths = [len_ref[meta_ref[0] + step * seqs + s] for s in range(seqs)]
     rows = tok_ref[...].reshape(seqs * L, D).astype(jnp.float32)
-    attention_block(lengths, rows, gain_ref[0:1, :], w_scr, bias_scr, ctx_ref)
+    together(attention_steps(lengths, rows, gain_ref[0:1, :], w_scr, bias_scr, ctx_ref, 0))
 
 
 def near_part(meta, lengths, tokens, gains, own, mate, table, onehot, own_seqs, seqs):
@@ -225,23 +238,18 @@
     )(meta, lengths, tokens, gains, own, mate, table, onehot)
 
 
-def feed_block(chunk, rows, near, far, gain, wo_scr, up_scr, down_scr, taps_scr):
+def feed_steps(chunk, rows, near, far, gain, wo_scr, up_scr, down_scr, taps_scr, at):
     width = near.shape[0]
-    size = rows.shape[0] // 2
-    halves = [slice(0, size), slice(size, 2 * size)]
-    middle = [
-        rows[at]
-        + mm(near[:, at], wo_scr[0:width, :], TN)
-        + mm(far[:, at], wo_scr[width:, :], TN)
-        for at in halves
-    ]
-    normed = [(part * rms_scale(part) * gain).astype(jnp.bfloat16) for part in middle]
-    for at, part, unit in zip(halves, middle, normed):
-        total = jnp.zeros_like(part)
-        for c in range(0, up_scr.shape[1], chunk):
-            hidden = gelu(mm(unit, up_scr[:, c : c + chunk])).astype(jnp.bfloat16)
-            total = total + mm(hidden, down_scr[c : c + chunk, :])
-        taps_scr[at, :] = (part + total).astype(jnp.bfloat16)
+    middle = rows + mm(near, wo_scr[0:width, :], TN) + mm(far, wo_scr[width:, :], TN)
+    normed = (middle * rms_scale(middle) * gain).astype(jnp.bfloat16)
+    total = jnp.zeros_like(middle)
+    yield
+    for c in range(0, up_scr.shape[1], chunk):
+        hidden = gelu(mm(normed, up_scr[:, c : c + chunk])).astype(jnp.bfloat16)
+        yield
+        total = total + mm(hidden, down_scr[c : c + chunk, :])
+        yield
+    taps_scr[at, :] = (middle + total).astype(jnp.bfloat16)
 
 
 def pick_rows(step, phase, count):
@@ -344,7 +352,7 @@
         ref[...] = jnp.zeros_like(ref)
 
 
-def side_block(lengths, taps_scr, x_ref, go_ref, w_ref, out_ref, ig_ref, scratch):
+def side_steps(lengths, base, taps, x_ref, go_ref, w_ref, out_ref, ig_ref, scratch):
     (
         gain_scr,
         wdown_scr,
@@ -371,10 +379,9 @@
     w_back = w_ref[AT_BACK : AT_END, :]
     key_row = lax.broadcasted_iota(jnp.int32, (SH, L, L), 1)
     token = lax.broadcasted_iota(jnp.int32, (DS, L), 1)
-    taps = taps_scr[...]
-    x = jnp.concatenate([x_ref[s] for s in range(seqs)], axis=1)
+    x = jnp.concatenate([x_ref[base + s] for s in range(seqs)], axis=1)
     grad_out = jnp.concatenate(
-        [jnp.where(token < lengths[s], go_ref[s], 0.0) for s in range(seqs)], axis=1
+        [jnp.where(token < lengths[s], go_ref[base + s], 0.0) for s in range(seqs)], axis=1
     )
 
     tapped = mm(wdown_scr[...], taps, NT)
@@ -386,6 +393,7 @@
 
     query, key, value = qkv[0:L], qkv[L : 2 * L], qkv[2 * L :]
     context, inverse = [], []
+    yield
     for s in range(0, seqs, 2):
         score_two = mm(two_by_head(key, s), two_apart(query, s))
         for side in range(2):
@@ -394,10 +402,11 @@
             scores = jnp.where(key_row < lengths[s + side], scores.reshape(SH, L, L), MASKED)
             shifted = jnp.exp(scores - jnp.max(scores, axis=1, keepdims=True))
             e_low = low(shifted).reshape(SH * L, L)
-            elow_scr[s + side] = e_low
+            elow_scr[base + s + side] = e_low
             total = 1.0 / jnp.sum(shifted, axis=1, keepdims=True)
             inverse.append(jnp.broadcast_to(total, (SH, SHD, L)).reshape(DS, L))
             context.append(mm(by_head_lanes(value[0:DS, at]), e_low) * inverse[-1])
+        yield
     context = jnp.concatenate(context, axis=1)
     inverse = jnp.concatenate(inverse, axis=1)
     context_low = low(context)
@@ -413,6 +422,7 @@
     hidden = low(pre * half)
     slope = half + (0.5 * GELU_RATE) * pre * (1.0 - bend * bend) * (1.0 + 3.0 * GELU_CUBE * square)
     side_out = middle + mm(wback_turn_scr[...], hidden)
+    yield
 
     grad_low = low(grad_out)
     gback_scr[...] += mm(hidden, grad_low, NT)
@@ -430,12 +440,13 @@
 
     grad_context = jnp.concatenate([grad_context, pad], axis=0)
     grad_query, grad_key, grad_value = [], [], []
+    yield
     for s in range(0, seqs, 2):
         prob_two = mm(two_by_head(value, s), two_apart(grad_context, s))
         for side in range(2):
             at = slice((s + side) * L, (s + side + 1) * L)
             grad_probs = prob_two[:, side * L : (side + 1) * L].reshape(SH, L, L)
-            grad_scores = elow_scr[s + side].astype(jnp.float32).reshape(SH, L, L) * (
+            grad_scores = elow_scr[base + s + side].astype(jnp.float32).reshape(SH, L, L) * (
                 grad_probs - dots[:, :, at]
             )
             gbias_scr[...] += grad_scores.reshape(SH * L, L)
@@ -443,8 +454,9 @@
             grad_query.append(low(mm(by_head_lanes(key[0:DS, at]), grad_scores)))
             grad_key.append(low(mm(lanes_of(grad_scores), by_head_rows(query[0:DS, at].T))))
             grad_value.append(
-                low(mm(lanes_of(elow_scr[s + side]), by_head_rows(grad_context[0:DS, at].T)))
+                low(mm(lanes_of(elow_scr[base + s + side]), by_head_rows(grad_context[0:DS, at].T)))
             )
+        yield
     grad_query = jnp.concatenate(grad_query, axis=1)
     grad_key = jnp.concatenate(grad_key, axis=0)
     grad_value = jnp.concatenate(grad_value, axis=0)
@@ -462,11 +474,11 @@
     gdown_scr[...] += mm(grad_tap, taps)
     ggain_scr[2] += fold_lanes(grad_mixed * (x - tapped))
     for s in range(seqs):
-        out_ref[s] = side_out[:, s * L : (s + 1) * L]
-        ig_ref[s] = input_grad[:, s * L : (s + 1) * L]
-
-
-def side_finish(onehot_ref, send_ref, grow_scr, scratch):
+        out_ref[base + s] = side_out[:, s * L : (s + 1) * L]
+        ig_ref[base + s] = input_grad[:, s * L : (s + 1) * L]
+
+
+def side_finish(parity, onehot_ref, mine_ref, other_ref, grow_scr, scratch):
     (
         gain_scr,
         wdown_scr,
@@ -514,28 +526,36 @@
         rolled = pltpu.roll(full, 0, 1, stride=1, stride_axis=0)
         diagonals.append(jnp.sum(rolled, axis=0, keepdims=True))
     diagonals = jnp.concatenate(diagonals, axis=0)
-    shard_rows = AT_END // send_ref.shape[0]
-    small = shard_rows + SH
-    for device in range(send_ref.shape[0]):
-        send_ref[device, 0:shard_rows, :] = grow_scr[
-            device * shard_rows : (device + 1) * shard_rows, :
-        ]
     gains = []
     for row in range(3):
         total = ggain_scr[row]
         if row == 2:
             total = total * (gain_scr[2] * (1.0 - gain_scr[2]))
-        gains.append(jnp.sum(total.T, axis=0, keepdims=True))
-    gains.append(jnp.zeros((SH - 3, DS), jnp.float32))
+        total = jnp.sum(total.T, axis=0, keepdims=True)
+        gains += [total[:, part * NARROW : (part + 1) * NARROW] for part in range(3)]
     table = lax.dot_general(
         diagonals, onehot_ref[...], NT, precision=PRECISE, preferred_element_type=jnp.float32
     )
-    extra = low(jnp.concatenate([jnp.concatenate(gains, axis=0), table], axis=1))
-    blank = jnp.zeros((send_ref.shape[1] - small, L), jnp.bfloat16)
-    for device in range(send_ref.shape[0]):
-        send_ref[device, shard_rows:small, :] = extra
-        if small < send_ref.shape[1]:
-            send_ref[device, small:, :] = blank
+    small = low(jnp.concatenate([table] + gains, axis=0))
+    pairs = mine_ref.shape[0]
+    shard_rows = AT_END // (2 * pairs)
+    blank = jnp.zeros((mine_ref.shape[1] - shard_rows, L), jnp.bfloat16)
+
+    def place(even_ref, odd_ref):
+        for device in range(2 * pairs):
+            ref, slot = (even_ref, odd_ref)[device % 2], device // 2
+            ref[slot, 0:shard_rows, :] = grow_scr[device * shard_rows : (device + 1) * shard_rows, :]
+            if blank.shape[0]:
+                ref[slot, shard_rows:, :] = blank
+            ref[slot, 0 : small.shape[0], DS:] = small
+
+    @pl.when(parity == 0)
+    def _():
+        place(mine_ref, other_ref)
+
+    @pl.when(parity == 1)
+    def _():
+        place(other_ref, mine_ref)
 
 
 def main_kernel(
@@ -561,7 +581,8 @@
     w_hbm,
     out_ref,
     ig_ref,
-    send_ref,
+    mine_ref,
+    other_ref,
     diag_scr,
     w_scr,
     bias_scr,
@@ -609,24 +630,63 @@
         )
 
     lengths = [len_ref[meta_ref[0] + step * seqs + s] for s in range(seqs)]
-    rows = tok_ref[...].reshape(seqs * L, D).astype(jnp.float32)
-    attention_block(lengths, rows, gain_ref[0:1, :], w_scr, bias_scr, ctx_scr)
-
+    half = seqs // 2
+    at = [slice(h * half * L, (h + 1) * half * L) for h in range(2)]
+
+    def rows(h):
+        return tok_ref[h * half : (h + 1) * half].reshape(half * L, D).astype(jnp.float32)
+
+    def attend(h):
+        return attention_steps(
+            lengths[h * half : (h + 1) * half],
+            rows(h),
+            gain_ref[0:1, :],
+            w_scr,
+            bias_scr,
+            ctx_scr,
+            h * half * L,
+        )
+
+    def feed(h):
+        return feed_steps(
+            chunk,
+            rows(h),
+            near_ref[:, at[h]],
+            ctx_scr[:, at[h]],
+            gain_ref[1:2, :],
+            wo_scr,
+            up_scr,
+            down_scr,
+            taps_scr,
+            at[h],
+        )
+
+    def side(h):
+        return side_steps(
+            lengths[h * half : (h + 1) * half],
+            h * half,
+            taps_scr[at[h], :],
+            x_ref,
+            go_ref,
+            wrow_scr,
+            out_ref,
+            ig_ref,
+            scratch,
+        )
+
+    together(attend(0), attend(1))
     @pl.when(step == 0)
     def _():
         for copy in copies:
             copy.wait()
         side_setup(side_gain_ref, wrow_scr, side_table_ref, onehot_ref, scratch)
 
-    rows = tok_ref[...].reshape(seqs * L, D).astype(jnp.float32)
-    feed_block(
-        chunk, rows, near_ref[...], ctx_scr[...], gain_ref[1:2, :], wo_scr, up_scr, down_scr, taps_scr
-    )
-    side_block(lengths, taps_scr, x_ref, go_ref, wrow_scr, out_ref, ig_ref, scratch)
+    together(feed(0), feed(1))
+    together(side(0), side(1))
 
     @pl.when(step == pl.num_programs(0) - 1)
     def _():
-        side_finish(turn_onehot_ref, send_ref, grow_scr, scratch)
+        side_finish(meta_ref[1], turn_onehot_ref, mine_ref, other_ref, grow_scr, scratch)
 
 
 def main_part(
@@ -655,7 +715,8 @@
     own_seqs = side_input.shape[0]
     width = ctx_near.shape[0]
     ff = w_up.shape[1]
-    send_rows = -(-(w_rows.shape[0] // devices + SH) // 8) * 8
+    send_rows = -(-max(w_rows.shape[0] // devices, SMALL_ROWS) // 8) * 8
+    send_shape = (devices // 2, send_rows, L)
     fixed = lambda *dims: pl.BlockSpec(dims, lambda i, m, n: (0,) * len(dims))
     block = pl.BlockSpec((seqs, DS, L), lambda i, m, n: (i, 0, 0))
     hbm = pl.BlockSpec(memory_space=pl.ANY)
@@ -684,7 +745,7 @@
                 hbm,
                 hbm,
             ],
-            out_specs=[block, block, fixed(devices, send_rows, L)],
+            out_specs=[block, block, fixed(*send_shape), fixed(*send_shape)],
             scratch_shapes=[
                 pltpu.VMEM((table.shape[0], SPAN), f32),
                 pltpu.VMEM((3 * width, D), bf16),
@@ -719,7 +780,8 @@
         out_shape=[
             jax.ShapeDtypeStruct(side_input.shape, f32),
             jax.ShapeDtypeStruct(side_input.shape, f32),
-            jax.ShapeDtypeStruct((devices, send_rows, L), bf16),
+            jax.ShapeDtypeStruct(send_shape, bf16),
+            jax.ShapeDtypeStruct(send_shape, bf16),
         ],
         compiler_params=pltpu.CompilerParams(
             dimension_semantics=("arbitrary",), vmem_limit_bytes=VMEM_MAIN * MIB
@@ -763,37 +825,41 @@
     return (first_new, second_new, weight_new)
 
 
-def collect_kernel(shard_rows, got_ref, shard_ref, small_ref, square_ref):
+def collect_kernel(got_ref, shard_ref, gains_ref, table_ref, square_ref):
     total = got_ref[0].astype(jnp.float32)
     for device in range(1, got_ref.shape[0]):
         total = total + got_ref[device].astype(jnp.float32)
-    shard = total[0:shard_rows, 0:DS]
+    shard = total[0 : shard_ref.shape[0], 0:DS]
     shard_ref[...] = shard
-    small_ref[...] = total[shard_rows : shard_rows + SH, :]
+    table_ref[...] = total[0:SH, DS:]
+    for row in range(3):
+        for part in range(3):
+            at = SH + 3 * row + part
+            gains_ref[row : row + 1, part * NARROW : (part + 1) * NARROW] = total[at : at + 1, DS:]
     square = jnp.sum(jnp.sum(shard * shard, axis=1, keepdims=True), axis=0, keepdims=True)
     square_ref[...] = jnp.broadcast_to(square, square_ref.shape)
 
 
 def collect_part(got, shard_rows):
-    devices = got.shape[0]
     return pl.pallas_call(
-        functools.partial(collect_kernel, shard_rows),
+        collect_kernel,
         name="collect",
         out_shape=[
             jax.ShapeDtypeStruct((shard_rows, DS), jnp.float32),
-            jax.ShapeDtypeStruct((SH, L), jnp.float32),
-            jax.ShapeDtypeStruct((devices, L), jnp.float32),
+            jax.ShapeDtypeStruct((3, DS), jnp.float32),
+            jax.ShapeDtypeStruct((SH, NARROW), jnp.float32),
+            jax.ShapeDtypeStruct((2 * got.shape[0], L), jnp.float32),
         ],
         in_specs=[pl.BlockSpec(memory_space=pltpu.VMEM)],
-        out_specs=[pl.BlockSpec(memory_space=pltpu.VMEM)] * 3,
+        out_specs=[pl.BlockSpec(memory_space=pltpu.VMEM)] * 4,
     )(got)
 
 
-def update_kernel(square_ref, small_ref, shard_ref, *refs):
+def update_kernel(square_ref, gains_sum_ref, table_sum_ref, shard_ref, *refs):
     weights, gains, table = refs[0:3], refs[3:6], refs[6:9]
     norm_ref, copy_ref = refs[9], refs[13]
-    gains_total = small_ref[0:3, 0:DS]
-    table_total = small_ref[:, DS:]
+    gains_total = gains_sum_ref[...]
+    table_total = table_sum_ref[...]
     whole = lambda values: jnp.sum(
         jnp.sum(values, axis=1, keepdims=True), axis=0, keepdims=True
     )
@@ -817,10 +883,10 @@
     update(table, table_total, refs[17:20], RATE_SMALL, 0.0)
 
 
-def update_part(squares, small, shard, weights, gains, table):
+def update_part(squares, gains_sum, table_sum, shard, weights, gains, table):
     f32 = jnp.float32
     like = lambda values, dtype=f32: jax.ShapeDtypeStruct(values.shape, dtype)
-    operands = (squares, small, shard, *weights, *gains, *table)
+    operands = (squares, gains_sum, table_sum, shard, *weights, *gains, *table)
     return pl.pallas_call(
         update_kernel,
         name="update",
@@ -843,6 +909,18 @@
 
 def exchange(values):
     return lax.all_to_all(values, ("batch", "mp"), split_axis=0, concat_axis=0, tiled=True)
+
+
+def exchange_alike(values):
+    groups = [[2 * i + parity for i in range(values.shape[0])] for parity in range(2)]
+    return lax.all_to_all(
+        values,
+        ("batch", "mp"),
+        split_axis=0,
+        concat_axis=0,
+        axis_index_groups=groups,
+        tiled=True,
+    )
 
 
 def on_device(
@@ -889,7 +967,7 @@
     )
     ctx_near, qkv_far, w_rows = lax.optimization_barrier((ctx_near, qkv_far, w_rows))
     qkv_far_mate = swap(qkv_far, 1)
-    side_output, input_grad, outgoing = main_part(
+    side_output, input_grad, mine, other = main_part(
         meta,
         lengths,
         tokens,
@@ -913,7 +991,10 @@
         1024,
     )
 
-    grad_shard, small, squares = collect_part(exchange(outgoing), shard_rows)
+    paired = mine.astype(jnp.float32) + swap(other, 1).astype(jnp.float32)
+    grad_shard, gains_sum, table_sum, squares = collect_part(
+        exchange_alike(paired.astype(jnp.bfloat16)), shard_rows
+    )
     (
         grad_norm,
         weights_moment,
@@ -928,7 +1009,8 @@
         table_new,
     ) = update_part(
         exchange(squares),
-        small,
+        gains_sum,
+        table_sum,
         flat(grad_shard),
         [flat(side_weights), flat(weights_first), flat(weights_second)],
         [side_gains, gains_first, gains_second],

time: 157 us -> 152 us (0.968)
  blocking collectives: 21.5 us -> 15.8 us
    all_to_all x1, blocking collectives: 21.5 us -> 15.8 us  [exchange_alike(): lax.all_to_all(values, ('batch', 'mp'), split_axis=0, concat_axis=0, axis...]
    ppermute x3 -> x4, starting transfers between devices: 3.09 us -> 3.32 us  [swap(): return lax.ppermute(values, 'mp', [(i, i ^ distance) for i in range(size)])]
  transfers between devices with their start and end apart: 5 -> 6, of which waited for: 3 -> 4; matrix products, arithmetic and copies ran while one was open for 3% -> 3% of each run, Pallas kernels for 9% -> 10%
where the time goes in v5:
time: 152 us
  Pallas kernels  105 us (69%)
  blocking collectives  15.8 us (10%)
  waiting for transfers between devices  11.6 us (8%)
  starting transfers between devices  10.8 us (7%)
  local copies, waits for them, and re-layouts  5.84 us (4%)
  other arithmetic  2.35 us (2%)
    pallas_call x1, Pallas kernels, main_part(): pl.pallas_call(functools.partial(main_kernel, seqs, chunk), name='main',...  86.5 us
    all_to_all x1, blocking collectives, exchange_alike(): lax.all_to_all(values, ('batch', 'mp'), split_axis=0, concat_axis=0, axis...  15.8 us
    pallas_call x1, Pallas kernels, near_part(): pl.pallas_call(functools.partial(near_kernel, seqs), name='near', grid_sp...  14.7 us
    all_to_all x2, waiting for transfers between devices, exchange(): lax.all_to_all(values, ('batch', 'mp'), split_axis=0, concat_axis=0, tile...  8.79 us
    all_to_all x2, starting transfers between devices, exchange(): lax.all_to_all(values, ('batch', 'mp'), split_axis=0, concat_axis=0, tile...  7.47 us
    ppermute x4, starting transfers between devices, swap(): return lax.ppermute(values, 'mp', [(i, i ^ distance) for i in range(size)])  3.32 us
  transfers between devices with their start and end apart: 6, of which 4 were waited for; matrix products, arithmetic and copies ran while one was open for 3% of the time, Pallas kernels for 10%

profile of v5, /device:TPU:0, one launch (start us, length us, event | category | flops | bytes accessed | tf_op | source)
XLA Modules:
  0.0 151.9 jit_solution(14269759354149753480)
XLA Ops:
  0.6 0.5 collective-permute-start
  1.2 2.6 %collective-permute-start.1 = (bf16[3,192,768]{2,1,0:T(8,128)(2,1)}, bf16[3,192,768]{2,1,0:T(8,128)(2,1)S(1)}, u32[]{:S(2)}, u32[]{:S(2)}) collective-permute-start(bf16[3,192,768]{2,1,0:T(8,128)(2,1)} %bitcast.30), channel_id=1, source_target_pairs={{0,2},{1,3},{2,0},{3,1},{4,6},{5,7},{6,4},{7,5},{8,10},{9,11},{10,... | collective-permute-start | bytes 2654216 | tf_op jit(solution)/shard_map/ppermute | solution.py:907
  3.7 0.7 convert_bitcast_fusion
  4.5 0.8 broadcast_in_dim.8
  5.3 4.9 %all-to-all-start = ((bf16[32,45,128]{2,1,0:T(8,128)(2,1)}), bf16[32,45,128]{2,1,0:T(8,128)(2,1)S(1)}, u32[]{:S(2)}, u32[]{:S(2)}) async-start(bf16[32,45,128]{2,1,0:T(8,128)(2,1)} %broadcast_in_dim.8), calls=%async_computation | async-start | bytes 786432 | tf_op jit(solution)/shard_map/all_to_all | solution.py:911
  10.2 0.6 pad_add_fusion.meta_ref
  10.8 0.0 collective-permute-done.mate_ref
  10.8 0.0 copy-start
  10.8 0.9 copy-done
  11.7 14.7 %near.1.near_ref = bf16[384,3072]{1,0:T(8,128)(2,1)} custom-call(s32[3]{0:T(128)} %pad_add_fusion.meta_ref, s32[96]{0:T(128)} %len_ref.3, bf16[96,128,768]{2,1,0:T(8,128)(2,1)} %tok_ref.3, f32[2,768]{1,0:T(2,128)} %gain_ref.3, bf16[3,192,768]{2,1,0:T(8,128)(2,1)} %bitcast.31, bf16[3,192,768]{2,1,0:T(8,128)(2,1)} %copy-done, f32[12,32]{1,0:T(8,128)} %bitcast.37, ...), custom_call_target="tpu_custom_call" | custom-call | flops 6039797760 | bytes 8847360 | tf_op jit(solution)/shard_map/near/pallas_call | solution.py:208
  26.4 3.2 %all-to-all-done = bf16[32,45,128]{2,1,0:T(8,128)(2,1)S(1)} async-done(((bf16[32,45,128]{2,1,0:T(8,128)(2,1)}), bf16[32,45,128]{2,1,0:T(8,128)(2,1)S(1)}, u32[]{:S(2)}, u32[]{:S(2)}) %all-to-all-start) | async-done | bytes 368672 | tf_op jit(solution)/shard_map/all_to_all | solution.py:911
  29.6 0.0 collective-permute-done.1.far_ref
  29.6 0.0 copy-start.2
  29.6 0.0 collective-permute-start.2
  29.6 1.1 reshape.59.w_hbm
  30.8 1.3 collective-permute-done.2.mate_ref
  32.0 0.0 copy-start.3
  32.0 0.0 copy-done.2
  32.1 0.9 copy-done.3
  33.0 86.5 %main.1 = (f32[24,96,128]{2,1,0:T(8,128)}, f32[24,96,128]{2,1,0:T(8,128)}, bf16[16,64,128]{2,1,0:T(8,128)(2,1)}, bf16[16,64,128]{2,1,0:T(8,128)(2,1)}) custom-call(s32[3]{0:T(128)} %pad_add_fusion.meta_ref, s32[96]{0:T(128)} %len_ref.3, bf16[96,128,768]{2,1,0:T(8,128)(2,1)} %tok_ref.3, f32[2,768]{1,0:T(2,128)} %gain_ref.3, bf16[3,192,768]{2,1,0:T(8,128)(2,1)} %copy-done.2, ...), custom_call_target="tpu_custom_call" | custom-call | flops 45854703616 | bytes 22413312 | tf_op jit(solution)/shard_map/main/pallas_call | solution.py:724
  119.5 0.2 collective-permute-start.3
  119.7 1.6 %collective-permute-done.3 = bf16[16,64,128]{2,1,0:T(8,128)(2,1)S(1)} collective-permute-done((bf16[16,64,128]{2,1,0:T(8,128)(2,1)}, bf16[16,64,128]{2,1,0:T(8,128)(2,1)S(1)}, u32[]{:S(2)}, u32[]{:S(2)}) %collective-permute-start.3) | collective-permute-done | bytes 262176 | tf_op jit(solution)/shard_map/ppermute | solution.py:907
  121.3 1.0 add_convert_fusion
  122.3 15.8 %all_to_all.21.got_ref = bf16[16,64,128]{2,1,0:T(8,128)(2,1)} all-to-all(bf16[16,64,128]{2,1,0:T(8,128)(2,1)S(1)} %add_convert_fusion), channel_id=1, replica_groups={{0,2,4,6,8,10,12,14,16,18,20,22,24,26,28,30},{1,3,5,7,9,11,13,15,17,19,..., dimensions={0} | all-to-all | bytes 524288 | tf_op jit(solution)/shard_map/all_to_all | solution.py:916
  138.1 1.7 %collect.1 = (f32[60,96]{1,0:T(8,128)}, f32[3,96]{1,0:T(4,128)}, f32[12,32]{1,0:T(8,128)}, f32[32,128]{1,0:T(8,128)}) custom-call(bf16[16,64,128]{2,1,0:T(8,128)(2,1)} %all_to_all.21.got_ref), custom_call_target="tpu_custom_call" | custom-call | tf_op jit(solution)/shard_map/collect/pallas_call | solution.py:844
  139.8 2.5 %all-to-all-start.2 = ((f32[32,1,128]{2,1,0:T(1,128)}), f32[32,1,128]{2,1,0:T(1,128)S(1)}, u32[]{:S(2)}, u32[]{:S(2)}) async-start(f32[32,1,128]{2,1,0:T(1,128)} %bitcast.36), calls=%async_computation.2 | async-start | bytes 32768 | tf_op jit(solution)/shard_map/all_to_all | solution.py:911
  142.3 1.4 reshape.60.shard_ref
  143.8 5.6 %all-to-all-done.2 = f32[32,1,128]{2,1,0:T(1,128)S(1)} async-done(((f32[32,1,128]{2,1,0:T(1,128)}), f32[32,1,128]{2,1,0:T(1,128)S(1)}, u32[]{:S(2)}, u32[]{:S(2)}) %all-to-all-start.2) | async-done | bytes 16416 | tf_op jit(solution)/shard_map/all_to_all | solution.py:911
  149.4 0.0 copy-start.1
  149.4 0.6 copy-done.1
  150.0 1.7 %update.1 = (f32[1,1]{1,0:T(1,128)}, f32[45,128]{1,0:T(8,128)}, f32[45,128]{1,0:T(8,128)}, f32[45,128]{1,0:T(8,128)}, bf16[45,128]{1,0:T(8,128)(2,1)}, /*index=5...) custom-call(f32[32,128]{1,0:T(8,128)} %bitcast.33, ...), custom_call_target="tpu_custom_call" | custom-call | tf_op jit(solution)/shard_map/update/pallas_call | solution.py:890
Async XLA Ops:
  0.6 10.2 %collective-permute-start = (bf16[3,192,768]{2,1,0:T(8,128)(2,1)}, bf16[3,192,768]{2,1,0:T(8,128)(2,1)S(1)}, u32[]{:S(2)}, u32[]{:S(2)}) collective-permute-start(bf16[3,192,768]{2,1,0:T(8,128)(2,1)} %bitcast.29), channel_id=1, source_target_pairs={{0,1},{1,0},{2,3},{3,2},{4,5},{5,4},{6,7},{7,6},{8,9},{9,8},{10,11... | collective-permute-start | bytes 2654216 | tf_op jit(solution)/shard_map/ppermute | solution.py:907
  1.2 28.5 %collective-permute-start.1 = (bf16[3,192,768]{2,1,0:T(8,128)(2,1)}, bf16[3,192,768]{2,1,0:T(8,128)(2,1)S(1)}, u32[]{:S(2)}, u32[]{:S(2)}) collective-permute-start(bf16[3,192,768]{2,1,0:T(8,128)(2,1)} %bitcast.30), channel_id=1, source_target_pairs={{0,2},{1,3},{2,0},{3,1},{4,6},{5,7},{6,4},{7,5},{8,10},{9,11},{10,... | collective-permute-start | bytes 2654216 | tf_op jit(solution)/shard_map/ppermute | solution.py:907
  5.3 24.3 %all-to-all-start = ((bf16[32,45,128]{2,1,0:T(8,128)(2,1)}), bf16[32,45,128]{2,1,0:T(8,128)(2,1)S(1)}, u32[]{:S(2)}, u32[]{:S(2)}) async-start(bf16[32,45,128]{2,1,0:T(8,128)(2,1)} %broadcast_in_dim.8), calls=%async_computation | async-start | bytes 786432 | tf_op jit(solution)/shard_map/all_to_all | solution.py:911
  10.8 0.9 copy-start
  29.6 2.4 %copy-start.2 = (bf16[3,192,768]{2,1,0:T(8,128)(2,1)}, bf16[3,192,768]{2,1,0:T(8,128)(2,1)S(1)}, u32[]{:S(2)}) copy-start(bf16[3,192,768]{2,1,0:T(8,128)(2,1)S(1)} %collective-permute-done.1.far_ref) | copy-start | bytes 2654212
  29.6 2.4 %collective-permute-start.2 = (bf16[3,192,768]{2,1,0:T(8,128)(2,1)S(1)}, bf16[3,192,768]{2,1,0:T(8,128)(2,1)S(1)}, u32[]{:S(2)}, u32[]{:S(2)}) collective-permute-start(bf16[3,192,768]{2,1,0:T(8,128)(2,1)S(1)} %collective-permute-done.1.far_ref), channel_id=1, source_target_pairs={{0,1},{1,0},{2,3},{3,2},{4,5},{5,4},{6,7},{7,6},{8,9},{9,8},{10,11... | collective-permute-start | bytes 2654216 | tf_op jit(solution)/shard_map/ppermute | solution.py:907
  32.0 0.9 copy-start.3
  119.5 1.8 %collective-permute-start.3 = (bf16[16,64,128]{2,1,0:T(8,128)(2,1)}, bf16[16,64,128]{2,1,0:T(8,128)(2,1)S(1)}, u32[]{:S(2)}, u32[]{:S(2)}) collective-permute-start(bf16[16,64,128]{2,1,0:T(8,128)(2,1)} %get-tuple-element.41), channel_id=1, source_target_pairs={{0,1},{1,0},{2,3},{3,2},{4,5},{5,4},{6,7},{7,6},{8,9},{9,8},{10,11... | collective-permute-start | bytes 786440 | tf_op jit(solution)/shard_map/ppermute | solution.py:907
  139.8 9.6 %all-to-all-start.2 = ((f32[32,1,128]{2,1,0:T(1,128)}), f32[32,1,128]{2,1,0:T(1,128)S(1)}, u32[]{:S(2)}, u32[]{:S(2)}) async-start(f32[32,1,128]{2,1,0:T(1,128)} %bitcast.36), calls=%async_computation.2 | async-start | bytes 32768 | tf_op jit(solution)/shard_map/all_to_all | solution.py:911
  149.4 0.6 copy-start.1

commit v6 on v5

--- a/solution.py
+++ b/solution.py
@@ -133,9 +133,8 @@
                 waiting.remove(stage)
 
 
-def attention_steps(lengths, rows, gain, w_scr, bias_scr, ctx_ref, base):
+def attention_steps(lengths, normed, w_scr, bias_scr, ctx_ref, base):
     width = w_scr.shape[0] // 3
-    normed = (rows * rms_scale(rows) * gain).astype(jnp.bfloat16)
     turned = mm(w_scr[...], normed, NT).astype(jnp.bfloat16)
     query, key, value = turned[0:width], turned[width : 2 * width], turned[2 * width :]
     yield
@@ -176,7 +175,10 @@
     mate_ref,
     table_ref,
     onehot_ref,
-    ctx_ref,
+    wo_ref,
+    normed_ref,
+    partial_ref,
+    ctx_scr,
     diag_scr,
     w_scr,
     bias_scr,
@@ -199,10 +201,13 @@
 
     lengths = [len_ref[meta_ref[0] + step * seqs + s] for s in range(seqs)]
     rows = tok_ref[...].reshape(seqs * L, D).astype(jnp.float32)
-    together(attention_steps(lengths, rows, gain_ref[0:1, :], w_scr, bias_scr, ctx_ref, 0))
-
-
-def near_part(meta, lengths, tokens, gains, own, mate, table, onehot, own_seqs, seqs):
+    normed = (rows * rms_scale(rows) * gain_ref[0:1, :]).astype(jnp.bfloat16)
+    normed_ref[...] = normed
+    together(attention_steps(lengths, normed, w_scr, bias_scr, ctx_scr, 0))
+    partial_ref[...] = (rows + mm(ctx_scr[...], wo_ref[...], TN)).astype(jnp.bfloat16)
+
+
+def near_part(meta, lengths, tokens, gains, own, mate, table, onehot, w_out, own_seqs, seqs):
     width = 2 * own.shape[1]
     fixed = lambda *dims: pl.BlockSpec(dims, lambda i, m, n: (0,) * len(dims))
     return pl.pallas_call(
@@ -218,29 +223,30 @@
                 fixed(*mate.shape),
                 fixed(*table.shape),
                 fixed(*onehot.shape),
+                pl.BlockSpec((width, D), lambda i, m, n: (m[2], 0)),
             ],
-            out_specs=pl.BlockSpec((width, seqs * L), lambda i, m, n: (0, i)),
+            out_specs=[pl.BlockSpec((seqs * L, D), lambda i, m, n: (i, 0))] * 2,
             scratch_shapes=[
+                pltpu.VMEM((width, seqs * L), jnp.bfloat16),
                 pltpu.VMEM((table.shape[0], SPAN), jnp.float32),
                 pltpu.VMEM((3 * width, D), jnp.bfloat16),
                 pltpu.VMEM((width // HD * L, L), jnp.float32),
             ],
         ),
-        out_shape=jax.ShapeDtypeStruct((width, own_seqs * L), jnp.bfloat16),
+        out_shape=[jax.ShapeDtypeStruct((own_seqs * L, D), jnp.bfloat16)] * 2,
         compiler_params=pltpu.CompilerParams(
             dimension_semantics=("arbitrary",), vmem_limit_bytes=56 * MIB
         ),
         cost_estimate=pl.CostEstimate(
-            flops=2 * own_seqs * L * width * (3 * D + 2 * L),
-            bytes_accessed=own_seqs * L * (D + width) * 2 + 6 * D * width,
+            flops=2 * own_seqs * L * width * (4 * D + 2 * L),
+            bytes_accessed=own_seqs * L * 3 * D * 2 + 6 * D * width,
             transcendentals=own_seqs * width // HD * L * L,
         ),
-    )(meta, lengths, tokens, gains, own, mate, table, onehot)
-
-
-def feed_steps(chunk, rows, near, far, gain, wo_scr, up_scr, down_scr, taps_scr, at):
-    width = near.shape[0]
-    middle = rows + mm(near, wo_scr[0:width, :], TN) + mm(far, wo_scr[width:, :], TN)
+    )(meta, lengths, tokens, gains, own, mate, table, onehot, w_out)
+
+
+def feed_steps(chunk, rows, far, gain, wo_scr, up_scr, down_scr, taps_scr, at):
+    middle = rows + mm(far, wo_scr[...], TN)
     normed = (middle * rms_scale(middle) * gain).astype(jnp.bfloat16)
     total = jnp.zeros_like(middle)
     yield
@@ -512,16 +518,14 @@
     grow_scr[AT_BACK : AT_END, 0:DS] = low(gback_scr[...])
     flip_row = lax.broadcasted_iota(jnp.int32, (L, L), 0)
     flip_column = lax.broadcasted_iota(jnp.int32, (L, L), 1)
-    flip = (flip_row + flip_column == L - 1).astype(jnp.float32)
+    flip = low((flip_row + flip_column == L - 1).astype(jnp.float32))
+    squares = lanes_of(gbias_scr[...])
+    upper = low(squares)
+    flipped = mm(flip, upper)
+    flipped = flipped + mm(flip, low(squares - upper.astype(jnp.float32)))
     diagonals = []
     for head in range(SH):
-        square = lax.dot_general(
-            flip,
-            gbias_scr[head * L : (head + 1) * L, :],
-            NN,
-            precision=PRECISE,
-            preferred_element_type=jnp.float32,
-        )
+        square = flipped[:, head * L : (head + 1) * L]
         full = jnp.concatenate([square, jnp.zeros_like(square)], axis=1)
         rolled = pltpu.roll(full, 0, 1, stride=1, stride_axis=0)
         diagonals.append(jnp.sum(rolled, axis=0, keepdims=True))
@@ -563,12 +567,12 @@
     chunk,
     meta_ref,
     len_ref,
-    tok_ref,
+    normed_ref,
+    partial_ref,
     gain_ref,
     far_ref,
     mate_ref,
     table_ref,
-    near_ref,
     x_ref,
     go_ref,
     side_gain_ref,
@@ -598,19 +602,12 @@
 ):
     step = pl.program_id(0)
     group = meta_ref[2]
-    width = near_ref.shape[0]
+    width = wo_scr.shape[0]
     copies = [
-        pltpu.make_async_copy(
-            wo_hbm.at[pl.ds(group * width, width), :], wo_scr.at[pl.ds(0, width), :], sems.at[0]
-        ),
-        pltpu.make_async_copy(
-            wo_hbm.at[pl.ds((1 - group) * width, width), :],
-            wo_scr.at[pl.ds(width, width), :],
-            sems.at[1],
-        ),
-        pltpu.make_async_copy(up_hbm, up_scr, sems.at[2]),
-        pltpu.make_async_copy(down_hbm, down_scr, sems.at[3]),
-        pltpu.make_async_copy(w_hbm, wrow_scr, sems.at[4]),
+        pltpu.make_async_copy(wo_hbm.at[pl.ds((1 - group) * width, width), :], wo_scr, sems.at[0]),
+        pltpu.make_async_copy(up_hbm, up_scr, sems.at[1]),
+        pltpu.make_async_copy(down_hbm, down_scr, sems.at[2]),
+        pltpu.make_async_copy(w_hbm, wrow_scr, sems.at[3]),
     ]
 
     @pl.when(step == 0)
@@ -633,32 +630,29 @@
     half = seqs // 2
     at = [slice(h * half * L, (h + 1) * half * L) for h in range(2)]
 
-    def rows(h):
-        return tok_ref[h * half : (h + 1) * half].reshape(half * L, D).astype(jnp.float32)
-
     def attend(h):
         return attention_steps(
             lengths[h * half : (h + 1) * half],
-            rows(h),
-            gain_ref[0:1, :],
+            normed_ref[at[h], :],
             w_scr,
             bias_scr,
             ctx_scr,
             h * half * L,
         )
 
-    def feed(h):
+    def feed(part):
+        size = seqs * L // 4
+        at = slice(part * size, (part + 1) * size)
         return feed_steps(
             chunk,
-            rows(h),
-            near_ref[:, at[h]],
-            ctx_scr[:, at[h]],
+            partial_ref[at, :].astype(jnp.float32),
+            ctx_scr[:, at],
             gain_ref[1:2, :],
             wo_scr,
             up_scr,
             down_scr,
             taps_scr,
-            at[h],
+            at,
         )
 
     def side(h):
@@ -681,7 +675,7 @@
             copy.wait()
         side_setup(side_gain_ref, wrow_scr, side_table_ref, onehot_ref, scratch)
 
-    together(feed(0), feed(1))
+    together(*[feed(part) for part in range(4)])
     together(side(0), side(1))
 
     @pl.when(step == pl.num_programs(0) - 1)
@@ -692,12 +686,12 @@
 def main_part(
     meta,
     lengths,
-    tokens,
+    normed,
+    partial,
     gains,
     far,
     mate,
     table,
-    ctx_near,
     side_input,
     output_grad,
     side_gains,
@@ -713,7 +707,7 @@
     chunk,
 ):
     own_seqs = side_input.shape[0]
-    width = ctx_near.shape[0]
+    width = w_out.shape[0] // 2
     ff = w_up.shape[1]
     send_rows = -(-max(w_rows.shape[0] // devices, SMALL_ROWS) // 8) * 8
     send_shape = (devices // 2, send_rows, L)
@@ -728,12 +722,12 @@
             num_scalar_prefetch=2,
             grid=(own_seqs // seqs,),
             in_specs=[
-                pl.BlockSpec((seqs, L, D), lambda i, m, n: (m[0] // seqs + i, 0, 0)),
+                pl.BlockSpec((seqs * L, D), lambda i, m, n: (i, 0)),
+                pl.BlockSpec((seqs * L, D), lambda i, m, n: (i, 0)),
                 fixed(2, D),
                 fixed(*far.shape),
                 fixed(*mate.shape),
                 fixed(*table.shape),
-                pl.BlockSpec((width, seqs * L), lambda i, m, n: (0, i)),
                 block,
                 block,
                 fixed(*side_gains.shape),
@@ -752,12 +746,12 @@
                 pltpu.VMEM((width // HD * L, L), f32),
                 pltpu.VMEM((width, seqs * L), bf16),
                 pltpu.VMEM((seqs * L, D), bf16),
-                pltpu.VMEM(w_out.shape, bf16),
+                pltpu.VMEM((width, D), bf16),
                 pltpu.VMEM(w_up.shape, bf16),
                 pltpu.VMEM(w_down.shape, bf16),
                 pltpu.VMEM(w_rows.shape, bf16),
                 pltpu.VMEM((w_rows.shape[0], L), bf16),
-                pltpu.SemaphoreType.DMA((5,)),
+                pltpu.SemaphoreType.DMA((4,)),
                 pltpu.VMEM((3, DS, L), f32),
                 pltpu.VMEM((DS, D), bf16),
                 pltpu.VMEM((3, DS, DS), bf16),
@@ -795,12 +789,12 @@
     )(
         meta,
         lengths,
-        tokens,
+        normed,
+        partial,
         gains,
         far,
         mate,
         table,
-        ctx_near,
         side_input,
         output_grad,
         side_gains,
@@ -962,20 +956,30 @@
     qkv_mate = swap(qkv_own, 1)
 
     onehot = jnp.asarray(diagonal_onehot(buckets))
-    ctx_near = near_part(
-        meta, lengths, tokens, base_gains, qkv_own, qkv_mate, base_table.T, onehot, own_seqs, 8
-    )
-    ctx_near, qkv_far, w_rows = lax.optimization_barrier((ctx_near, qkv_far, w_rows))
+    normed, partial = near_part(
+        meta,
+        lengths,
+        tokens,
+        base_gains,
+        qkv_own,
+        qkv_mate,
+        base_table.T,
+        onehot,
+        base_out,
+        own_seqs,
+        8,
+    )
+    normed, partial, qkv_far, w_rows = lax.optimization_barrier((normed, partial, qkv_far, w_rows))
     qkv_far_mate = swap(qkv_far, 1)
     side_output, input_grad, mine, other = main_part(
         meta,
         lengths,
-        tokens,
+        normed,
+        partial,
         base_gains,
         qkv_far,
         qkv_far_mate,
         base_table.T,
-        ctx_near,
         turn(side_input),
         turn(output_grad),
         side_gains,

time: 152 us -> 151 us (level)
  waiting for transfers between devices: 11.6 us -> 8.18 us
    pallas_call x1, Pallas kernels: 14.7 us -> 18.5 us  [near_part(): pl.pallas_call(functools.partial(near_kernel, seqs), name='near', grid_sp...]
    pallas_call x1, Pallas kernels: 86.5 us -> 83.2 us  [main_part(): pl.pallas_call(functools.partial(main_kernel, seqs, chunk), name='main',...]
    all_to_all x2, waiting for transfers between devices: 8.79 us -> 5.64 us  [exchange(): lax.all_to_all(values, ('batch', 'mp'), split_axis=0, concat_axis=0, tile...]
  transfers between devices with their start and end apart: 6 -> 6, of which waited for: 4 -> 3; matrix products, arithmetic and copies ran while one was open for 3% -> 3% of each run, Pallas kernels for 10% -> 12%
where the time goes in v6:
time: 151 us; the launch traced here: 150 us
  Pallas kernels  105 us (70%)
  blocking collectives  17 us (11%)
  starting transfers between devices  11.2 us (7%)
  waiting for transfers between devices  8.18 us (5%)
  local copies, waits for them, and re-layouts  5.79 us (4%)
  other arithmetic  2.35 us (2%)
    pallas_call x1, Pallas kernels, main_part(): pl.pallas_call(functools.partial(main_kernel, seqs, chunk), name='main',...  83.2 us
    pallas_call x1, Pallas kernels, near_part(): pl.pallas_call(functools.partial(near_kernel, seqs), name='near', grid_sp...  18.5 us
    all_to_all x1, blocking collectives, exchange_alike(): lax.all_to_all(values, ('batch', 'mp'), split_axis=0, concat_axis=0, axis...  17 us
    all_to_all x2, starting transfers between devices, exchange(): lax.all_to_all(values, ('batch', 'mp'), split_axis=0, concat_axis=0, tile...  7.47 us
    all_to_all x2, waiting for transfers between devices, exchange(): lax.all_to_all(values, ('batch', 'mp'), split_axis=0, concat_axis=0, tile...  5.64 us
    ppermute x4, starting transfers between devices, swap(): return lax.ppermute(values, 'mp', [(i, i ^ distance) for i in range(size)])  3.73 us
  transfers between devices with their start and end apart: 6, of which 3 were waited for; matrix products, arithmetic and copies ran while one was open for 3% of the time, Pallas kernels for 12%

profile of v6, /device:TPU:0, one launch (start us, length us, event | category | flops | bytes accessed | tf_op | source)
XLA Modules:
  0.0 150.5 jit_solution(6714420468626701176)
XLA Ops:
  0.6 0.5 collective-permute-start
  1.2 2.6 %collective-permute-start.1 = (bf16[3,192,768]{2,1,0:T(8,128)(2,1)}, bf16[3,192,768]{2,1,0:T(8,128)(2,1)S(1)}, u32[]{:S(2)}, u32[]{:S(2)}) collective-permute-start(bf16[3,192,768]{2,1,0:T(8,128)(2,1)} %bitcast.41), channel_id=1, source_target_pairs={{0,2},{1,3},{2,0},{3,1},{4,6},{5,7},{6,4},{7,5},{8,10},{9,11},{10,... | collective-permute-start | bytes 2654216 | tf_op jit(solution)/shard_map/ppermute | solution.py:901
  3.7 0.7 convert_bitcast_fusion
  4.5 0.8 broadcast_in_dim.8
  5.3 4.9 %all-to-all-start = ((bf16[32,45,128]{2,1,0:T(8,128)(2,1)}), bf16[32,45,128]{2,1,0:T(8,128)(2,1)S(1)}, u32[]{:S(2)}, u32[]{:S(2)}) async-start(bf16[32,45,128]{2,1,0:T(8,128)(2,1)} %broadcast_in_dim.8), calls=%async_computation | async-start | bytes 786432 | tf_op jit(solution)/shard_map/all_to_all | solution.py:905
  10.2 0.6 pad_add_fusion.meta_ref
  10.8 0.0 collective-permute-done.mate_ref
  10.8 0.0 copy-start.2
  10.8 0.9 copy-done.2
  11.7 18.5 %near.1 = (bf16[3072,768]{1,0:T(8,128)(2,1)}, bf16[3072,768]{1,0:T(8,128)(2,1)}) custom-call(s32[3]{0:T(128)} %pad_add_fusion.meta_ref, s32[96]{0:T(128)} %len_ref.3, bf16[96,128,768]{2,1,0:T(8,128)(2,1)} %tok_ref.1, f32[2,768]{1,0:T(2,128)} %gain_ref.3, bf16[3,192,768]{2,1,0:T(8,128)(2,1)} %bitcast.42, bf16[3,192,768]{2,1,0:T(8,128)(2,1)} %copy-done.2, ...), custom_call_target="tpu_custom_call" | custom-call | flops 7851737088 | bytes 15925248 | tf_op jit(solution)/shard_map/near/pallas_call | solution.py:213
  30.2 0.0 all-to-all-done
  30.2 0.0 collective-permute-done.1.far_ref
  30.2 0.0 copy-start.1
  30.2 0.3 collective-permute-start.2
  30.5 1.1 reshape.59.w_hbm
  31.6 1.1 collective-permute-done.2.mate_ref
  32.7 0.0 copy-start.3
  32.7 0.0 copy-done.1
  32.7 0.9 copy-done.3
  33.6 83.2 %main.1 = (f32[24,96,128]{2,1,0:T(8,128)}, f32[24,96,128]{2,1,0:T(8,128)}, bf16[16,64,128]{2,1,0:T(8,128)(2,1)}, bf16[16,64,128]{2,1,0:T(8,128)(2,1)}) custom-call(s32[3]{0:T(128)} %pad_add_fusion.meta_ref, s32[96]{0:T(128)} %len_ref.3, bf16[3072,768]{1,0:T(8,128)(2,1)} %get-tuple-element.40.normed_ref, bf16[3072,768]{1,0:T(8,128)(2,1)} %get-tuple-element.41.partial_ref, ...), custom_call_target="tpu_custom_call" | custom-call | flops 45854703616 | bytes 22413312 | tf_op jit(solution)/shard_map/main/pallas_call | solution.py:718
  116.8 0.3 collective-permute-start.3
  117.2 1.5 collective-permute-done.3
  118.6 1.0 add_convert_fusion
  119.7 17.0 %all_to_all.21.got_ref = bf16[16,64,128]{2,1,0:T(8,128)(2,1)} all-to-all(bf16[16,64,128]{2,1,0:T(8,128)(2,1)S(1)} %add_convert_fusion), channel_id=1, replica_groups={{0,2,4,6,8,10,12,14,16,18,20,22,24,26,28,30},{1,3,5,7,9,11,13,15,17,19,..., dimensions={0} | all-to-all | bytes 524288 | tf_op jit(solution)/shard_map/all_to_all | solution.py:910
  136.7 1.7 %collect.1 = (f32[60,96]{1,0:T(8,128)}, f32[3,96]{1,0:T(4,128)}, f32[12,32]{1,0:T(8,128)}, f32[32,128]{1,0:T(8,128)}) custom-call(bf16[16,64,128]{2,1,0:T(8,128)(2,1)} %all_to_all.21.got_ref), custom_call_target="tpu_custom_call" | custom-call | tf_op jit(solution)/shard_map/collect/pallas_call | solution.py:838
  138.3 2.5 %all-to-all-start.2 = ((f32[32,1,128]{2,1,0:T(1,128)}), f32[32,1,128]{2,1,0:T(1,128)S(1)}, u32[]{:S(2)}, u32[]{:S(2)}) async-start(f32[32,1,128]{2,1,0:T(1,128)} %bitcast.33), calls=%async_computation.2 | async-start | bytes 32768 | tf_op jit(solution)/shard_map/all_to_all | solution.py:905
  140.9 1.4 reshape.60.shard_ref
  142.3 5.6 %all-to-all-done.2 = f32[32,1,128]{2,1,0:T(1,128)S(1)} async-done(((f32[32,1,128]{2,1,0:T(1,128)}), f32[32,1,128]{2,1,0:T(1,128)S(1)}, u32[]{:S(2)}, u32[]{:S(2)}) %all-to-all-start.2) | async-done | bytes 16416 | tf_op jit(solution)/shard_map/all_to_all | solution.py:905
  148.0 0.0 copy-start
  148.0 0.6 copy-done
  148.6 1.7 %update.1 = (f32[1,1]{1,0:T(1,128)}, f32[45,128]{1,0:T(8,128)}, f32[45,128]{1,0:T(8,128)}, f32[45,128]{1,0:T(8,128)}, bf16[45,128]{1,0:T(8,128)(2,1)}, /*index=5...) custom-call(f32[32,128]{1,0:T(8,128)} %bitcast.30, ...), custom_call_target="tpu_custom_call" | custom-call | tf_op jit(solution)/shard_map/update/pallas_call | solution.py:884
Async XLA Ops:
  0.6 10.2 %collective-permute-start = (bf16[3,192,768]{2,1,0:T(8,128)(2,1)}, bf16[3,192,768]{2,1,0:T(8,128)(2,1)S(1)}, u32[]{:S(2)}, u32[]{:S(2)}) collective-permute-start(bf16[3,192,768]{2,1,0:T(8,128)(2,1)} %bitcast.40), channel_id=1, source_target_pairs={{0,1},{1,0},{2,3},{3,2},{4,5},{5,4},{6,7},{7,6},{8,9},{9,8},{10,11... | collective-permute-start | bytes 2654216 | tf_op jit(solution)/shard_map/ppermute | solution.py:901
  1.2 29.0 %collective-permute-start.1 = (bf16[3,192,768]{2,1,0:T(8,128)(2,1)}, bf16[3,192,768]{2,1,0:T(8,128)(2,1)S(1)}, u32[]{:S(2)}, u32[]{:S(2)}) collective-permute-start(bf16[3,192,768]{2,1,0:T(8,128)(2,1)} %bitcast.41), channel_id=1, source_target_pairs={{0,2},{1,3},{2,0},{3,1},{4,6},{5,7},{6,4},{7,5},{8,10},{9,11},{10,... | collective-permute-start | bytes 2654216 | tf_op jit(solution)/shard_map/ppermute | solution.py:901
  5.3 24.9 %all-to-all-start = ((bf16[32,45,128]{2,1,0:T(8,128)(2,1)}), bf16[32,45,128]{2,1,0:T(8,128)(2,1)S(1)}, u32[]{:S(2)}, u32[]{:S(2)}) async-start(bf16[32,45,128]{2,1,0:T(8,128)(2,1)} %broadcast_in_dim.8), calls=%async_computation | async-start | bytes 786432 | tf_op jit(solution)/shard_map/all_to_all | solution.py:905
  10.8 0.9 copy-start.2
  30.2 2.5 %copy-start.1 = (bf16[3,192,768]{2,1,0:T(8,128)(2,1)}, bf16[3,192,768]{2,1,0:T(8,128)(2,1)S(1)}, u32[]{:S(2)}) copy-start(bf16[3,192,768]{2,1,0:T(8,128)(2,1)S(1)} %collective-permute-done.1.far_ref) | copy-start | bytes 2654212
  30.2 2.5 %collective-permute-start.2 = (bf16[3,192,768]{2,1,0:T(8,128)(2,1)S(1)}, bf16[3,192,768]{2,1,0:T(8,128)(2,1)S(1)}, u32[]{:S(2)}, u32[]{:S(2)}) collective-permute-start(bf16[3,192,768]{2,1,0:T(8,128)(2,1)S(1)} %collective-permute-done.1.far_ref), channel_id=1, source_target_pairs={{0,1},{1,0},{2,3},{3,2},{4,5},{5,4},{6,7},{7,6},{8,9},{9,8},{10,11... | collective-permute-start | bytes 2654216 | tf_op jit(solution)/shard_map/ppermute | solution.py:901
  32.7 0.9 copy-start.3
  116.8 1.8 %collective-permute-start.3 = (bf16[16,64,128]{2,1,0:T(8,128)(2,1)}, bf16[16,64,128]{2,1,0:T(8,128)(2,1)S(1)}, u32[]{:S(2)}, u32[]{:S(2)}) collective-permute-start(bf16[16,64,128]{2,1,0:T(8,128)(2,1)} %get-tuple-element.47), channel_id=1, source_target_pairs={{0,1},{1,0},{2,3},{3,2},{4,5},{5,4},{6,7},{7,6},{8,9},{9,8},{10,11... | collective-permute-start | bytes 786440 | tf_op jit(solution)/shard_map/ppermute | solution.py:901
  138.3 9.6 %all-to-all-start.2 = ((f32[32,1,128]{2,1,0:T(1,128)}), f32[32,1,128]{2,1,0:T(1,128)S(1)}, u32[]{:S(2)}, u32[]{:S(2)}) async-start(f32[32,1,128]{2,1,0:T(1,128)} %bitcast.33), calls=%async_computation.2 | async-start | bytes 32768 | tf_op jit(solution)/shard_map/all_to_all | solution.py:905
  148.0 0.6 copy-start

commit v7 on v6

--- a/solution.py
+++ b/solution.py
@@ -992,7 +992,7 @@
         w_rows.reshape(devices * shard_rows, DS),
         devices,
         8,
-        1024,
+        1536,
     )
 
     paired = mine.astype(jnp.float32) + swap(other, 1).astype(jnp.float32)

time: 151 us -> 151 us (level)
  no operation moved by 1% of the time
where the time goes in v7:
time: 151 us; the launch traced here: 150 us
  Pallas kernels  105 us (70%)
  blocking collectives  17 us (11%)
  starting transfers between devices  11.2 us (7%)
  waiting for transfers between devices  8.18 us (5%)
  local copies, waits for them, and re-layouts  5.79 us (4%)
  other arithmetic  2.35 us (2%)
    pallas_call x1, Pallas kernels, main_part(): pl.pallas_call(functools.partial(main_kernel, seqs, chunk), name='main',...  83.2 us
    pallas_call x1, Pallas kernels, near_part(): pl.pallas_call(functools.partial(near_kernel, seqs), name='near', grid_sp...  18.5 us
    all_to_all x1, blocking collectives, exchange_alike(): lax.all_to_all(values, ('batch', 'mp'), split_axis=0, concat_axis=0, axis...  17 us
    all_to_all x2, starting transfers between devices, exchange(): lax.all_to_all(values, ('batch', 'mp'), split_axis=0, concat_axis=0, tile...  7.47 us
    all_to_all x2, waiting for transfers between devices, exchange(): lax.all_to_all(values, ('batch', 'mp'), split_axis=0, concat_axis=0, tile...  5.64 us
    ppermute x4, starting transfers between devices, swap(): return lax.ppermute(values, 'mp', [(i, i ^ distance) for i in range(size)])  3.73 us
  transfers between devices with their start and end apart: 6, of which 3 were waited for; matrix products, arithmetic and copies ran while one was open for 3% of the time, Pallas kernels for 12%

profile of v7, /device:TPU:0, one launch (start us, length us, event | category | flops | bytes accessed | tf_op | source)
XLA Modules:
  0.0 150.4 jit_solution(818950128886458216)
XLA Ops:
  0.6 0.5 collective-permute-start
  1.2 2.6 %collective-permute-start.1 = (bf16[3,192,768]{2,1,0:T(8,128)(2,1)}, bf16[3,192,768]{2,1,0:T(8,128)(2,1)S(1)}, u32[]{:S(2)}, u32[]{:S(2)}) collective-permute-start(bf16[3,192,768]{2,1,0:T(8,128)(2,1)} %bitcast.41), channel_id=1, source_target_pairs={{0,2},{1,3},{2,0},{3,1},{4,6},{5,7},{6,4},{7,5},{8,10},{9,11},{10,... | collective-permute-start | bytes 2654216 | tf_op jit(solution)/shard_map/ppermute | solution.py:901
  3.7 0.7 convert_bitcast_fusion
  4.5 0.8 broadcast_in_dim.8
  5.3 4.9 %all-to-all-start = ((bf16[32,45,128]{2,1,0:T(8,128)(2,1)}), bf16[32,45,128]{2,1,0:T(8,128)(2,1)S(1)}, u32[]{:S(2)}, u32[]{:S(2)}) async-start(bf16[32,45,128]{2,1,0:T(8,128)(2,1)} %broadcast_in_dim.8), calls=%async_computation | async-start | bytes 786432 | tf_op jit(solution)/shard_map/all_to_all | solution.py:905
  10.2 0.6 pad_add_fusion.meta_ref
  10.8 0.0 collective-permute-done.mate_ref
  10.8 0.0 copy-start.2
  10.8 0.9 copy-done.2
  11.7 18.5 %near.1 = (bf16[3072,768]{1,0:T(8,128)(2,1)}, bf16[3072,768]{1,0:T(8,128)(2,1)}) custom-call(s32[3]{0:T(128)} %pad_add_fusion.meta_ref, s32[96]{0:T(128)} %len_ref.3, bf16[96,128,768]{2,1,0:T(8,128)(2,1)} %tok_ref.1, f32[2,768]{1,0:T(2,128)} %gain_ref.3, bf16[3,192,768]{2,1,0:T(8,128)(2,1)} %bitcast.42, bf16[3,192,768]{2,1,0:T(8,128)(2,1)} %copy-done.2, ...), custom_call_target="tpu_custom_call" | custom-call | flops 7851737088 | bytes 15925248 | tf_op jit(solution)/shard_map/near/pallas_call | solution.py:213
  30.2 0.0 all-to-all-done
  30.2 0.0 collective-permute-done.1.far_ref
  30.2 0.0 copy-start.1
  30.2 0.3 collective-permute-start.2
  30.5 1.1 reshape.59.w_hbm
  31.6 1.1 collective-permute-done.2.mate_ref
  32.7 0.0 copy-start.3
  32.7 0.0 copy-done.1
  32.7 0.9 copy-done.3
  33.6 83.2 %main.1 = (f32[24,96,128]{2,1,0:T(8,128)}, f32[24,96,128]{2,1,0:T(8,128)}, bf16[16,64,128]{2,1,0:T(8,128)(2,1)}, bf16[16,64,128]{2,1,0:T(8,128)(2,1)}) custom-call(s32[3]{0:T(128)} %pad_add_fusion.meta_ref, s32[96]{0:T(128)} %len_ref.3, bf16[3072,768]{1,0:T(8,128)(2,1)} %get-tuple-element.40.normed_ref, bf16[3072,768]{1,0:T(8,128)(2,1)} %get-tuple-element.41.partial_ref, ...), custom_call_target="tpu_custom_call" | custom-call | flops 45854703616 | bytes 22413312 | tf_op jit(solution)/shard_map/main/pallas_call | solution.py:718
  116.8 0.3 collective-permute-start.3
  117.1 1.5 collective-permute-done.3
  118.6 1.0 add_convert_fusion
  119.7 17.0 %all_to_all.21.got_ref = bf16[16,64,128]{2,1,0:T(8,128)(2,1)} all-to-all(bf16[16,64,128]{2,1,0:T(8,128)(2,1)S(1)} %add_convert_fusion), channel_id=1, replica_groups={{0,2,4,6,8,10,12,14,16,18,20,22,24,26,28,30},{1,3,5,7,9,11,13,15,17,19,..., dimensions={0} | all-to-all | bytes 524288 | tf_op jit(solution)/shard_map/all_to_all | solution.py:910
  136.6 1.7 %collect.1 = (f32[60,96]{1,0:T(8,128)}, f32[3,96]{1,0:T(4,128)}, f32[12,32]{1,0:T(8,128)}, f32[32,128]{1,0:T(8,128)}) custom-call(bf16[16,64,128]{2,1,0:T(8,128)(2,1)} %all_to_all.21.got_ref), custom_call_target="tpu_custom_call" | custom-call | tf_op jit(solution)/shard_map/collect/pallas_call | solution.py:838
  138.3 2.5 %all-to-all-start.2 = ((f32[32,1,128]{2,1,0:T(1,128)}), f32[32,1,128]{2,1,0:T(1,128)S(1)}, u32[]{:S(2)}, u32[]{:S(2)}) async-start(f32[32,1,128]{2,1,0:T(1,128)} %bitcast.33), calls=%async_computation.2 | async-start | bytes 32768 | tf_op jit(solution)/shard_map/all_to_all | solution.py:905
  140.9 1.4 reshape.60.shard_ref
  142.3 5.6 %all-to-all-done.2 = f32[32,1,128]{2,1,0:T(1,128)S(1)} async-done(((f32[32,1,128]{2,1,0:T(1,128)}), f32[32,1,128]{2,1,0:T(1,128)S(1)}, u32[]{:S(2)}, u32[]{:S(2)}) %all-to-all-start.2) | async-done | bytes 16416 | tf_op jit(solution)/shard_map/all_to_all | solution.py:905
  148.0 0.0 copy-start
  148.0 0.6 copy-done
  148.6 1.7 %update.1 = (f32[1,1]{1,0:T(1,128)}, f32[45,128]{1,0:T(8,128)}, f32[45,128]{1,0:T(8,128)}, f32[45,128]{1,0:T(8,128)}, bf16[45,128]{1,0:T(8,128)(2,1)}, /*index=5...) custom-call(f32[32,128]{1,0:T(8,128)} %bitcast.30, ...), custom_call_target="tpu_custom_call" | custom-call | tf_op jit(solution)/shard_map/update/pallas_call | solution.py:884
Async XLA Ops:
  0.6 10.2 %collective-permute-start = (bf16[3,192,768]{2,1,0:T(8,128)(2,1)}, bf16[3,192,768]{2,1,0:T(8,128)(2,1)S(1)}, u32[]{:S(2)}, u32[]{:S(2)}) collective-permute-start(bf16[3,192,768]{2,1,0:T(8,128)(2,1)} %bitcast.40), channel_id=1, source_target_pairs={{0,1},{1,0},{2,3},{3,2},{4,5},{5,4},{6,7},{7,6},{8,9},{9,8},{10,11... | collective-permute-start | bytes 2654216 | tf_op jit(solution)/shard_map/ppermute | solution.py:901
  1.2 29.0 %collective-permute-start.1 = (bf16[3,192,768]{2,1,0:T(8,128)(2,1)}, bf16[3,192,768]{2,1,0:T(8,128)(2,1)S(1)}, u32[]{:S(2)}, u32[]{:S(2)}) collective-permute-start(bf16[3,192,768]{2,1,0:T(8,128)(2,1)} %bitcast.41), channel_id=1, source_target_pairs={{0,2},{1,3},{2,0},{3,1},{4,6},{5,7},{6,4},{7,5},{8,10},{9,11},{10,... | collective-permute-start | bytes 2654216 | tf_op jit(solution)/shard_map/ppermute | solution.py:901
  5.3 24.9 %all-to-all-start = ((bf16[32,45,128]{2,1,0:T(8,128)(2,1)}), bf16[32,45,128]{2,1,0:T(8,128)(2,1)S(1)}, u32[]{:S(2)}, u32[]{:S(2)}) async-start(bf16[32,45,128]{2,1,0:T(8,128)(2,1)} %broadcast_in_dim.8), calls=%async_computation | async-start | bytes 786432 | tf_op jit(solution)/shard_map/all_to_all | solution.py:905
  10.8 0.9 copy-start.2
  30.2 2.5 %copy-start.1 = (bf16[3,192,768]{2,1,0:T(8,128)(2,1)}, bf16[3,192,768]{2,1,0:T(8,128)(2,1)S(1)}, u32[]{:S(2)}) copy-start(bf16[3,192,768]{2,1,0:T(8,128)(2,1)S(1)} %collective-permute-done.1.far_ref) | copy-start | bytes 2654212
  30.2 2.5 %collective-permute-start.2 = (bf16[3,192,768]{2,1,0:T(8,128)(2,1)S(1)}, bf16[3,192,768]{2,1,0:T(8,128)(2,1)S(1)}, u32[]{:S(2)}, u32[]{:S(2)}) collective-permute-start(bf16[3,192,768]{2,1,0:T(8,128)(2,1)S(1)} %collective-permute-done.1.far_ref), channel_id=1, source_target_pairs={{0,1},{1,0},{2,3},{3,2},{4,5},{5,4},{6,7},{7,6},{8,9},{9,8},{10,11... | collective-permute-start | bytes 2654216 | tf_op jit(solution)/shard_map/ppermute | solution.py:901
  32.7 0.9 copy-start.3
  116.8 1.8 %collective-permute-start.3 = (bf16[16,64,128]{2,1,0:T(8,128)(2,1)}, bf16[16,64,128]{2,1,0:T(8,128)(2,1)S(1)}, u32[]{:S(2)}, u32[]{:S(2)}) collective-permute-start(bf16[16,64,128]{2,1,0:T(8,128)(2,1)} %get-tuple-element.47), channel_id=1, source_target_pairs={{0,1},{1,0},{2,3},{3,2},{4,5},{5,4},{6,7},{7,6},{8,9},{9,8},{10,11... | collective-permute-start | bytes 786440 | tf_op jit(solution)/shard_map/ppermute | solution.py:901
  138.3 9.6 %all-to-all-start.2 = ((f32[32,1,128]{2,1,0:T(1,128)}), f32[32,1,128]{2,1,0:T(1,128)S(1)}, u32[]{:S(2)}, u32[]{:S(2)}) async-start(f32[32,1,128]{2,1,0:T(1,128)} %bitcast.33), calls=%async_computation.2 | async-start | bytes 32768 | tf_op jit(solution)/shard_map/all_to_all | solution.py:905
  148.0 0.6 copy-start
